TPU v7x, 1024 devices: a whole 4x8x16 slice. The times are simulated.
1024 devices in a mesh: inp: 16 (over z), out: 8 (over y_hi, core), dep: 8 (over y_lo, x).
Axes of the slice: x: 4, y: 8 (y_hi: 4, y_lo: 2; y = y_hi * 2 + y_lo), z: 16, core: 2. Of those that a mesh axis runs over, the one named last changes fastest.
Arguments:
- tokens: bfloat16 [1536, 8192], P('dep', 'inp'), may hold values from -6 to 6
- grad_hidden: bfloat16 [1536, 14336], P('dep', 'out'), may hold values from -3 to 3
- w_gate: bfloat16 [8192, 14336], P('inp', 'out'), may hold values from -0.0625 to 0.0625
- w_up: bfloat16 [8192, 14336], P('inp', 'out'), may hold values from -0.0625 to 0.0625
Outputs:
- grad_input: bfloat16 [1536, 8192], P('dep', ('inp', 'out'))
- gate_grad: bfloat16 [8192, 14336], P(('inp', 'dep'), 'out')
- up_grad: bfloat16 [8192, 14336], P(('inp', 'dep'), 'out')
All inputs are finite; a program needn't handle non-finite values.
Results may differ from a plain program's by a relative error of at most 0.019.
Values may be sent and summed in bfloat16 or wider, within the bound.
No kernel may reach another device: no remote copies, remote signals or barrier semaphores. Data moves between devices by JAX's collectives and lax.ppermute only.
A program may use at most 32 MiB of HBM per device.

v0:
```python
import math

import jax
import jax.numpy as jnp
from jax import lax
from jax.sharding import PartitionSpec as P


def local_product(left, right):
    return jnp.dot(left, right, preferred_element_type=jnp.float32)


def contract_rows(left, right):
    return lax.dot_general(
        left, right, (((0,), (0,)), ((), ())), preferred_element_type=jnp.float32
    )


def contract_cols(left, right):
    return lax.dot_general(
        left, right, (((1,), (1,)), ((), ())), preferred_element_type=jnp.float32
    )


def shards(tokens, grad_hidden, w_gate, w_up):
    token_count = tokens.shape[0]
    own_rows = token_count // lax.axis_size("inp")
    hidden_width = w_gate.shape[1]
    factor = 1.0 / math.sqrt(token_count * lax.axis_size("dep"))
    summed = lax.psum_scatter(
        jnp.concatenate([local_product(tokens, w_gate), local_product(tokens, w_up)], axis=1),
        "inp",
        scatter_dimension=0,
        tiled=True,
    )
    gate_value = summed[:, :hidden_width]
    up_value = summed[:, hidden_width:]
    offset = lax.axis_index("inp") * own_rows
    cotangent = lax.dynamic_slice_in_dim(grad_hidden, offset, own_rows, 0).astype(jnp.float32)
    sigmoid_gate = jax.nn.sigmoid(gate_value)
    grad_gate = (
        cotangent * up_value * sigmoid_gate * (1.0 + gate_value * (1.0 - sigmoid_gate))
    ).astype(jnp.bfloat16)
    grad_upper = (cotangent * gate_value * sigmoid_gate).astype(jnp.bfloat16)
    paired = jnp.concatenate([grad_gate, grad_upper], axis=1)
    gathered = lax.all_gather(paired, "inp", axis=0, tiled=True)
    full_gate = gathered[:, :hidden_width]
    full_upper = gathered[:, hidden_width:]
    input_terms = contract_cols(full_gate, w_gate) + contract_cols(full_upper, w_up)
    grad_input = lax.psum_scatter(input_terms, "out", scatter_dimension=1, tiled=True).astype(
        jnp.bfloat16
    )
    gate_part = contract_rows(tokens, full_gate)
    upper_part = contract_rows(tokens, full_upper)
    gate_sum, upper_sum = (
        lax.psum_scatter(
            gate_part.astype(jnp.bfloat16), "dep", scatter_dimension=0, tiled=True
        ).astype(jnp.float32),
        lax.psum_scatter(
            upper_part.astype(jnp.bfloat16), "dep", scatter_dimension=0, tiled=True
        ).astype(jnp.float32),
    )
    return (
        grad_input,
        (gate_sum * factor).astype(jnp.bfloat16),
        (upper_sum * factor).astype(jnp.bfloat16),
    )


def solution(mesh):
    return jax.shard_map(
        shards,
        mesh=mesh,
        in_specs=(P("dep", "inp"), P("dep", "out"), P("inp", "out"), P("inp", "out")),
        out_specs=(P("dep", ("inp", "out")), P(("inp", "dep"), "out"), P(("inp", "dep"), "out")),
        check_vma=False,
    )
```

profile of v0, /device:TPU:16, one launch (start us, length us, event | category | flops | bytes accessed | tf_op | source)
XLA Modules:
  0.0 415.9 jit_solution(6743495357225615447)
XLA Ops:
  7.2 0.0 copy-start
  7.2 0.0 copy-start.2
  7.2 0.0 all-reduce.3.cloned.1.call-start
  7.2 2.3 fusion.13
  9.5 0.0 copy-done
  9.5 0.0 copy-done.2
  9.5 0.5 fusion.12
  10.1 1.9 pad_maximum_fusion
  11.9 0.0 all-reduce.3.cloned.1.call-update
  12.0 0.0 all-gather.3.cloned.1.call-start
  12.0 1.3 dynamic-slice
  13.9 160.6 %all-reduce.3.cloned.1.call-done = f32[192,3584]{1,0:T(8,128)} async-done(((f32[192,3584]{1,0:T(8,128)}), f32[192,3584]{1,0:T(8,128)}) %all-reduce.3.cloned.1.call-update) | async-done | bytes 2752528
  174.6 1.2 fusion.9
  175.7 0.7 maximum_bitcast_fusion
  176.4 0.0 all-gather.3.cloned.1.call-update
  176.4 0.0 reduce-scatter.8.cloned.1.call-start
  176.5 74.1 %all-gather.3.cloned.1.call-done = bf16[16,12,3584]{2,1,0:T(8,128)(2,1)} async-done(((bf16[1,12,3584]{2,1,0:T(8,128)(2,1)}), bf16[16,12,3584]{2,1,0:T(8,128)(2,1)}) %all-gather.3.cloned.1.call-update) | async-done | bytes 1376272 | tf_op jit(solution)/shard_map/all_gather | solution.py:46
  250.6 2.4 reshape.7
  253.0 0.0 copy-start.1
  253.0 0.7 fusion.5
  253.7 0.8 copy-done.1
  254.5 1.5 convolution_add_fusion
  255.9 0.0 reduce-scatter.8.cloned.1.call-update
  256.0 0.0 reduce-scatter.10.cloned.1.call-start
  256.0 1.9 fusion
  257.9 3.9 copy.13
  261.8 0.0 reduce-scatter.10.cloned.1.call-update
  261.8 0.0 reduce-scatter.12.cloned.1.call-start
  261.9 1.9 fusion.1
  263.8 3.8 copy.15
  267.6 0.0 reduce-scatter.12.cloned.1.call-update
  267.6 26.1 %reduce-scatter.8.cloned.1.call-done = f32[192,64]{0,1:T(8,128)} async-done(((f32[192,512]{0,1:T(8,128)}), f32[192,64]{0,1:T(8,128)}) %reduce-scatter.8.cloned.1.call-update) | async-done | bytes 49168 | tf_op jit(solution)/shard_map/reduce_scatter | solution.py:50
  293.7 1.5 convert_element_type.39
  295.2 56.9 %reduce-scatter.10.cloned.1.call-done = bf16[64,1792]{1,0:T(8,128)(2,1)} async-done(((bf16[512,1792]{1,0:T(8,128)(2,1)}), bf16[64,1792]{1,0:T(8,128)(2,1)}) %reduce-scatter.10.cloned.1.call-update) | async-done | bytes 229392
  352.1 1.2 copy.14
  353.3 0.1 multiply_convert_fusion.1
  353.4 0.9 copy.11
  354.3 52.9 %reduce-scatter.12.cloned.1.call-done = bf16[64,1792]{1,0:T(8,128)(2,1)} async-done(((bf16[512,1792]{1,0:T(8,128)(2,1)}), bf16[64,1792]{1,0:T(8,128)(2,1)}) %reduce-scatter.12.cloned.1.call-update) | async-done | bytes 229392
  407.2 1.2 copy.16
  408.4 0.1 multiply_convert_fusion
  408.5 0.9 copy.12
Async XLA Ops:
  7.2 2.3 copy-start
  7.2 2.3 copy-start.2
  7.2 167.4 %all-reduce.3.cloned.1.call-start = ((), (), s32[]{:S(2)}) async-start(), calls=%async_computation.7 | async-start | bytes 5505024
  12.0 238.6 %all-gather.3.cloned.1.call-start = ((), (), s32[]{:S(2)}) async-start(), calls=%async_computation.4 | async-start | bytes 1949696 | tf_op jit(solution)/shard_map/all_gather | solution.py:46
  176.4 117.3 %reduce-scatter.8.cloned.1.call-start = ((), (), s32[]{:S(2)}) async-start(), calls=%async_computation.3 | async-start | bytes 589824 | tf_op jit(solution)/shard_map/reduce_scatter | solution.py:50
  253.0 1.5 copy-start.1
  256.0 96.1 %reduce-scatter.10.cloned.1.call-start = ((), (), s32[]{:S(2)}) async-start(), calls=%async_computation.5 | async-start | bytes 2064384
  261.8 145.4 %reduce-scatter.12.cloned.1.call-start = ((), (), s32[]{:S(2)}) async-start(), calls=%async_computation.6 | async-start | bytes 2064384
Sparse Core Ops, SparseCore 0:
  12.1 162.4 all-reduce.2
  178.2 72.3 all-gather.2
  256.1 37.5 reduce-scatter.7
  297.0 54.9 reduce-scatter.9
  355.4 51.7 reduce-scatter.11
where the time goes:
time: 416 us
  waiting for transfers between devices  371 us (89%)
  local copies, waits for them, and re-layouts  16.4 us (4%)
  between operations  14.5 us (3%)
  matrix products  8.71 us (2%)
  other arithmetic  5.35 us (1%)
    unnamed x8, waiting for transfers between devices  271 us
    all_gather x1, waiting for transfers between devices, shards(): gathered = lax.all_gather(paired, 'inp', axis=0, tiled=True)  74.1 us
    reduce_scatter x1, waiting for transfers between devices, shards(): lax.psum_scatter(input_terms, 'out', scatter_dimension=1, tiled=True)  26.1 us
    unnamed x14, local copies, waits for them, and re-layouts  16.4 us
  transfers between devices with their start and end apart: 5, of which 5 were waited for; matrix products, arithmetic and copies ran while one was open for 4% of the time, Pallas kernels for 0%

commit v1 on v0

v1 whole, which is shorter than its diff:
```python
import math

import jax
import jax.numpy as jnp
from jax import lax
from jax.sharding import PartitionSpec as P

BF16 = jnp.bfloat16
F32 = jnp.float32
LANES = 128


def product(left, right):
    return jnp.dot(left, right, preferred_element_type=F32)


def contract_rows(left, right):
    return lax.dot_general(left, right, (((0,), (0,)), ((), ())), preferred_element_type=F32)


def contract_cols(left, right):
    return lax.dot_general(left, right, (((1,), (1,)), ((), ())), preferred_element_type=F32)


def shards(tokens, grad_hidden, w_gate, w_up):
    token_count, feature_count = tokens.shape
    hidden = w_gate.shape[1]
    inp, out, dep = (lax.axis_size(name) for name in ("inp", "out", "dep"))
    factor = 1.0 / math.sqrt(token_count * dep)
    half = hidden // 2
    group = inp // 2
    rows = token_count // group
    pairs = [(i, i ^ 1) for i in range(inp)]
    alike = [[p + 2 * i for i in range(group)] for p in range(2)]
    place = lax.axis_index("inp")
    parity = place % 2
    even = parity == 0

    all_tokens = lax.all_to_all(
        jnp.broadcast_to(tokens[None], (dep, token_count, feature_count)), "dep", 0, 0
    ).reshape(dep * token_count, feature_count)

    halves = [
        jnp.concatenate(
            [
                product(tokens, w_gate[:, h * half : (h + 1) * half]),
                product(tokens, w_up[:, h * half : (h + 1) * half]),
            ],
            axis=1,
        )
        for h in range(2)
    ]
    given = jnp.where(even, halves[1], halves[0]).astype(BF16)
    kept = jnp.where(even, halves[0], halves[1])
    kept = (kept + lax.ppermute(given, "inp", pairs).astype(F32)).astype(BF16)
    terms = lax.all_to_all(
        kept.reshape(group, rows, hidden), "inp", 0, 0, axis_index_groups=alike
    )
    summed = jnp.sum(terms.astype(F32), axis=0)
    gate_value = summed[:, :half]
    up_value = summed[:, half:]
    cotangent = lax.dynamic_slice(
        grad_hidden, ((place // 2) * rows, parity * half), (rows, half)
    ).astype(F32)
    sigmoid_gate = jax.nn.sigmoid(gate_value)
    grad_gate = cotangent * up_value * sigmoid_gate * (1.0 + gate_value * (1.0 - sigmoid_gate))
    grad_upper = cotangent * gate_value * sigmoid_gate
    paired = jnp.concatenate([grad_gate, grad_upper], axis=1).astype(BF16)
    own = lax.all_gather(paired, "inp", axis=0, tiled=True, axis_index_groups=alike)
    other = lax.ppermute(own, "inp", pairs)

    width = 2 * LANES
    blocks = dep // 2
    starts = [min(b * width, half - width) for b in range(blocks)]
    skips = [b * width - s for b, s in enumerate(starts)]

    def weight_gradient(pair):
        pieces = jnp.stack(
            [pair[:, u * half + s : u * half + s + width] for u in range(2) for s in starts]
        )
        block = lax.all_to_all(pieces, "dep", 0, 0).reshape(dep * token_count, width)
        grad = (contract_rows(all_tokens, block) * factor).astype(BF16)
        swapped = lax.all_to_all(grad.reshape(dep, feature_count // dep, width), "dep", 0, 0)
        return [
            jnp.concatenate(
                [swapped[u * blocks + b][:, skips[b] :] for b in range(blocks)], axis=1
            )
            for u in range(2)
        ]

    own_grads = weight_gradient(own)
    other_grads = weight_gradient(other)
    gate_grad, up_grad = (
        jnp.concatenate([jnp.where(even, a, b), jnp.where(even, b, a)], axis=1)
        for a, b in zip(own_grads, other_grads)
    )

    full = [jnp.where(even, own, other), jnp.where(even, other, own)]
    input_terms = sum(
        contract_cols(w[:, h * half : (h + 1) * half], full[h][:, u * half : (u + 1) * half])
        for h in range(2)
        for u, w in enumerate((w_gate, w_up))
    ).astype(BF16)
    shares = lax.all_to_all(
        input_terms.reshape(out, feature_count // out, token_count), "out", 0, 0
    )
    grad_input = jnp.sum(shares.astype(F32), axis=0).astype(BF16).T
    return grad_input, gate_grad, up_grad


def solution(mesh):
    return jax.shard_map(
        shards,
        mesh=mesh,
        in_specs=(P("dep", "inp"), P("dep", "out"), P("inp", "out"), P("inp", "out")),
        out_specs=(P("dep", ("inp", "out")), P(("inp", "dep"), "out"), P(("inp", "dep"), "out")),
        check_vma=False,
    )
```

time: 416 us -> 210 us (0.50)
  the two profiles are of different devices: /device:TPU:16 before, /device:TPU:8 now
where the time goes in v1:
time: 210 us; the launch traced here: 209 us
  waiting for transfers between devices  95.2 us (45%)
  starting transfers between devices  56.3 us (27%)
  blocking collectives  37.4 us (18%)
  matrix products  8.25 us (4%)
  local copies, waits for them, and re-layouts  7.42 us (4%)
  other arithmetic  3.83 us (2%)
    all_gather x1, blocking collectives, shards(): lax.all_gather(paired, 'inp', axis=0, tiled=True, axis_index_groups=alike)  37.4 us
    all_to_all x1, waiting for transfers between devices, shards(): lax.all_to_all(kept.reshape(group, rows, hidden), 'inp', 0, 0, axis_index...  30.7 us
    all_to_all x2, waiting for transfers between devices, weight_gradient(): lax.all_to_all(pieces, 'dep', 0, 0).reshape(dep * token_count, width)  19.6 us
    all_to_all x1, starting transfers between devices, shards(): lax.all_to_all(kept.reshape(group, rows, hidden), 'inp', 0, 0, axis_index...  18.1 us
    ppermute x1, waiting for transfers between devices, shards(): kept = (kept + lax.ppermute(given, 'inp', pairs).astype(F32)).astype(BF16)  15.4 us
    all_to_all x1, waiting for transfers between devices, shards(): lax.all_to_all(input_terms.reshape(out, feature_count // out, token_count...  10.7 us
    all_to_all x2, starting transfers between devices, weight_gradient(): lax.all_to_all(pieces, 'dep', 0, 0).reshape(dep * token_count, width)  10.5 us
    all_to_all x2, waiting for transfers between devices, weight_gradient(): lax.all_to_all(grad.reshape(dep, feature_count // dep, width), 'dep', 0, 0)  9.7 us
  transfers between devices with their start and end apart: 9, of which 8 were waited for; matrix products, arithmetic and copies ran while one was open for 4% of the time, Pallas kernels for 0%

profile of v1, /device:TPU:8, one launch (start us, length us, event | category | flops | bytes accessed | tf_op | source)
XLA Modules:
  0.0 209.5 jit_solution(7243374598330917082)
XLA Ops:
  0.6 0.0 copy-start.1
  0.7 1.8 fusion.12
  2.5 1.6 fusion.20
  4.0 0.0 copy-done.1
  4.0 0.4 fusion.16
  4.4 0.4 fusion.23
  4.8 0.1 select_convert_fusion
  5.0 4.3 %collective-permute-start = (bf16[192,1792]{1,0:T(8,128)(2,1)S(1)}, bf16[192,1792]{1,0:T(8,128)(2,1)S(1)}, u32[]{:S(2)}, u32[]{:S(2)}) collective-permute-start(bf16[192,1792]{1,0:T(8,128)(2,1)S(1)} %select_convert_fusion), channel_id=1, source_target_pairs={{0,64},{64,0},{128,192},{192,128},{256,320},{320,256},{384,448},{4... | collective-permute-start | bytes 2064392 | tf_op jit(solution)/shard_map/ppermute | solution.py:55
  9.2 15.4 %collective-permute-done = bf16[192,1792]{1,0:T(8,128)(2,1)S(1)} collective-permute-done((bf16[192,1792]{1,0:T(8,128)(2,1)S(1)}, bf16[192,1792]{1,0:T(8,128)(2,1)S(1)}, u32[]{:S(2)}, u32[]{:S(2)}) %collective-permute-start) | collective-permute-done | bytes 688160 | tf_op jit(solution)/shard_map/ppermute | solution.py:55
  24.7 1.1 add_convert_fusion
  25.8 18.1 %all-to-all-start = ((bf16[8,24,1792]{2,1,0:T(8,128)(2,1)}), bf16[8,24,1792]{2,1,0:T(8,128)(2,1)S(1)}, u32[]{:S(2)}, u32[]{:S(2)}) async-start(bf16[8,24,1792]{2,1,0:T(8,128)(2,1)} %bitcast.131), calls=%async_computation | async-start | bytes 1376256 | tf_op jit(solution)/shard_map/all_to_all | solution.py:56
  43.9 30.7 %all-to-all-done = bf16[8,24,1792]{2,1,0:T(8,128)(2,1)S(1)} async-done(((bf16[8,24,1792]{2,1,0:T(8,128)(2,1)}), bf16[8,24,1792]{2,1,0:T(8,128)(2,1)S(1)}, u32[]{:S(2)}, u32[]{:S(2)}) %all-to-all-start) | async-done | bytes 688160 | tf_op jit(solution)/shard_map/all_to_all | solution.py:56
  74.5 1.3 broadcast_in_dim.2
  75.8 5.6 %all-to-all-start.3 = ((bf16[8,192,512]{2,1,0:T(8,128)(2,1)}), bf16[8,192,512]{2,1,0:T(8,128)(2,1)S(1)}, u32[]{:S(2)}, u32[]{:S(2)}) async-start(bf16[8,192,512]{2,1,0:T(8,128)(2,1)} %broadcast_in_dim.2), calls=%async_computation.3 | async-start | bytes 3145728 | tf_op jit(solution)/shard_map/all_to_all | solution.py:39
  81.5 0.1 convert_reduce_fusion
  81.6 0.8 fusion.47
  82.4 37.4 %all_gather.3 = bf16[192,1792]{1,0:T(8,128)(2,1)S(1)} all-gather(bf16[24,1792]{1,0:T(8,128)(2,1)S(1)} %pad_maximum_fusion.8), channel_id=1, replica_groups={{0,128,256,384,512,640,768,896},{64,192,320,448,576,704,832,960},{1,129..., dimensions={0}, use_global_device_ids=true | all-gather | bytes 774144 | tf_op jit(solution)/shard_map/all_gather | solution.py:69
  119.9 2.6 %collective-permute-start.1 = (bf16[192,1792]{1,0:T(8,128)(2,1)S(1)}, bf16[192,1792]{1,0:T(8,128)(2,1)S(1)}, u32[]{:S(2)}, u32[]{:S(2)}) collective-permute-start(bf16[192,1792]{1,0:T(8,128)(2,1)S(1)} %all_gather.3), channel_id=1, source_target_pairs={{0,64},{64,0},{128,192},{192,128},{256,320},{320,256},{384,448},{4... | collective-permute-start | bytes 2064392 | tf_op jit(solution)/shard_map/ppermute | solution.py:70
  122.6 0.0 copy-start.3
  122.7 0.9 copy-done.5
  123.5 9.2 %collective-permute-done.1 = bf16[192,1792]{1,0:T(8,128)(2,1)S(1)} collective-permute-done((bf16[192,1792]{1,0:T(8,128)(2,1)S(1)}, bf16[192,1792]{1,0:T(8,128)(2,1)S(1)}, u32[]{:S(2)}, u32[]{:S(2)}) %collective-permute-start.1) | collective-permute-done | bytes 688160 | tf_op jit(solution)/shard_map/ppermute | solution.py:70
  132.7 0.1 broadcast_select_fusion.1
  132.8 0.0 copy-start.2
  132.8 0.5 fusion.10
  133.3 1.0 copy-done.2
  134.3 0.5 fusion.14
  134.8 0.5 fusion.18
  135.2 0.5 fusion.9
  135.7 0.8 copy.9
  136.5 0.0 all-to-all-done.3
  136.6 6.2 %all-to-all-start.1 = ((bf16[8,64,192]{2,1,0:T(8,128)(2,1)}), bf16[8,64,192]{2,1,0:T(8,128)(2,1)S(1)}, u32[]{:S(2)}, u32[]{:S(2)}) async-start(bf16[8,64,192]{2,1,0:T(8,128)(2,1)} %bitcast.2), calls=%async_computation.1 | async-start | bytes 524288 | tf_op jit(solution)/shard_map/all_to_all | solution.py:104
  142.7 0.6 fusion.37
  143.3 10.7 %all-to-all-done.1 = bf16[8,64,192]{2,1,0:T(8,128)(2,1)S(1)} async-done(((bf16[8,64,192]{2,1,0:T(8,128)(2,1)}), bf16[8,64,192]{2,1,0:T(8,128)(2,1)S(1)}, u32[]{:S(2)}, u32[]{:S(2)}) %all-to-all-start.1) | async-done | bytes 196640 | tf_op jit(solution)/shard_map/all_to_all | solution.py:104
  154.1 6.3 %all-to-all-start.2 = ((bf16[8,192,256]{2,1,0:T(8,128)(2,1)}), bf16[8,192,256]{2,1,0:T(8,128)(2,1)}, u32[]{:S(2)}, u32[]{:S(2)}) async-start(bf16[8,192,256]{2,1,0:T(8,128)(2,1)} %fusion.37), calls=%async_computation.2 | async-start | bytes 1572864 | tf_op jit(solution)/shard_map/all_to_all | solution.py:81
  160.5 0.9 copy-done.4
  161.4 10.5 %all-to-all-done.2 = bf16[8,192,256]{2,1,0:T(8,128)(2,1)} async-done(((bf16[8,192,256]{2,1,0:T(8,128)(2,1)}), bf16[8,192,256]{2,1,0:T(8,128)(2,1)}, u32[]{:S(2)}, u32[]{:S(2)}) %all-to-all-start.2) | async-done | bytes 786464 | tf_op jit(solution)/shard_map/all_to_all | solution.py:81
  171.9 4.2 %all-to-all-start.5 = ((bf16[8,192,256]{2,1,0:T(8,128)(2,1)}), bf16[8,192,256]{2,1,0:T(8,128)(2,1)S(1)}, u32[]{:S(2)}, u32[]{:S(2)}) async-start(bf16[8,192,256]{2,1,0:T(8,128)(2,1)} %copy-done.4), calls=%async_computation.5 | async-start | bytes 1572864 | tf_op jit(solution)/shard_map/all_to_all | solution.py:81
  176.1 1.7 fusion.8
  177.8 0.8 copy.10
  178.7 9.0 %all-to-all-done.5 = bf16[8,192,256]{2,1,0:T(8,128)(2,1)S(1)} async-done(((bf16[8,192,256]{2,1,0:T(8,128)(2,1)}), bf16[8,192,256]{2,1,0:T(8,128)(2,1)S(1)}, u32[]{:S(2)}, u32[]{:S(2)}) %all-to-all-start.5) | async-done | bytes 786464 | tf_op jit(solution)/shard_map/all_to_all | solution.py:81
  187.7 4.2 %all-to-all-start.4 = ((bf16[8,64,256]{2,1,0:T(8,128)(2,1)}), bf16[8,64,256]{2,1,0:T(8,128)(2,1)S(1)}, u32[]{:S(2)}, u32[]{:S(2)}) async-start(bf16[8,64,256]{2,1,0:T(8,128)(2,1)} %bitcast.14), calls=%async_computation.4 | async-start | bytes 524288 | tf_op jit(solution)/shard_map/all_to_all | solution.py:83
  191.9 0.6 fusion.7
  192.5 0.8 copy.11
  193.4 4.6 %all-to-all-done.4 = bf16[8,64,256]{2,1,0:T(8,128)(2,1)S(1)} async-done(((bf16[8,64,256]{2,1,0:T(8,128)(2,1)}), bf16[8,64,256]{2,1,0:T(8,128)(2,1)S(1)}, u32[]{:S(2)}, u32[]{:S(2)}) %all-to-all-start.4) | async-done | bytes 262176 | tf_op jit(solution)/shard_map/all_to_all | solution.py:83
  197.9 4.7 %all-to-all-start.6 = ((bf16[8,64,256]{2,1,0:T(8,128)(2,1)}), bf16[8,64,256]{2,1,0:T(8,128)(2,1)S(1)}, u32[]{:S(2)}, u32[]{:S(2)}) async-start(bf16[8,64,256]{2,1,0:T(8,128)(2,1)} %bitcast.29), calls=%async_computation.6 | async-start | bytes 524288 | tf_op jit(solution)/shard_map/all_to_all | solution.py:83
  202.7 0.7 reduce_sum.22
  203.4 5.1 %all-to-all-done.6 = bf16[8,64,256]{2,1,0:T(8,128)(2,1)S(1)} async-done(((bf16[8,64,256]{2,1,0:T(8,128)(2,1)}), bf16[8,64,256]{2,1,0:T(8,128)(2,1)S(1)}, u32[]{:S(2)}, u32[]{:S(2)}) %all-to-all-start.6) | async-done | bytes 262176 | tf_op jit(solution)/shard_map/all_to_all | solution.py:83
  208.7 0.8 pad_maximum_fusion.2
  (29 shorter events, 0.3 us)
Async XLA Ops:
  0.6 1.8 copy-start
  0.6 3.4 %copy-start.1 = (bf16[512,1792]{1,0:T(8,128)(2,1)S(1)}, bf16[512,1792]{1,0:T(8,128)(2,1)}, u32[]{:S(2)}) copy-start(bf16[512,1792]{1,0:T(8,128)(2,1)} %param.6) | copy-start | bytes 5505028
  5.0 19.7 %collective-permute-start = (bf16[192,1792]{1,0:T(8,128)(2,1)S(1)}, bf16[192,1792]{1,0:T(8,128)(2,1)S(1)}, u32[]{:S(2)}, u32[]{:S(2)}) collective-permute-start(bf16[192,1792]{1,0:T(8,128)(2,1)S(1)} %select_convert_fusion), channel_id=1, source_target_pairs={{0,64},{64,0},{128,192},{192,128},{256,320},{320,256},{384,448},{4... | collective-permute-start | bytes 2064392 | tf_op jit(solution)/shard_map/ppermute | solution.py:55
  25.8 48.8 %all-to-all-start = ((bf16[8,24,1792]{2,1,0:T(8,128)(2,1)}), bf16[8,24,1792]{2,1,0:T(8,128)(2,1)S(1)}, u32[]{:S(2)}, u32[]{:S(2)}) async-start(bf16[8,24,1792]{2,1,0:T(8,128)(2,1)} %bitcast.131), calls=%async_computation | async-start | bytes 1376256 | tf_op jit(solution)/shard_map/all_to_all | solution.py:56
  75.8 60.7 %all-to-all-start.3 = ((bf16[8,192,512]{2,1,0:T(8,128)(2,1)}), bf16[8,192,512]{2,1,0:T(8,128)(2,1)S(1)}, u32[]{:S(2)}, u32[]{:S(2)}) async-start(bf16[8,192,512]{2,1,0:T(8,128)(2,1)} %broadcast_in_dim.2), calls=%async_computation.3 | async-start | bytes 3145728 | tf_op jit(solution)/shard_map/all_to_all | solution.py:39
  119.9 12.8 %collective-permute-start.1 = (bf16[192,1792]{1,0:T(8,128)(2,1)S(1)}, bf16[192,1792]{1,0:T(8,128)(2,1)S(1)}, u32[]{:S(2)}, u32[]{:S(2)}) collective-permute-start(bf16[192,1792]{1,0:T(8,128)(2,1)S(1)} %all_gather.3), channel_id=1, source_target_pairs={{0,64},{64,0},{128,192},{192,128},{256,320},{320,256},{384,448},{4... | collective-permute-start | bytes 2064392 | tf_op jit(solution)/shard_map/ppermute | solution.py:70
  122.6 10.2 %copy-start.3 = (bf16[512,1792]{1,0:T(8,128)(2,1)S(1)}, bf16[512,1792]{1,0:T(8,128)(2,1)}, u32[]{:S(2)}) copy-start(bf16[512,1792]{1,0:T(8,128)(2,1)} %param.7) | copy-start | bytes 5505028
  122.7 0.9 copy-start.5
  132.8 1.5 copy-start.2
  136.6 17.5 %all-to-all-start.1 = ((bf16[8,64,192]{2,1,0:T(8,128)(2,1)}), bf16[8,64,192]{2,1,0:T(8,128)(2,1)S(1)}, u32[]{:S(2)}, u32[]{:S(2)}) async-start(bf16[8,64,192]{2,1,0:T(8,128)(2,1)} %bitcast.2), calls=%async_computation.1 | async-start | bytes 524288 | tf_op jit(solution)/shard_map/all_to_all | solution.py:104
  154.1 17.9 %all-to-all-start.2 = ((bf16[8,192,256]{2,1,0:T(8,128)(2,1)}), bf16[8,192,256]{2,1,0:T(8,128)(2,1)}, u32[]{:S(2)}, u32[]{:S(2)}) async-start(bf16[8,192,256]{2,1,0:T(8,128)(2,1)} %fusion.37), calls=%async_computation.2 | async-start | bytes 1572864 | tf_op jit(solution)/shard_map/all_to_all | solution.py:81
  160.5 0.9 copy-start.4
  171.9 15.8 %all-to-all-start.5 = ((bf16[8,192,256]{2,1,0:T(8,128)(2,1)}), bf16[8,192,256]{2,1,0:T(8,128)(2,1)S(1)}, u32[]{:S(2)}, u32[]{:S(2)}) async-start(bf16[8,192,256]{2,1,0:T(8,128)(2,1)} %copy-done.4), calls=%async_computation.5 | async-start | bytes 1572864 | tf_op jit(solution)/shard_map/all_to_all | solution.py:81
  187.7 10.2 %all-to-all-start.4 = ((bf16[8,64,256]{2,1,0:T(8,128)(2,1)}), bf16[8,64,256]{2,1,0:T(8,128)(2,1)S(1)}, u32[]{:S(2)}, u32[]{:S(2)}) async-start(bf16[8,64,256]{2,1,0:T(8,128)(2,1)} %bitcast.14), calls=%async_computation.4 | async-start | bytes 524288 | tf_op jit(solution)/shard_map/all_to_all | solution.py:83
  197.9 10.6 %all-to-all-start.6 = ((bf16[8,64,256]{2,1,0:T(8,128)(2,1)}), bf16[8,64,256]{2,1,0:T(8,128)(2,1)S(1)}, u32[]{:S(2)}, u32[]{:S(2)}) async-start(bf16[8,64,256]{2,1,0:T(8,128)(2,1)} %bitcast.29), calls=%async_computation.6 | async-start | bytes 524288 | tf_op jit(solution)/shard_map/all_to_all | solution.py:83

commit v2 on v1

--- a/solution.py
+++ b/solution.py
@@ -36,9 +36,7 @@
     parity = place % 2
     even = parity == 0
 
-    all_tokens = lax.all_to_all(
-        jnp.broadcast_to(tokens[None], (dep, token_count, feature_count)), "dep", 0, 0
-    ).reshape(dep * token_count, feature_count)
+    all_tokens = lax.all_gather(tokens, "dep", axis=0, tiled=True)
 
     halves = [
         jnp.concatenate(
@@ -74,38 +72,56 @@
     starts = [min(b * width, half - width) for b in range(blocks)]
     skips = [b * width - s for b, s in enumerate(starts)]
 
-    def weight_gradient(pair):
+    def column_block(pair):
         pieces = jnp.stack(
             [pair[:, u * half + s : u * half + s + width] for u in range(2) for s in starts]
         )
-        block = lax.all_to_all(pieces, "dep", 0, 0).reshape(dep * token_count, width)
-        grad = (contract_rows(all_tokens, block) * factor).astype(BF16)
-        swapped = lax.all_to_all(grad.reshape(dep, feature_count // dep, width), "dep", 0, 0)
+        return lax.all_to_all(pieces, "dep", 0, 0).reshape(dep * token_count, width)
+
+    own_block = column_block(own)
+    other_block = column_block(other)
+
+    first = [jnp.where(even, own, other), jnp.where(even, other, own)]
+    terms = sum(
+        contract_cols(w[:, h * half : (h + 1) * half], first[h][:, u * half : (u + 1) * half])
+        for h in range(2)
+        for u, w in enumerate((w_gate, w_up))
+    )
+    at_out = lax.axis_index("out")
+    terms = terms.reshape(out // 2, 2, feature_count // out, token_count)
+    low = at_out % 2 == 0
+    given = jnp.where(low, terms[:, 1], terms[:, 0]).astype(BF16)
+    kept = jnp.where(low, terms[:, 0], terms[:, 1])
+    kept = kept + lax.ppermute(given, "out", [(i, i ^ 1) for i in range(out)]).astype(F32)
+    bit = out // 2
+    while bit > 1:
+        low = at_out & bit == 0
+        middle = kept.shape[0] // 2
+        given = jnp.where(low, kept[middle:], kept[:middle]).astype(BF16)
+        kept = jnp.where(low, kept[:middle], kept[middle:])
+        swaps = [(i, i ^ bit) for i in range(out)]
+        kept = kept + lax.ppermute(given, "out", swaps).astype(F32)
+        bit //= 2
+    grad_input = kept[0].astype(BF16).T
+
+    grad = contract_rows(all_tokens, jnp.concatenate([own_block, other_block], axis=1))
+    grad = (grad * factor).astype(BF16)
+    swapped = lax.all_to_all(grad.reshape(dep, feature_count // dep, 2 * width), "dep", 0, 0)
+
+    def columns(u, side):
         return [
-            jnp.concatenate(
-                [swapped[u * blocks + b][:, skips[b] :] for b in range(blocks)], axis=1
-            )
-            for u in range(2)
+            swapped[u * blocks + b][:, side * width + skips[b] : (side + 1) * width]
+            for b in range(blocks)
         ]
 
-    own_grads = weight_gradient(own)
-    other_grads = weight_gradient(other)
-    gate_grad, up_grad = (
-        jnp.concatenate([jnp.where(even, a, b), jnp.where(even, b, a)], axis=1)
-        for a, b in zip(own_grads, other_grads)
-    )
+    def assembled(u):
+        own_part = jnp.concatenate(columns(u, 0), axis=1)
+        other_part = jnp.concatenate(columns(u, 1), axis=1)
+        return jnp.concatenate(
+            [jnp.where(even, own_part, other_part), jnp.where(even, other_part, own_part)], axis=1
+        )
 
-    full = [jnp.where(even, own, other), jnp.where(even, other, own)]
-    input_terms = sum(
-        contract_cols(w[:, h * half : (h + 1) * half], full[h][:, u * half : (u + 1) * half])
-        for h in range(2)
-        for u, w in enumerate((w_gate, w_up))
-    ).astype(BF16)
-    shares = lax.all_to_all(
-        input_terms.reshape(out, feature_count // out, token_count), "out", 0, 0
-    )
-    grad_input = jnp.sum(shares.astype(F32), axis=0).astype(BF16).T
-    return grad_input, gate_grad, up_grad
+    return grad_input, assembled(0), assembled(1)
 
 
 def solution(mesh):

time: 210 us -> 196 us (0.933)
  the two profiles are of different devices: /device:TPU:8 before, /device:TPU:10 now
where the time goes in v2:
time: 196 us; the launch traced here: 195 us
  waiting for transfers between devices  63.1 us (32%)
  starting transfers between devices  53.7 us (27%)
  blocking collectives  36.3 us (19%)
  between operations  14.4 us (7%)
  matrix products  11.9 us (6%)
  local copies, waits for them, and re-layouts  10.6 us (5%)
  other arithmetic  5.35 us (3%)
    all_gather x1, blocking collectives, shards(): lax.all_gather(paired, 'inp', axis=0, tiled=True, axis_index_groups=alike)  36.3 us
    all_to_all x1, waiting for transfers between devices, shards(): lax.all_to_all(kept.reshape(group, rows, hidden), 'inp', 0, 0, axis_index...  29.9 us
    all_to_all x1, starting transfers between devices, shards(): lax.all_to_all(kept.reshape(group, rows, hidden), 'inp', 0, 0, axis_index...  18.1 us
    ppermute x1, waiting for transfers between devices, shards(): kept = (kept + lax.ppermute(given, 'inp', pairs).astype(F32)).astype(BF16)  15.4 us
    all_to_all x2, starting transfers between devices, column_block(): return lax.all_to_all(pieces, 'dep', 0, 0).reshape(dep * token_count, width)  11.4 us
    ppermute x2, waiting for transfers between devices, shards(): kept = kept + lax.ppermute(given, 'out', swaps).astype(F32)  10.2 us
    ppermute x2, starting transfers between devices, shards(): kept = kept + lax.ppermute(given, 'out', swaps).astype(F32)  9.19 us
    unnamed x24, local copies, waits for them, and re-layouts  9.03 us
  transfers between devices with their start and end apart: 10, of which 7 were waited for; matrix products, arithmetic and copies ran while one was open for 9% of the time, Pallas kernels for 0%

profile of v2, /device:TPU:10, one launch (start us, length us, event | category | flops | bytes accessed | tf_op | source)
XLA Modules:
  0.0 195.3 jit_solution(5443111258134481934)
XLA Ops:
  7.2 1.8 fusion.15
  9.0 1.6 fusion.23
  10.6 0.4 fusion.19
  11.5 4.3 %collective-permute-start = (bf16[192,1792]{1,0:T(8,128)(2,1)S(1)}, bf16[192,1792]{1,0:T(8,128)(2,1)S(1)}, u32[]{:S(2)}, u32[]{:S(2)}) collective-permute-start(bf16[192,1792]{1,0:T(8,128)(2,1)S(1)} %select_convert_fusion), channel_id=1, source_target_pairs={{0,64},{64,0},{128,192},{192,128},{256,320},{320,256},{384,448},{4... | collective-permute-start | bytes 2064392 | tf_op jit(solution)/shard_map/ppermute | solution.py:53
  15.8 15.4 %collective-permute-done = bf16[192,1792]{1,0:T(8,128)(2,1)S(1)} collective-permute-done((bf16[192,1792]{1,0:T(8,128)(2,1)S(1)}, bf16[192,1792]{1,0:T(8,128)(2,1)S(1)}, u32[]{:S(2)}, u32[]{:S(2)}) %collective-permute-start) | collective-permute-done | bytes 688160 | tf_op jit(solution)/shard_map/ppermute | solution.py:53
  31.2 1.1 add_convert_fusion
  32.3 18.1 %all-to-all-start = ((bf16[8,24,1792]{2,1,0:T(8,128)(2,1)}), bf16[8,24,1792]{2,1,0:T(8,128)(2,1)S(1)}, u32[]{:S(2)}, u32[]{:S(2)}) async-start(bf16[8,24,1792]{2,1,0:T(8,128)(2,1)} %bitcast), calls=%async_computation | async-start | bytes 1376256 | tf_op jit(solution)/shard_map/all_to_all | solution.py:54
  50.4 0.7 all-gather.2.cloned.1.call-update
  51.2 29.9 %all-to-all-done = bf16[8,24,1792]{2,1,0:T(8,128)(2,1)S(1)} async-done(((bf16[8,24,1792]{2,1,0:T(8,128)(2,1)}), bf16[8,24,1792]{2,1,0:T(8,128)(2,1)S(1)}, u32[]{:S(2)}, u32[]{:S(2)}) %all-to-all-start) | async-done | bytes 688160 | tf_op jit(solution)/shard_map/all_to_all | solution.py:54
  81.1 0.8 fusion.53
  82.0 36.3 %all_gather.6 = bf16[192,1792]{1,0:T(8,128)(2,1)S(1)} all-gather(bf16[24,1792]{1,0:T(8,128)(2,1)S(1)} %pad_maximum_fusion.8), channel_id=1, replica_groups={{0,128,256,384,512,640,768,896},{64,192,320,448,576,704,832,960},{1,129..., dimensions={0}, use_global_device_ids=true | all-gather | bytes 774144 | tf_op jit(solution)/shard_map/all_gather | solution.py:67
  118.3 3.9 %collective-permute-start.1 = (bf16[192,1792]{1,0:T(8,128)(2,1)S(1)}, bf16[192,1792]{1,0:T(8,128)(2,1)S(1)}, u32[]{:S(2)}, u32[]{:S(2)}) collective-permute-start(bf16[192,1792]{1,0:T(8,128)(2,1)S(1)} %all_gather.6), channel_id=1, source_target_pairs={{0,64},{64,0},{128,192},{192,128},{256,320},{320,256},{384,448},{4... | collective-permute-start | bytes 2064392 | tf_op jit(solution)/shard_map/ppermute | solution.py:68
  122.2 0.7 fusion.50
  122.9 0.6 fusion.49
  123.5 0.6 fusion.48
  124.2 0.6 fusion.47
  124.8 0.6 fusion.46
  125.4 0.6 fusion.45
  126.1 0.6 fusion.44
  126.7 0.6 fusion.43
  127.4 6.6 %all-to-all-start.1 = ((bf16[8,192,256]{2,1,0:T(8,128)(2,1)}), bf16[8,192,256]{2,1,0:T(8,128)(2,1)}, u32[]{:S(2)}, u32[]{:S(2)}) async-start(bf16[8,192,256]{2,1,0:T(8,128)(2,1)} %fusion.43), calls=%async_computation.1 | async-start | bytes 1572864 | tf_op jit(solution)/shard_map/all_to_all | solution.py:79
  133.9 0.6 fusion.42
  134.6 0.6 fusion.41
  135.2 0.6 fusion.40
  135.8 0.6 fusion.39
  136.5 0.6 fusion.38
  137.1 0.6 fusion.37
  137.8 0.6 fusion.36
  138.4 0.6 fusion.35
  139.1 0.9 broadcast_select_fusion.1
  140.0 1.6 fusion.13
  141.6 3.5 %all-to-all-done.1 = bf16[8,192,256]{2,1,0:T(8,128)(2,1)} async-done(((bf16[8,192,256]{2,1,0:T(8,128)(2,1)}), bf16[8,192,256]{2,1,0:T(8,128)(2,1)}, u32[]{:S(2)}, u32[]{:S(2)}) %all-to-all-start.1) | async-done | bytes 786464 | tf_op jit(solution)/shard_map/all_to_all | solution.py:79
  145.1 4.8 %all-to-all-start.2 = ((bf16[8,192,256]{2,1,0:T(8,128)(2,1)}), bf16[8,192,256]{2,1,0:T(8,128)(2,1)}, u32[]{:S(2)}, u32[]{:S(2)}) async-start(bf16[8,192,256]{2,1,0:T(8,128)(2,1)} %fusion.35), calls=%async_computation.2 | async-start | bytes 1572864 | tf_op jit(solution)/shard_map/all_to_all | solution.py:79
  149.9 1.6 fusion.17
  151.5 0.5 fusion.21
  152.0 0.5 fusion.12
  152.7 1.9 collective-permute-start.2
  154.6 1.3 collective-permute-done.2
  156.0 2.0 %all-to-all-done.2 = bf16[8,192,256]{2,1,0:T(8,128)(2,1)} async-done(((bf16[8,192,256]{2,1,0:T(8,128)(2,1)}), bf16[8,192,256]{2,1,0:T(8,128)(2,1)}, u32[]{:S(2)}, u32[]{:S(2)}) %all-to-all-start.2) | async-done | bytes 786464 | tf_op jit(solution)/shard_map/all_to_all | solution.py:79
  158.0 3.7 %fusion.7 = bf16[512,512]{0,1:T(8,128)(2,1)} fusion(bf16[1536,512]{1,0:T(8,128)(2,1)} %all-gather.2.cloned.1.call-done, bf16[1536,256]{1,0:T(8,128)(2,1)} %bitcast.27, bf16[1536,256]{1,0:T(8,128)(2,1)} %bitcast.18), kind=kOutput, calls=%fused_computation.10 | convolution fusion | flops 808976384 | bytes 3670016 | tf_op jit(solution)/shard_map/dot_general | solution.py:18
  161.8 4.9 %all-to-all-start.3 = ((bf16[8,64,512]{2,1,0:T(8,128)(2,1)}), bf16[8,64,512]{2,1,0:T(8,128)(2,1)S(1)}, u32[]{:S(2)}, u32[]{:S(2)}) async-start(bf16[8,64,512]{2,1,0:T(8,128)(2,1)} %bitcast.29), calls=%async_computation.3 | async-start | bytes 1048576 | tf_op jit(solution)/shard_map/all_to_all | solution.py:109
  166.7 6.7 %collective-permute-start.3 = (bf16[2,64,192]{2,1,0:T(8,128)(2,1)S(1)}, bf16[2,64,192]{2,1,0:T(8,128)(2,1)S(1)}, u32[]{:S(2)}, u32[]{:S(2)}) collective-permute-start(bf16[2,64,192]{2,1,0:T(8,128)(2,1)S(1)} %select_convert_fusion.2), channel_id=1, source_target_pairs={{0,32},{8,40},{16,48},{24,56},{32,0},{40,8},{48,16},{56,24},{1,33}... | collective-permute-start | bytes 147464 | tf_op jit(solution)/shard_map/ppermute | solution.py:103
  173.4 6.0 %collective-permute-done.3 = bf16[2,64,192]{2,1,0:T(8,128)(2,1)S(1)} collective-permute-done((bf16[2,64,192]{2,1,0:T(8,128)(2,1)S(1)}, bf16[2,64,192]{2,1,0:T(8,128)(2,1)S(1)}, u32[]{:S(2)}, u32[]{:S(2)}) %collective-permute-start.3) | collective-permute-done | bytes 49184 | tf_op jit(solution)/shard_map/ppermute | solution.py:103
  179.4 2.4 %collective-permute-start.4 = (bf16[1,64,192]{2,1,0:T(8,128)(2,1)S(1)}, bf16[1,64,192]{2,1,0:T(8,128)(2,1)S(1)}, u32[]{:S(2)}, u32[]{:S(2)}) collective-permute-start(bf16[1,64,192]{2,1,0:T(8,128)(2,1)S(1)} %select_convert_fusion.3), channel_id=1, source_target_pairs={{0,16},{8,24},{16,0},{24,8},{32,48},{40,56},{48,32},{56,40},{1,17}... | collective-permute-start | bytes 73736 | tf_op jit(solution)/shard_map/ppermute | solution.py:103
  181.9 4.3 %collective-permute-done.4 = bf16[1,64,192]{2,1,0:T(8,128)(2,1)S(1)} collective-permute-done((bf16[1,64,192]{2,1,0:T(8,128)(2,1)S(1)}, bf16[1,64,192]{2,1,0:T(8,128)(2,1)S(1)}, u32[]{:S(2)}, u32[]{:S(2)}) %collective-permute-start.4) | collective-permute-done | bytes 24608 | tf_op jit(solution)/shard_map/ppermute | solution.py:103
  186.2 0.6 fusion.56
  186.9 0.7 pad_maximum_fusion.2
  187.7 0.7 pad_maximum_fusion.3
  (31 shorter events, 1.2 us)
Async XLA Ops:
  7.2 1.8 copy-start
  7.2 3.4 %copy-start.1 = (bf16[512,1792]{1,0:T(8,128)(2,1)S(1)}, bf16[512,1792]{1,0:T(8,128)(2,1)}, u32[]{:S(2)}) copy-start(bf16[512,1792]{1,0:T(8,128)(2,1)} %param.6) | copy-start | bytes 5505028
  11.5 19.7 %collective-permute-start = (bf16[192,1792]{1,0:T(8,128)(2,1)S(1)}, bf16[192,1792]{1,0:T(8,128)(2,1)S(1)}, u32[]{:S(2)}, u32[]{:S(2)}) collective-permute-start(bf16[192,1792]{1,0:T(8,128)(2,1)S(1)} %select_convert_fusion), channel_id=1, source_target_pairs={{0,64},{64,0},{128,192},{192,128},{256,320},{320,256},{384,448},{4... | collective-permute-start | bytes 2064392 | tf_op jit(solution)/shard_map/ppermute | solution.py:53
  32.3 48.8 %all-to-all-start = ((bf16[8,24,1792]{2,1,0:T(8,128)(2,1)}), bf16[8,24,1792]{2,1,0:T(8,128)(2,1)S(1)}, u32[]{:S(2)}, u32[]{:S(2)}) async-start(bf16[8,24,1792]{2,1,0:T(8,128)(2,1)} %bitcast), calls=%async_computation | async-start | bytes 1376256 | tf_op jit(solution)/shard_map/all_to_all | solution.py:54
  50.4 105.6 %all-gather.2.cloned.1.call-start = ((), (), s32[]{:S(2)}) async-start(), calls=%async_computation.4 | async-start | bytes 1769472 | tf_op jit(solution)/shard_map/all_gather | solution.py:39
  118.3 15.6 %collective-permute-start.1 = (bf16[192,1792]{1,0:T(8,128)(2,1)S(1)}, bf16[192,1792]{1,0:T(8,128)(2,1)S(1)}, u32[]{:S(2)}, u32[]{:S(2)}) collective-permute-start(bf16[192,1792]{1,0:T(8,128)(2,1)S(1)} %all_gather.6), channel_id=1, source_target_pairs={{0,64},{64,0},{128,192},{192,128},{256,320},{320,256},{384,448},{4... | collective-permute-start | bytes 2064392 | tf_op jit(solution)/shard_map/ppermute | solution.py:68
  127.4 17.8 %all-to-all-start.1 = ((bf16[8,192,256]{2,1,0:T(8,128)(2,1)}), bf16[8,192,256]{2,1,0:T(8,128)(2,1)}, u32[]{:S(2)}, u32[]{:S(2)}) async-start(bf16[8,192,256]{2,1,0:T(8,128)(2,1)} %fusion.43), calls=%async_computation.1 | async-start | bytes 1572864 | tf_op jit(solution)/shard_map/all_to_all | solution.py:79
  137.8 2.2 %copy-start.3 = (bf16[512,1792]{1,0:T(8,128)(2,1)S(1)}, bf16[512,1792]{1,0:T(8,128)(2,1)}, u32[]{:S(2)}) copy-start(bf16[512,1792]{1,0:T(8,128)(2,1)} %param.7) | copy-start | bytes 5505028
  140.0 9.9 %copy-start.2 = (bf16[512,1792]{1,0:T(8,128)(2,1)S(1)}, bf16[512,1792]{1,0:T(8,128)(2,1)}, u32[]{:S(2)}) copy-start(bf16[512,1792]{1,0:T(8,128)(2,1)} %param.6) | copy-start | bytes 5505028
  145.1 12.9 %all-to-all-start.2 = ((bf16[8,192,256]{2,1,0:T(8,128)(2,1)}), bf16[8,192,256]{2,1,0:T(8,128)(2,1)}, u32[]{:S(2)}, u32[]{:S(2)}) async-start(bf16[8,192,256]{2,1,0:T(8,128)(2,1)} %fusion.35), calls=%async_computation.2 | async-start | bytes 1572864 | tf_op jit(solution)/shard_map/all_to_all | solution.py:79
  149.9 1.6 copy-start.4
  152.7 3.2 %collective-permute-start.2 = (bf16[4,64,192]{2,1,0:T(8,128)(2,1)S(1)}, bf16[4,64,192]{2,1,0:T(8,128)(2,1)S(1)}, u32[]{:S(2)}, u32[]{:S(2)}) collective-permute-start(bf16[4,64,192]{2,1,0:T(8,128)(2,1)S(1)} %fusion.34), channel_id=1, source_target_pairs={{0,8},{8,0},{16,24},{24,16},{32,40},{40,32},{48,56},{56,48},{1,9},... | collective-permute-start | bytes 294920 | tf_op jit(solution)/shard_map/ppermute | solution.py:95
  161.8 25.0 %all-to-all-start.3 = ((bf16[8,64,512]{2,1,0:T(8,128)(2,1)}), bf16[8,64,512]{2,1,0:T(8,128)(2,1)S(1)}, u32[]{:S(2)}, u32[]{:S(2)}) async-start(bf16[8,64,512]{2,1,0:T(8,128)(2,1)} %bitcast.29), calls=%async_computation.3 | async-start | bytes 1048576 | tf_op jit(solution)/shard_map/all_to_all | solution.py:109
  166.7 12.7 %collective-permute-start.3 = (bf16[2,64,192]{2,1,0:T(8,128)(2,1)S(1)}, bf16[2,64,192]{2,1,0:T(8,128)(2,1)S(1)}, u32[]{:S(2)}, u32[]{:S(2)}) collective-permute-start(bf16[2,64,192]{2,1,0:T(8,128)(2,1)S(1)} %select_convert_fusion.2), channel_id=1, source_target_pairs={{0,32},{8,40},{16,48},{24,56},{32,0},{40,8},{48,16},{56,24},{1,33}... | collective-permute-start | bytes 147464 | tf_op jit(solution)/shard_map/ppermute | solution.py:103
  179.4 6.7 %collective-permute-start.4 = (bf16[1,64,192]{2,1,0:T(8,128)(2,1)S(1)}, bf16[1,64,192]{2,1,0:T(8,128)(2,1)S(1)}, u32[]{:S(2)}, u32[]{:S(2)}) collective-permute-start(bf16[1,64,192]{2,1,0:T(8,128)(2,1)S(1)} %select_convert_fusion.3), channel_id=1, source_target_pairs={{0,16},{8,24},{16,0},{24,8},{32,48},{40,56},{48,32},{56,40},{1,17}... | collective-permute-start | bytes 73736 | tf_op jit(solution)/shard_map/ppermute | solution.py:103
Sparse Core Ops, SparseCore 0:
  53.9 49.6 all-gather.1

commit v3 on v2

v3 whole, which is shorter than its diff:
```python
import functools
import math

import jax
import jax.numpy as jnp
from jax import lax
from jax.experimental import pallas as pl
from jax.experimental.pallas import tpu as pltpu
from jax.sharding import PartitionSpec as P

BF16 = jnp.bfloat16
F32 = jnp.float32
LANES = 128
ROWS_BY_COLS = (((1,), (0,)), ((), ()))
COLS_BY_COLS = (((1,), (1,)), ((), ()))


def values_kernel(side_ref, tokens_ref, gate_ref, up_ref, out_ref):
    del side_ref
    half = gate_ref.shape[1]
    tokens = tokens_ref[...]
    for u, w_ref in enumerate((gate_ref, up_ref)):
        part = lax.dot_general(tokens, w_ref[...], ROWS_BY_COLS, preferred_element_type=F32)
        out_ref[:, u * half : (u + 1) * half] = part.astype(out_ref.dtype)


def partial_values(side, tokens, w_gate, w_up, dtype):
    token_count, feature_count = tokens.shape
    half = w_gate.shape[1] // 2
    weights = pl.BlockSpec((feature_count, half), lambda g, s: (0, s[0]))
    return pl.pallas_call(
        values_kernel,
        out_shape=jax.ShapeDtypeStruct((token_count, 2 * half), dtype),
        grid_spec=pltpu.PrefetchScalarGridSpec(
            num_scalar_prefetch=1,
            grid=(1,),
            in_specs=[
                pl.BlockSpec((token_count, feature_count), lambda g, s: (0, 0)),
                weights,
                weights,
            ],
            out_specs=pl.BlockSpec((token_count, 2 * half), lambda g, s: (0, 0)),
        ),
        compiler_params=pltpu.CompilerParams(vmem_limit_bytes=24 * 2**20),
        cost_estimate=pl.CostEstimate(
            flops=4 * token_count * feature_count * half,
            bytes_accessed=4 * feature_count * half + 8 * token_count * half,
            transcendentals=0,
        ),
    )(side, tokens, w_gate, w_up)


def grads_kernel(starts, terms_ref, cotangent_ref, pieces_ref):
    half = cotangent_ref.shape[1]
    width = pieces_ref.shape[2]
    values = terms_ref[0].astype(F32)
    for k in range(1, terms_ref.shape[0]):
        values = values + terms_ref[k].astype(F32)
    gate_value = values[:, :half]
    up_value = values[:, half:]
    cotangent = cotangent_ref[...].astype(F32)
    sigmoid_gate = jax.nn.sigmoid(gate_value)
    grad_gate = cotangent * up_value * sigmoid_gate * (1.0 + gate_value * (1.0 - sigmoid_gate))
    grad_upper = cotangent * gate_value * sigmoid_gate
    for u, grad in enumerate((grad_gate, grad_upper)):
        grad = grad.astype(BF16)
        for b, start in enumerate(starts):
            pieces_ref[u * len(starts) + b] = grad[:, start : start + width]


def grad_pieces(terms, cotangent, starts, width):
    rows, half = cotangent.shape
    return pl.pallas_call(
        functools.partial(grads_kernel, starts),
        out_shape=jax.ShapeDtypeStruct((2 * len(starts), rows, width), BF16),
        compiler_params=pltpu.CompilerParams(vmem_limit_bytes=16 * 2**20),
        cost_estimate=pl.CostEstimate(
            flops=40 * rows * half,
            bytes_accessed=2 * terms.size + 8 * rows * half,
            transcendentals=rows * half,
        ),
    )(terms, cotangent)


def input_kernel(starts, skips, side_ref, gate_ref, up_ref, pieces_ref, *rest):
    total_ref, out_ref = rest if len(rest) == 2 else (None, rest[0])
    del side_ref
    width = pieces_ref.shape[2]
    total = None if total_ref is None else total_ref[...]
    for u, w_ref in enumerate((gate_ref, up_ref)):
        for b, (start, skip) in enumerate(zip(starts, skips)):
            term = lax.dot_general(
                w_ref[:, start + skip : start + width],
                pieces_ref[u * len(starts) + b][:, skip:],
                COLS_BY_COLS,
                preferred_element_type=F32,
            )
            total = term if total is None else total + term
    out_ref[...] = total


def input_terms(side, w_gate, w_up, pieces, starts, skips, total=None):
    feature_count = w_gate.shape[0]
    half = w_gate.shape[1] // 2
    token_count = pieces.shape[1]
    weights = pl.BlockSpec((feature_count, half), lambda g, s: (0, s[0]))
    result = pl.BlockSpec((feature_count, token_count), lambda g, s: (0, 0))
    more = () if total is None else (total,)
    return pl.pallas_call(
        functools.partial(input_kernel, starts, skips),
        out_shape=jax.ShapeDtypeStruct((feature_count, token_count), F32),
        grid_spec=pltpu.PrefetchScalarGridSpec(
            num_scalar_prefetch=1,
            grid=(1,),
            in_specs=[weights, weights, pl.BlockSpec(pieces.shape, lambda g, s: (0, 0, 0))]
            + [result] * len(more),
            out_specs=result,
        ),
        compiler_params=pltpu.CompilerParams(vmem_limit_bytes=24 * 2**20),
        cost_estimate=pl.CostEstimate(
            flops=4 * token_count * feature_count * half,
            bytes_accessed=4 * feature_count * half + 8 * token_count * half,
            transcendentals=0,
        ),
    )(side, w_gate, w_up, pieces, *more)


def weight_kernel(factor, tokens_ref, own_ref, other_ref, out_ref):
    dep = tokens_ref.shape[0]
    width = own_ref.shape[2]
    for side, block_ref in enumerate((own_ref, other_ref)):
        total = None
        for d in range(dep):
            term = lax.dot_general(
                tokens_ref[d], block_ref[d], ROWS_BY_COLS, preferred_element_type=F32
            )
            total = term if total is None else total + term
        out_ref[:, side * width : (side + 1) * width] = (total * factor).astype(BF16)


def weight_terms(tokens, own, other, factor):
    dep, feature_count, token_count = tokens.shape
    width = own.shape[2]
    return pl.pallas_call(
        functools.partial(weight_kernel, factor),
        out_shape=jax.ShapeDtypeStruct((feature_count, 2 * width), BF16),
        compiler_params=pltpu.CompilerParams(vmem_limit_bytes=24 * 2**20),
        cost_estimate=pl.CostEstimate(
            flops=4 * dep * token_count * feature_count * width,
            bytes_accessed=2 * dep * token_count * (feature_count + 2 * width),
            transcendentals=0,
        ),
    )(tokens, own, other)


def shards(tokens, grad_hidden, w_gate, w_up):
    token_count, feature_count = tokens.shape
    hidden = w_gate.shape[1]
    inp, out, dep = (lax.axis_size(name) for name in ("inp", "out", "dep"))
    factor = 1.0 / math.sqrt(token_count * dep)
    half = hidden // 2
    group = inp // 2
    rows = token_count // group
    pairs = [(i, i ^ 1) for i in range(inp)]
    alike = [[p + 2 * i for i in range(group)] for p in range(2)]
    place = lax.axis_index("inp")
    parity = place % 2
    even = parity == 0
    own_side = parity.reshape(1)
    other_side = 1 - own_side

    given = partial_values(other_side, tokens, w_gate, w_up, BF16)
    kept = partial_values(own_side, tokens, w_gate, w_up, F32)
    kept = (kept + lax.ppermute(given, "inp", pairs).astype(F32)).astype(BF16)

    all_tokens = lax.all_gather(tokens.T, "dep", axis=0)

    terms = lax.all_to_all(
        kept.reshape(group, rows, hidden), "inp", 0, 0, axis_index_groups=alike
    )
    cotangent = lax.dynamic_slice(
        grad_hidden, ((place // 2) * rows, parity * half), (rows, half)
    )

    width = 2 * LANES
    blocks = dep // 2
    starts = [min(b * width, half - width) for b in range(blocks)]
    skips = [b * width - s for b, s in enumerate(starts)]
    pieces = grad_pieces(terms, cotangent, starts, width)
    own = lax.all_gather(pieces, "inp", axis=1, tiled=True, axis_index_groups=alike)
    other = lax.ppermute(own, "inp", pairs)

    shares = input_terms(own_side, w_gate, w_up, own, starts, skips)
    own, shares = lax.optimization_barrier((own, shares))
    own_block = lax.all_to_all(own, "dep", 0, 0)
    shares = input_terms(other_side, w_gate, w_up, other, starts, skips, shares)
    other, shares, all_tokens = lax.optimization_barrier((other, shares, all_tokens))
    other_block = lax.all_to_all(other, "dep", 0, 0)
    at_out = lax.axis_index("out")
    shares = shares.reshape(out // 2, 2, feature_count // out, token_count)
    low = at_out % 2 == 0
    given = jnp.where(low, shares[:, 1], shares[:, 0]).astype(BF16)
    kept = jnp.where(low, shares[:, 0], shares[:, 1])
    kept = kept + lax.ppermute(given, "out", [(i, i ^ 1) for i in range(out)]).astype(F32)
    bit = out // 2
    while bit > 1:
        low = at_out & bit == 0
        middle = kept.shape[0] // 2
        given = jnp.where(low, kept[middle:], kept[:middle]).astype(BF16)
        kept = jnp.where(low, kept[:middle], kept[middle:])
        swaps = [(i, i ^ bit) for i in range(out)]
        kept = kept + lax.ppermute(given, "out", swaps).astype(F32)
        if bit == out // 2:
            own_block, kept = lax.optimization_barrier((own_block, kept))
        bit //= 2
    grad_input = kept[0].astype(BF16).T

    grad = weight_terms(all_tokens, own_block, other_block, factor)
    swapped = lax.all_to_all(grad.reshape(dep, feature_count // dep, 2 * width), "dep", 0, 0)

    def columns(u, side):
        return [
            swapped[u * blocks + b][:, side * width + skips[b] : (side + 1) * width]
            for b in range(blocks)
        ]

    def assembled(u):
        own_part = jnp.concatenate(columns(u, 0), axis=1)
        other_part = jnp.concatenate(columns(u, 1), axis=1)
        return jnp.concatenate(
            [jnp.where(even, own_part, other_part), jnp.where(even, other_part, own_part)], axis=1
        )

    return grad_input, assembled(0), assembled(1)


def solution(mesh):
    return jax.shard_map(
        shards,
        mesh=mesh,
        in_specs=(P("dep", "inp"), P("dep", "out"), P("inp", "out"), P("inp", "out")),
        out_specs=(P("dep", ("inp", "out")), P(("inp", "dep"), "out"), P(("inp", "dep"), "out")),
        check_vma=False,
    )
```

time: 196 us -> 200 us (1.020)
  matrix products: 11.9 us -> 0 us
  Pallas kernels: 0 us -> 7.21 us
  local copies, waits for them, and re-layouts: 10.6 us -> 15.5 us
  starting transfers between devices: 53.7 us -> 57.5 us
  blocking collectives: 36.3 us -> 39.2 us
  waiting for transfers between devices: 63.1 us -> 61.1 us
    dot_general x9 -> x0, matrix products: 11.9 us -> none  [the longest x4 4.11 us: product(): return jnp.dot(left, right, preferred_element_type=F32)]
    pallas_call x0 -> x6, Pallas kernels: none -> 7.21 us  [the longest x1 3.17 us: weight_terms(): pl.pallas_call(functools.partial(weight_kernel, factor), out_shape=jax.Sh...]
    ppermute x1, waiting for transfers between devices: 0.01 us -> 6.3 us  [shards(): other = lax.ppermute(own, 'inp', pairs)]
    all_to_all x2, waiting for transfers between devices: 5.55 us -> 0.01 us  [the longest x1 0.01 us: shards(): other_block = lax.all_to_all(other, 'dep', 0, 0)]
    all_gather x0 -> x1, local copies, waits for them, and re-layouts: none -> 3.83 us  [shards(): all_tokens = lax.all_gather(tokens.T, 'dep', axis=0)]
    all_gather x1, blocking collectives: 36.3 us -> 39.2 us  [shards(): lax.all_gather(pieces, 'inp', axis=1, tiled=True, axis_index_groups=alike)]
  transfers between devices with their start and end apart: 10 -> 10, of which waited for: 7 -> 6; matrix products, arithmetic and copies ran while one was open for 9% -> 3% of each run, Pallas kernels for 0% -> 2%
where the time goes in v3:
time: 200 us; the launch traced here: 199 us
  waiting for transfers between devices  61.1 us (31%)
  starting transfers between devices  57.5 us (29%)
  blocking collectives  39.2 us (20%)
  local copies, waits for them, and re-layouts  15.5 us (8%)
  between operations  14.3 us (7%)
  Pallas kernels  7.21 us (4%)
  other arithmetic  3.91 us (2%)
    all_gather x1, blocking collectives, shards(): lax.all_gather(pieces, 'inp', axis=1, tiled=True, axis_index_groups=alike)  39.2 us
    all_to_all x1, waiting for transfers between devices, shards(): lax.all_to_all(kept.reshape(group, rows, hidden), 'inp', 0, 0, axis_index...  29 us
    all_to_all x1, starting transfers between devices, shards(): lax.all_to_all(kept.reshape(group, rows, hidden), 'inp', 0, 0, axis_index...  18.1 us
    ppermute x1, waiting for transfers between devices, shards(): kept = (kept + lax.ppermute(given, 'inp', pairs).astype(F32)).astype(BF16)  14.8 us
    ppermute x2, starting transfers between devices, shards(): kept = kept + lax.ppermute(given, 'out', swaps).astype(F32)  10.8 us
    unnamed x24, local copies, waits for them, and re-layouts  10.8 us
    ppermute x2, waiting for transfers between devices, shards(): kept = kept + lax.ppermute(given, 'out', swaps).astype(F32)  8.8 us
    ppermute x1, waiting for transfers between devices, shards(): other = lax.ppermute(own, 'inp', pairs)  6.3 us
  transfers between devices with their start and end apart: 10, of which 6 were waited for; matrix products, arithmetic and copies ran while one was open for 3% of the time, Pallas kernels for 2%

profile of v3, /device:TPU:10, one launch (start us, length us, event | category | flops | bytes accessed | tf_op | source)
XLA Modules:
  0.0 198.8 jit_solution(17274027136122782087)
XLA Ops:
  7.2 0.0 copy-start
  7.2 1.5 copy-done
  8.7 1.5 copy-done.2
  10.2 0.9 copy-done.10
  11.1 0.6 shard_map.68
  11.7 4.3 %collective-permute-start = (bf16[192,1792]{1,0:T(8,128)(2,1)S(1)}, bf16[192,1792]{1,0:T(8,128)(2,1)S(1)}, u32[]{:S(2)}, u32[]{:S(2)}) collective-permute-start(bf16[192,1792]{1,0:T(8,128)(2,1)S(1)} %shard_map.68), channel_id=1, source_target_pairs={{0,64},{64,0},{128,192},{192,128},{256,320},{320,256},{384,448},{4... | collective-permute-start | bytes 2064392 | tf_op jit(solution)/shard_map/ppermute | solution.py:174
  16.0 0.0 copy-done.1
  16.0 0.0 copy-done.11
  16.0 0.6 shard_map.67
  16.6 14.8 %collective-permute-done = bf16[192,1792]{1,0:T(8,128)(2,1)S(1)} collective-permute-done((bf16[192,1792]{1,0:T(8,128)(2,1)S(1)}, bf16[192,1792]{1,0:T(8,128)(2,1)S(1)}, u32[]{:S(2)}, u32[]{:S(2)}) %collective-permute-start) | collective-permute-done | bytes 688160 | tf_op jit(solution)/shard_map/ppermute | solution.py:174
  31.4 1.0 add_convert_fusion
  32.4 18.1 %all-to-all-start = ((bf16[8,24,1792]{2,1,0:T(8,128)(2,1)}), bf16[8,24,1792]{2,1,0:T(8,128)(2,1)S(1)}, u32[]{:S(2)}, u32[]{:S(2)}) async-start(bf16[8,24,1792]{2,1,0:T(8,128)(2,1)} %bitcast.1), calls=%async_computation | async-start | bytes 1376256 | tf_op jit(solution)/shard_map/all_to_all | solution.py:178
  50.5 0.0 all-gather.3.cloned.1.call-start
  50.6 0.7 all-gather.3.cloned.1.call-update
  51.3 0.8 dynamic_slice.3.cotangent_ref
  52.1 29.0 %all-to-all-done.terms_ref = bf16[8,24,1792]{2,1,0:T(8,128)(2,1)S(1)} async-done(((bf16[8,24,1792]{2,1,0:T(8,128)(2,1)}), bf16[8,24,1792]{2,1,0:T(8,128)(2,1)S(1)}, u32[]{:S(2)}, u32[]{:S(2)}) %all-to-all-start) | async-done | bytes 688160 | tf_op jit(solution)/shard_map/all_to_all | solution.py:178
  81.1 0.1 shard_map.69
  81.2 39.2 %all_gather.9.pieces_ref = bf16[8,192,256]{2,1,0:T(8,128)(2,1)} all-gather(bf16[8,24,256]{2,1,0:T(8,128)(2,1)S(1)} %shard_map.69), channel_id=1, replica_groups={{0,128,256,384,512,640,768,896},{64,192,320,448,576,704,832,960},{1,129..., dimensions={1}, use_global_device_ids=true | all-gather | bytes 884736 | tf_op jit(solution)/shard_map/all_gather | solution.py:190
  120.5 1.5 copy-done.3
  122.0 2.0 %shard_map.70.rest_0_ = f32[512,192]{1,0:T(8,128)S(1)} custom-call(s32[1]{0:T(128)} %bitcast.side_ref, bf16[512,1792]{1,0:T(8,128)(2,1)S(1)} %copy-done.1, bf16[512,1792]{1,0:T(8,128)(2,1)S(1)} %copy-done.3, bf16[8,192,256]{2,1,0:T(8,128)(2,1)} %all_gather.9.pieces_ref), custom_call_target="tpu_custom_call" | custom-call | flops 352321536 | bytes 3211264 | tf_op jit(solution)/shard_map/pallas_call | solution.py:109
  124.0 0.0 copy-start.8
  124.0 0.8 copy-done.8
  124.8 5.9 %all-to-all-start.1 = ((bf16[8,192,256]{2,1,0:T(8,128)(2,1)}), bf16[8,192,256]{2,1,0:T(8,128)(2,1)S(1)}, u32[]{:S(2)}, u32[]{:S(2)}) async-start(bf16[8,192,256]{2,1,0:T(8,128)(2,1)} %all_gather.9.pieces_ref), calls=%async_computation.1 | async-start | bytes 1572864 | tf_op jit(solution)/shard_map/all_to_all | solution.py:195
  130.7 4.8 %collective-permute-start.1 = (bf16[8,192,256]{2,1,0:T(8,128)(2,1)}, bf16[8,192,256]{2,1,0:T(8,128)(2,1)S(1)}, u32[]{:S(2)}, u32[]{:S(2)}) collective-permute-start(bf16[8,192,256]{2,1,0:T(8,128)(2,1)} %all_gather.9.pieces_ref), channel_id=1, source_target_pairs={{0,64},{64,0},{128,192},{192,128},{256,320},{320,256},{384,448},{4... | collective-permute-start | bytes 2359304 | tf_op jit(solution)/shard_map/ppermute | solution.py:191
  135.5 0.0 all-gather.3.cloned.1.call-done
  135.6 3.8 %copy.7 = bf16[4096,192]{1,0:T(8,128)(2,1)} copy(bf16[4096,192]{0,1:T(8,128)(2,1)} %all-gather.3.cloned.1.call-done) | data formatting | bytes 3145728 | tf_op jit(solution)/shard_map/all_gather | solution.py:176
  139.4 6.3 %collective-permute-done.1.pieces_ref = bf16[8,192,256]{2,1,0:T(8,128)(2,1)S(1)} collective-permute-done((bf16[8,192,256]{2,1,0:T(8,128)(2,1)}, bf16[8,192,256]{2,1,0:T(8,128)(2,1)S(1)}, u32[]{:S(2)}, u32[]{:S(2)}) %collective-permute-start.1) | collective-permute-done | bytes 786464 | tf_op jit(solution)/shard_map/ppermute | solution.py:191
  145.7 0.9 copy-done.6
  146.6 1.5 copy-done.4
  148.1 1.1 copy-done.7
  149.2 1.0 copy-done.9
  150.3 0.7 shard_map.71
  151.0 0.0 all-to-all-done.1.own_ref
  151.0 5.9 %all-to-all-start.2 = ((bf16[8,192,256]{2,1,0:T(8,128)(2,1)}), bf16[8,192,256]{2,1,0:T(8,128)(2,1)}, u32[]{:S(2)}, u32[]{:S(2)}) async-start(bf16[8,192,256]{2,1,0:T(8,128)(2,1)} %copy-done.6), calls=%async_computation.2 | async-start | bytes 1572864 | tf_op jit(solution)/shard_map/all_to_all | solution.py:198
  156.9 0.7 fusion
  157.6 1.9 collective-permute-start.2
  159.5 1.5 collective-permute-done.2
  161.1 6.2 %collective-permute-start.3 = (bf16[2,64,192]{2,1,0:T(8,128)(2,1)S(1)}, bf16[2,64,192]{2,1,0:T(8,128)(2,1)S(1)}, u32[]{:S(2)}, u32[]{:S(2)}) collective-permute-start(bf16[2,64,192]{2,1,0:T(8,128)(2,1)S(1)} %select_convert_fusion.1), channel_id=1, source_target_pairs={{0,32},{8,40},{16,48},{24,56},{32,0},{40,8},{48,16},{56,24},{1,33}... | collective-permute-start | bytes 147464 | tf_op jit(solution)/shard_map/ppermute | solution.py:212
  167.3 3.9 %collective-permute-done.3 = bf16[2,64,192]{2,1,0:T(8,128)(2,1)S(1)} collective-permute-done((bf16[2,64,192]{2,1,0:T(8,128)(2,1)S(1)}, bf16[2,64,192]{2,1,0:T(8,128)(2,1)S(1)}, u32[]{:S(2)}, u32[]{:S(2)}) %collective-permute-start.3) | collective-permute-done | bytes 49184 | tf_op jit(solution)/shard_map/ppermute | solution.py:212
  171.2 0.0 all-to-all-done.2.other_ref
  171.2 3.2 %shard_map.72 = bf16[512,512]{1,0:T(8,128)(2,1)} custom-call(bf16[8,512,192]{2,1,0:T(8,128)(2,1)S(1)} %bitcast.46, bf16[8,192,256]{2,1,0:T(8,128)(2,1)S(1)} %all-to-all-done.1.own_ref, bf16[8,192,256]{2,1,0:T(8,128)(2,1)} %all-to-all-done.2.other_ref), custom_call_target="tpu_custom_call" | custom-call | flops 805306368 | bytes 3145728 | tf_op jit(solution)/shard_map/pallas_call | solution.py:144
  174.4 5.7 %all-to-all-start.3 = ((bf16[8,64,512]{2,1,0:T(8,128)(2,1)}), bf16[8,64,512]{2,1,0:T(8,128)(2,1)S(1)}, u32[]{:S(2)}, u32[]{:S(2)}) async-start(bf16[8,64,512]{2,1,0:T(8,128)(2,1)} %bitcast.9), calls=%async_computation.3 | async-start | bytes 1048576 | tf_op jit(solution)/shard_map/all_to_all | solution.py:219
  180.1 4.6 %collective-permute-start.4 = (bf16[1,64,192]{2,1,0:T(8,128)(2,1)S(1)}, bf16[1,64,192]{2,1,0:T(8,128)(2,1)S(1)}, u32[]{:S(2)}, u32[]{:S(2)}) collective-permute-start(bf16[1,64,192]{2,1,0:T(8,128)(2,1)S(1)} %select_convert_fusion.2), channel_id=1, source_target_pairs={{0,16},{8,24},{16,0},{24,8},{32,48},{40,56},{48,32},{56,40},{1,17}... | collective-permute-start | bytes 73736 | tf_op jit(solution)/shard_map/ppermute | solution.py:212
  184.7 4.9 %collective-permute-done.4 = bf16[1,64,192]{2,1,0:T(8,128)(2,1)S(1)} collective-permute-done((bf16[1,64,192]{2,1,0:T(8,128)(2,1)S(1)}, bf16[1,64,192]{2,1,0:T(8,128)(2,1)S(1)}, u32[]{:S(2)}, u32[]{:S(2)}) %collective-permute-start.4) | collective-permute-done | bytes 24608 | tf_op jit(solution)/shard_map/ppermute | solution.py:212
  189.7 0.6 fusion.1
  190.3 0.0 all-to-all-done.3
  190.4 0.7 pad_maximum_fusion.1
  191.2 0.7 pad_maximum_fusion
  (22 shorter events, 0.3 us)
Async XLA Ops:
  7.2 1.5 copy-start
  8.7 1.5 copy-start.2
  10.2 0.9 copy-start.10
  11.1 4.9 %copy-start.1 = (bf16[512,1792]{1,0:T(8,128)(2,1)S(1)}, bf16[512,1792]{1,0:T(8,128)(2,1)}, u32[]{:S(2)}) copy-start(bf16[512,1792]{1,0:T(8,128)(2,1)} %gate_ref.7) | copy-start | bytes 5505028
  11.1 4.9 %copy-start.11 = (bf16[192,512]{1,0:T(8,128)(2,1)S(1)}, bf16[192,512]{1,0:T(8,128)(2,1)}, u32[]{:S(2)}) copy-start(bf16[192,512]{1,0:T(8,128)(2,1)} %tokens_ref.3) | copy-start | bytes 589828
  11.7 19.7 %collective-permute-start = (bf16[192,1792]{1,0:T(8,128)(2,1)S(1)}, bf16[192,1792]{1,0:T(8,128)(2,1)S(1)}, u32[]{:S(2)}, u32[]{:S(2)}) collective-permute-start(bf16[192,1792]{1,0:T(8,128)(2,1)S(1)} %shard_map.68), channel_id=1, source_target_pairs={{0,64},{64,0},{128,192},{192,128},{256,320},{320,256},{384,448},{4... | collective-permute-start | bytes 2064392 | tf_op jit(solution)/shard_map/ppermute | solution.py:174
  32.4 48.7 %all-to-all-start = ((bf16[8,24,1792]{2,1,0:T(8,128)(2,1)}), bf16[8,24,1792]{2,1,0:T(8,128)(2,1)S(1)}, u32[]{:S(2)}, u32[]{:S(2)}) async-start(bf16[8,24,1792]{2,1,0:T(8,128)(2,1)} %bitcast.1), calls=%async_computation | async-start | bytes 1376256 | tf_op jit(solution)/shard_map/all_to_all | solution.py:178
  50.5 85.0 %all-gather.3.cloned.1.call-start = ((), (), s32[]{:S(2)}) async-start(), calls=%async_computation.4 | async-start | bytes 1769472 | tf_op jit(solution)/shard_map/all_gather | solution.py:176
  120.5 1.5 copy-start.3
  124.0 0.8 copy-start.8
  124.8 26.2 %all-to-all-start.1 = ((bf16[8,192,256]{2,1,0:T(8,128)(2,1)}), bf16[8,192,256]{2,1,0:T(8,128)(2,1)S(1)}, u32[]{:S(2)}, u32[]{:S(2)}) async-start(bf16[8,192,256]{2,1,0:T(8,128)(2,1)} %all_gather.9.pieces_ref), calls=%async_computation.1 | async-start | bytes 1572864 | tf_op jit(solution)/shard_map/all_to_all | solution.py:195
  130.7 15.0 %collective-permute-start.1 = (bf16[8,192,256]{2,1,0:T(8,128)(2,1)}, bf16[8,192,256]{2,1,0:T(8,128)(2,1)S(1)}, u32[]{:S(2)}, u32[]{:S(2)}) collective-permute-start(bf16[8,192,256]{2,1,0:T(8,128)(2,1)} %all_gather.9.pieces_ref), channel_id=1, source_target_pairs={{0,64},{64,0},{128,192},{192,128},{256,320},{320,256},{384,448},{4... | collective-permute-start | bytes 2359304 | tf_op jit(solution)/shard_map/ppermute | solution.py:191
  145.7 0.9 copy-start.6
  146.6 1.5 copy-start.4
  148.1 1.1 copy-start.7
  149.2 1.0 copy-start.9
  151.0 20.2 %copy-start.5 = (bf16[4096,192]{1,0:T(8,128)(2,1)S(1)}, bf16[4096,192]{1,0:T(8,128)(2,1)}, u32[]{:S(2)}) copy-start(bf16[4096,192]{1,0:T(8,128)(2,1)} %copy.7) | copy-start | bytes 4718596
  151.0 20.1 %all-to-all-start.2 = ((bf16[8,192,256]{2,1,0:T(8,128)(2,1)}), bf16[8,192,256]{2,1,0:T(8,128)(2,1)}, u32[]{:S(2)}, u32[]{:S(2)}) async-start(bf16[8,192,256]{2,1,0:T(8,128)(2,1)} %copy-done.6), calls=%async_computation.2 | async-start | bytes 1572864 | tf_op jit(solution)/shard_map/all_to_all | solution.py:198
  157.6 3.4 %collective-permute-start.2 = (bf16[4,64,192]{2,1,0:T(8,128)(2,1)}, bf16[4,64,192]{2,1,0:T(8,128)(2,1)S(1)}, u32[]{:S(2)}, u32[]{:S(2)}) collective-permute-start(bf16[4,64,192]{2,1,0:T(8,128)(2,1)} %fusion), channel_id=1, source_target_pairs={{0,8},{8,0},{16,24},{24,16},{32,40},{40,32},{48,56},{56,48},{1,9},... | collective-permute-start | bytes 294920 | tf_op jit(solution)/shard_map/ppermute | solution.py:204
  161.1 10.1 %collective-permute-start.3 = (bf16[2,64,192]{2,1,0:T(8,128)(2,1)S(1)}, bf16[2,64,192]{2,1,0:T(8,128)(2,1)S(1)}, u32[]{:S(2)}, u32[]{:S(2)}) collective-permute-start(bf16[2,64,192]{2,1,0:T(8,128)(2,1)S(1)} %select_convert_fusion.1), channel_id=1, source_target_pairs={{0,32},{8,40},{16,48},{24,56},{32,0},{40,8},{48,16},{56,24},{1,33}... | collective-permute-start | bytes 147464 | tf_op jit(solution)/shard_map/ppermute | solution.py:212
  174.4 15.9 %all-to-all-start.3 = ((bf16[8,64,512]{2,1,0:T(8,128)(2,1)}), bf16[8,64,512]{2,1,0:T(8,128)(2,1)S(1)}, u32[]{:S(2)}, u32[]{:S(2)}) async-start(bf16[8,64,512]{2,1,0:T(8,128)(2,1)} %bitcast.9), calls=%async_computation.3 | async-start | bytes 1048576 | tf_op jit(solution)/shard_map/all_to_all | solution.py:219
  180.1 9.6 %collective-permute-start.4 = (bf16[1,64,192]{2,1,0:T(8,128)(2,1)S(1)}, bf16[1,64,192]{2,1,0:T(8,128)(2,1)S(1)}, u32[]{:S(2)}, u32[]{:S(2)}) collective-permute-start(bf16[1,64,192]{2,1,0:T(8,128)(2,1)S(1)} %select_convert_fusion.2), channel_id=1, source_target_pairs={{0,16},{8,24},{16,0},{24,8},{32,48},{40,56},{48,32},{56,40},{1,17}... | collective-permute-start | bytes 73736 | tf_op jit(solution)/shard_map/ppermute | solution.py:212
Sparse Core Ops, SparseCore 0:
  54.0 49.7 all-gather.2

commit v4 on v3

v4 whole, which is shorter than its diff:
```python
import functools
import math

import jax
import jax.numpy as jnp
from jax import lax
from jax.experimental import pallas as pl
from jax.experimental.pallas import tpu as pltpu
from jax.sharding import PartitionSpec as P

BF16 = jnp.bfloat16
F32 = jnp.float32
LANES = 128
CHUNKS = 2
ROWS_BY_COLS = (((1,), (0,)), ((), ()))
COLS_BY_COLS = (((1,), (1,)), ((), ()))


def fetch_half(side, hbm_refs, vmem_refs, sems):
    copies = []
    for w, (src, dst) in enumerate(zip(hbm_refs, vmem_refs)):
        half = dst.shape[1]
        rows = dst.shape[0] // CHUNKS
        first = pl.multiple_of(side * half, LANES)
        for c in range(CHUNKS):
            copy = pltpu.make_async_copy(
                src.at[pl.ds(c * rows, rows), pl.ds(first, half)],
                dst.at[pl.ds(c * rows, rows), :],
                sems.at[w, c],
            )
            copy.start()
            copies.append(copy)
    return copies


def values_kernel(side_ref, tokens_ref, gate_hbm, up_hbm, out_ref, gate_ref, up_ref, sems):
    copies = fetch_half(side_ref[0], (gate_hbm, up_hbm), (gate_ref, up_ref), sems)
    half = gate_ref.shape[1]
    for u, w_ref in enumerate((gate_ref, up_ref)):
        for copy in copies[u * CHUNKS : (u + 1) * CHUNKS]:
            copy.wait()
        part = lax.dot_general(
            tokens_ref[...], w_ref[...], ROWS_BY_COLS, preferred_element_type=F32
        )
        out_ref[:, u * half : (u + 1) * half] = part.astype(out_ref.dtype)


def half_scratch(w_gate):
    half = pltpu.VMEM((w_gate.shape[0], w_gate.shape[1] // 2), BF16)
    return [half, half, pltpu.SemaphoreType.DMA((2, CHUNKS))]


IN_HBM = pl.BlockSpec(memory_space=pltpu.HBM)
IN_SMEM = pl.BlockSpec(memory_space=pltpu.SMEM)
IN_VMEM = pl.BlockSpec(memory_space=pltpu.VMEM)
PARAMS = pltpu.CompilerParams(vmem_limit_bytes=16 * 2**20)
WHOLE = pltpu.CompilerParams(vmem_limit_bytes=60 * 2**20)


def partial_values(side, tokens, w_gate, w_up, dtype):
    token_count, feature_count = tokens.shape
    half = w_gate.shape[1] // 2
    return pl.pallas_call(
        values_kernel,
        out_shape=jax.ShapeDtypeStruct((token_count, 2 * half), dtype),
        in_specs=[IN_SMEM, IN_VMEM, IN_HBM, IN_HBM],
        out_specs=IN_VMEM,
        scratch_shapes=half_scratch(w_gate),
        compiler_params=WHOLE,
        cost_estimate=pl.CostEstimate(
            flops=4 * token_count * feature_count * half,
            bytes_accessed=4 * feature_count * half + 8 * token_count * half,
            transcendentals=0,
        ),
    )(side, tokens, w_gate, w_up)


def grads_kernel(terms_ref, cotangent_ref, pair_ref):
    half = cotangent_ref.shape[1]
    values = terms_ref[0].astype(F32)
    for k in range(1, terms_ref.shape[0]):
        values = values + terms_ref[k].astype(F32)
    gate_value = values[:, :half]
    up_value = values[:, half:]
    cotangent = cotangent_ref[...].astype(F32)
    sigmoid_gate = jax.nn.sigmoid(gate_value)
    grad_gate = cotangent * up_value * sigmoid_gate * (1.0 + gate_value * (1.0 - sigmoid_gate))
    grad_upper = cotangent * gate_value * sigmoid_gate
    pair_ref[:, :half] = grad_gate.astype(BF16)
    pair_ref[:, half:] = grad_upper.astype(BF16)


def grad_pair(terms, cotangent):
    rows, half = cotangent.shape
    return pl.pallas_call(
        grads_kernel,
        out_shape=jax.ShapeDtypeStruct((rows, 2 * half), BF16),
        compiler_params=PARAMS,
        cost_estimate=pl.CostEstimate(
            flops=40 * rows * half,
            bytes_accessed=2 * terms.size + 8 * rows * half,
            transcendentals=rows * half,
        ),
    )(terms, cotangent)


def pieces_kernel(starts, pair_ref, pieces_ref):
    half = pair_ref.shape[1] // 2
    width = pieces_ref.shape[2]
    for u in range(2):
        for b, start in enumerate(starts):
            first = u * half + start
            pieces_ref[u * len(starts) + b] = pair_ref[:, first : first + width]


def dep_pieces(pair, starts, width):
    shape = (2 * len(starts), pair.shape[0], width)
    return pl.pallas_call(
        functools.partial(pieces_kernel, starts),
        out_shape=jax.ShapeDtypeStruct(shape, BF16),
        compiler_params=PARAMS,
        cost_estimate=pl.CostEstimate(
            flops=0, bytes_accessed=4 * math.prod(shape), transcendentals=0
        ),
    )(pair)


def input_kernel(side_ref, gate_hbm, up_hbm, pair_ref, *rest):
    *totals, out_ref, gate_ref, up_ref, sems = rest
    copies = fetch_half(side_ref[0], (gate_hbm, up_hbm), (gate_ref, up_ref), sems)
    half = gate_ref.shape[1]
    total = totals[0][...] if totals else None
    for u, w_ref in enumerate((gate_ref, up_ref)):
        for copy in copies[u * CHUNKS : (u + 1) * CHUNKS]:
            copy.wait()
        term = lax.dot_general(
            w_ref[...],
            pair_ref[:, u * half : (u + 1) * half],
            COLS_BY_COLS,
            preferred_element_type=F32,
        )
        total = term if total is None else total + term
    out_ref[...] = total.astype(out_ref.dtype)


def input_terms(side, w_gate, w_up, pair, dtype, *total):
    feature_count = w_gate.shape[0]
    half = w_gate.shape[1] // 2
    token_count = pair.shape[0]
    return pl.pallas_call(
        input_kernel,
        out_shape=jax.ShapeDtypeStruct((feature_count, token_count), dtype),
        in_specs=[IN_SMEM, IN_HBM, IN_HBM, IN_VMEM] + [IN_VMEM] * len(total),
        out_specs=IN_VMEM,
        scratch_shapes=half_scratch(w_gate),
        compiler_params=WHOLE,
        cost_estimate=pl.CostEstimate(
            flops=4 * token_count * feature_count * half,
            bytes_accessed=4 * feature_count * half + 8 * token_count * half,
            transcendentals=0,
        ),
    )(side, w_gate, w_up, pair, *total)


def weight_kernel(factor, tokens_ref, own_ref, other_ref, out_ref):
    width = own_ref.shape[1]
    for side, block_ref in enumerate((own_ref, other_ref)):
        total = lax.dot_general(
            tokens_ref[...], block_ref[...], ROWS_BY_COLS, preferred_element_type=F32
        )
        out_ref[:, side * width : (side + 1) * width] = (total * factor).astype(BF16)


def weight_terms(tokens, own, other, factor):
    feature_count, token_count = tokens.shape
    width = own.shape[1]
    return pl.pallas_call(
        functools.partial(weight_kernel, factor),
        out_shape=jax.ShapeDtypeStruct((feature_count, 2 * width), BF16),
        compiler_params=PARAMS,
        cost_estimate=pl.CostEstimate(
            flops=4 * token_count * feature_count * width,
            bytes_accessed=2 * token_count * (feature_count + 2 * width),
            transcendentals=0,
        ),
    )(tokens, own, other)


def finish_kernel(skips, side_ref, swapped_ref, gate_ref, up_ref):
    width = swapped_ref.shape[2] // 2
    half = gate_ref.shape[1] // 2
    blocks = len(skips)
    for u, out_ref in enumerate((gate_ref, up_ref)):
        for s in range(2):
            first = (side_ref[0] if s == 0 else 1 - side_ref[0]) * half
            for b, skip in enumerate(skips):
                at = pl.multiple_of(first + b * width, LANES)
                out_ref[:, pl.ds(at, width - skip)] = swapped_ref[u * blocks + b][
                    :, s * width + skip : (s + 1) * width
                ]


def finished(side, swapped, half, skips):
    shape = jax.ShapeDtypeStruct((swapped.shape[1], 2 * half), BF16)
    return pl.pallas_call(
        functools.partial(finish_kernel, skips),
        out_shape=(shape, shape),
        in_specs=[IN_SMEM, IN_VMEM],
        out_specs=(IN_VMEM, IN_VMEM),
        compiler_params=PARAMS,
        cost_estimate=pl.CostEstimate(
            flops=0, bytes_accessed=4 * swapped.size, transcendentals=0
        ),
    )(side, swapped)


def shards(tokens, grad_hidden, w_gate, w_up):
    token_count, feature_count = tokens.shape
    hidden = w_gate.shape[1]
    inp, out, dep = (lax.axis_size(name) for name in ("inp", "out", "dep"))
    factor = 1.0 / math.sqrt(token_count * dep)
    half = hidden // 2
    group = inp // 2
    rows = token_count // group
    pairs = [(i, i ^ 1) for i in range(inp)]
    alike = [[p + 2 * i for i in range(group)] for p in range(2)]
    place = lax.axis_index("inp")
    parity = place % 2
    own_side = parity.reshape(1)
    other_side = 1 - own_side

    given = partial_values(other_side, tokens, w_gate, w_up, BF16)
    kept = partial_values(own_side, tokens, w_gate, w_up, F32)
    kept = (kept + lax.ppermute(given, "inp", pairs).astype(F32)).astype(BF16)

    all_tokens = lax.all_gather(tokens, "dep", axis=0, tiled=True)

    terms = lax.all_to_all(
        kept.reshape(group, rows, hidden), "inp", 0, 0, axis_index_groups=alike
    )
    cotangent = lax.dynamic_slice(
        grad_hidden, ((place // 2) * rows, parity * half), (rows, half)
    )
    own = lax.all_gather(
        grad_pair(terms, cotangent), "inp", axis=0, tiled=True, axis_index_groups=alike
    )
    other = lax.ppermute(own, "inp", pairs)

    width = 2 * LANES
    blocks = dep // 2
    starts = [min(b * width, half - width) for b in range(blocks)]
    skips = [b * width - s for b, s in enumerate(starts)]
    own_block = lax.all_to_all(dep_pieces(own, starts, width), "dep", 0, 0)
    own_block = own_block.reshape(dep * token_count, width)
    shares = input_terms(own_side, w_gate, w_up, own, F32)
    own_block, across, shares = lax.optimization_barrier((own_block, all_tokens.T, shares))
    other_block = lax.ppermute(own_block, "inp", pairs)

    shares = input_terms(other_side, w_gate, w_up, other, BF16, shares)
    shares = lax.all_to_all(
        shares.reshape(out, feature_count // out, token_count), "out", 0, 0
    )
    grad_input = jnp.sum(shares.astype(F32), axis=0).astype(BF16).T

    grad = weight_terms(across, own_block, other_block, factor)
    swapped = lax.all_to_all(grad.reshape(dep, feature_count // dep, 2 * width), "dep", 0, 0)
    gate_grad, up_grad = finished(own_side, swapped, half, skips)
    return grad_input, gate_grad, up_grad


def solution(mesh):
    return jax.shard_map(
        shards,
        mesh=mesh,
        in_specs=(P("dep", "inp"), P("dep", "out"), P("inp", "out"), P("inp", "out")),
        out_specs=(P("dep", ("inp", "out")), P(("inp", "dep"), "out"), P(("inp", "dep"), "out")),
        check_vma=False,
    )
```

time: 200 us -> 191 us (0.955)
  the two profiles are of different devices: /device:TPU:10 before, /device:TPU:64 now
where the time goes in v4:
time: 191 us
  waiting for transfers between devices  70.7 us (37%)
  starting transfers between devices  48.1 us (25%)
  blocking collectives  30.8 us (16%)
  Pallas kernels  21.2 us (11%)
  between operations  14.2 us (7%)
  other arithmetic  2.97 us (2%)
  local copies, waits for them, and re-layouts  2.51 us (1%)
    all_to_all x1, waiting for transfers between devices, shards(): lax.all_to_all(kept.reshape(group, rows, hidden), 'inp', 0, 0, axis_index...  35.9 us
    all_gather x1, blocking collectives, shards(): lax.all_gather(grad_pair(terms, cotangent), 'inp', axis=0, tiled=True, ax...  30.8 us
    ppermute x1, starting transfers between devices, shards(): kept = (kept + lax.ppermute(given, 'inp', pairs).astype(F32)).astype(BF16)  14.2 us
    all_to_all x1, starting transfers between devices, shards(): lax.all_to_all(kept.reshape(group, rows, hidden), 'inp', 0, 0, axis_index...  13.8 us
    all_to_all x1, waiting for transfers between devices, shards(): lax.all_to_all(shares.reshape(out, feature_count // out, token_count), 'o...  9.82 us
    all_to_all x1, waiting for transfers between devices, shards(): lax.all_to_all(grad.reshape(dep, feature_count // dep, 2 * width), 'dep',...  8.92 us
    pallas_call x2, Pallas kernels, input_terms(): pl.pallas_call(input_kernel, out_shape=jax.ShapeDtypeStruct((feature_coun...  8.66 us
    ppermute x1, waiting for transfers between devices, shards(): other = lax.ppermute(own, 'inp', pairs)  8.56 us
  transfers between devices with their start and end apart: 8, of which 6 were waited for; matrix products, arithmetic and copies ran while one was open for 2% of the time, Pallas kernels for 9%

profile of v4, /device:TPU:64, one launch (start us, length us, event | category | flops | bytes accessed | tf_op | source)
XLA Modules:
  0.0 190.5 jit_solution(1275577796793210996)
XLA Ops:
  7.2 3.7 %shard_map.68 = bf16[192,1792]{1,0:T(8,128)(2,1)} custom-call(s32[1]{0:T(128)S(6)} %sub.7.side_ref, bf16[192,512]{1,0:T(8,128)(2,1)} %tokens_ref.3, bf16[512,1792]{1,0:T(8,128)(2,1)} %gate_hbm.7, bf16[512,1792]{1,0:T(8,128)(2,1)} %up_hbm.7), custom_call_target="tpu_custom_call" | custom-call | flops 352321536 | bytes 3211264 | tf_op jit(solution)/shard_map/pallas_call | solution.py:63
  10.9 14.2 %collective-permute-start = (bf16[192,1792]{1,0:T(8,128)(2,1)}, bf16[192,1792]{1,0:T(8,128)(2,1)S(1)}, u32[]{:S(2)}, u32[]{:S(2)}) collective-permute-start(bf16[192,1792]{1,0:T(8,128)(2,1)} %shard_map.68), channel_id=1, source_target_pairs={{0,64},{64,0},{128,192},{192,128},{256,320},{320,256},{384,448},{4... | collective-permute-start | bytes 2064392 | tf_op jit(solution)/shard_map/ppermute | solution.py:234
  25.1 4.0 %shard_map.67 = f32[192,1792]{1,0:T(8,128)} custom-call(s32[1]{0:T(128)} %bitcast.side_ref, bf16[192,512]{1,0:T(8,128)(2,1)} %tokens_ref.3, bf16[512,1792]{1,0:T(8,128)(2,1)} %gate_hbm.7, bf16[512,1792]{1,0:T(8,128)(2,1)} %up_hbm.7), custom_call_target="tpu_custom_call" | custom-call | flops 352321536 | bytes 3211264 | tf_op jit(solution)/shard_map/pallas_call | solution.py:63
  29.1 5.1 %collective-permute-done = bf16[192,1792]{1,0:T(8,128)(2,1)S(1)} collective-permute-done((bf16[192,1792]{1,0:T(8,128)(2,1)}, bf16[192,1792]{1,0:T(8,128)(2,1)S(1)}, u32[]{:S(2)}, u32[]{:S(2)}) %collective-permute-start) | collective-permute-done | bytes 688160 | tf_op jit(solution)/shard_map/ppermute | solution.py:234
  34.3 2.3 %add_convert_fusion = bf16[192,1792]{1,0:T(8,128)(2,1)} fusion(f32[192,1792]{1,0:T(8,128)} %shard_map.67, bf16[192,1792]{1,0:T(8,128)(2,1)S(1)} %collective-permute-done), kind=kLoop, calls=%fused_computation | loop fusion | flops 1032192 | bytes 2752512 | tf_op jit(solution)/shard_map/convert_element_type | solution.py:234
  36.6 13.8 %all-to-all-start = ((bf16[8,24,1792]{2,1,0:T(8,128)(2,1)}), bf16[8,24,1792]{2,1,0:T(8,128)(2,1)S(1)}, u32[]{:S(2)}, u32[]{:S(2)}) async-start(bf16[8,24,1792]{2,1,0:T(8,128)(2,1)} %bitcast.1), calls=%async_computation | async-start | bytes 1376256 | tf_op jit(solution)/shard_map/all_to_all | solution.py:238
  50.4 0.0 all-gather.2.cloned.1.call-start
  50.4 0.7 all-gather.2.cloned.1.call-update
  51.1 0.8 dynamic_slice.3.cotangent_ref
  51.9 35.9 %all-to-all-done.terms_ref = bf16[8,24,1792]{2,1,0:T(8,128)(2,1)S(1)} async-done(((bf16[8,24,1792]{2,1,0:T(8,128)(2,1)}), bf16[8,24,1792]{2,1,0:T(8,128)(2,1)S(1)}, u32[]{:S(2)}, u32[]{:S(2)}) %all-to-all-start) | async-done | bytes 688160 | tf_op jit(solution)/shard_map/all_to_all | solution.py:238
  87.8 0.1 shard_map.69
  88.0 30.8 %all_gather.6.pair_ref = bf16[192,1792]{1,0:T(8,128)(2,1)S(1)} all-gather(bf16[24,1792]{1,0:T(8,128)(2,1)S(1)} %shard_map.69), channel_id=1, replica_groups={{0,128,256,384,512,640,768,896},{64,192,320,448,576,704,832,960},{1,129..., dimensions={0}, use_global_device_ids=true | all-gather | bytes 774144 | tf_op jit(solution)/shard_map/all_gather | solution.py:244
  118.8 0.0 copy-start
  118.8 1.0 shard_map.70
  119.7 5.7 %all-to-all-start.1 = ((bf16[8,192,256]{2,1,0:T(8,128)(2,1)}), bf16[8,192,256]{2,1,0:T(8,128)(2,1)S(1)}, u32[]{:S(2)}, u32[]{:S(2)}) async-start(bf16[8,192,256]{2,1,0:T(8,128)(2,1)} %shard_map.70), calls=%async_computation.1 | async-start | bytes 1572864 | tf_op jit(solution)/shard_map/all_to_all | solution.py:253
  125.5 1.9 %collective-permute-start.1 = (bf16[192,1792]{1,0:T(8,128)(2,1)S(1)}, bf16[192,1792]{1,0:T(8,128)(2,1)}, u32[]{:S(2)}, u32[]{:S(2)}) collective-permute-start(bf16[192,1792]{1,0:T(8,128)(2,1)S(1)} %all_gather.6.pair_ref), channel_id=1, source_target_pairs={{0,64},{64,0},{128,192},{192,128},{256,320},{320,256},{384,448},{4... | collective-permute-start | bytes 2064392 | tf_op jit(solution)/shard_map/ppermute | solution.py:247
  127.4 0.0 all-gather.2.cloned.1.call-done
  127.4 1.7 copy.8
  129.1 0.0 copy-done
  129.1 4.1 %shard_map.71.rest_0_ = f32[512,192]{1,0:T(8,128)} custom-call(s32[1]{0:T(128)} %bitcast.side_ref, bf16[512,1792]{1,0:T(8,128)(2,1)} %gate_hbm.7, bf16[512,1792]{1,0:T(8,128)(2,1)} %up_hbm.7, bf16[192,1792]{1,0:T(8,128)(2,1)} %copy-done), custom_call_target="tpu_custom_call" | custom-call | flops 352321536 | bytes 3211264 | tf_op jit(solution)/shard_map/pallas_call | solution.py:150
  133.3 1.7 all-to-all-done.1
  134.9 2.2 %collective-permute-start.2 = (bf16[1536,256]{1,0:T(8,128)(2,1)S(1)}, bf16[1536,256]{1,0:T(8,128)(2,1)}, u32[]{:S(2)}, u32[]{:S(2)}) collective-permute-start(bf16[1536,256]{1,0:T(8,128)(2,1)S(1)} %bitcast.8), channel_id=1, source_target_pairs={{0,64},{64,0},{128,192},{192,128},{256,320},{320,256},{384,448},{4... | collective-permute-start | bytes 2359304 | tf_op jit(solution)/shard_map/ppermute | solution.py:257
  137.2 8.6 %collective-permute-done.1.pair_ref = bf16[192,1792]{1,0:T(8,128)(2,1)} collective-permute-done((bf16[192,1792]{1,0:T(8,128)(2,1)S(1)}, bf16[192,1792]{1,0:T(8,128)(2,1)}, u32[]{:S(2)}, u32[]{:S(2)}) %collective-permute-start.1) | collective-permute-done | bytes 688160 | tf_op jit(solution)/shard_map/ppermute | solution.py:247
  145.8 4.6 %shard_map.72 = bf16[512,192]{1,0:T(8,128)(2,1)} custom-call(s32[1]{0:T(128)S(6)} %sub.7.side_ref, bf16[512,1792]{1,0:T(8,128)(2,1)} %gate_hbm.7, bf16[512,1792]{1,0:T(8,128)(2,1)} %up_hbm.7, bf16[192,1792]{1,0:T(8,128)(2,1)} %collective-permute-done.1.pair_ref, f32[512,192]{1,0:T(8,128)} %shard_map.71.rest_0_), custom_call_target="tpu_custom_call" | custom-call | flops 352321536 | bytes 3211264 | tf_op jit(solution)/shard_map/pallas_call | solution.py:150
  150.3 5.5 %all-to-all-start.2 = ((bf16[8,64,192]{2,1,0:T(8,128)(2,1)}), bf16[8,64,192]{2,1,0:T(8,128)(2,1)S(1)}, u32[]{:S(2)}, u32[]{:S(2)}) async-start(bf16[8,64,192]{2,1,0:T(8,128)(2,1)} %bitcast.10), calls=%async_computation.2 | async-start | bytes 524288 | tf_op jit(solution)/shard_map/all_to_all | solution.py:260
  155.8 0.0 collective-permute-done.2.other_ref
  155.8 2.9 %shard_map.73 = bf16[512,512]{1,0:T(8,128)(2,1)} custom-call(bf16[512,1536]{1,0:T(8,128)(2,1)S(1)} %bitcast.7, bf16[1536,256]{1,0:T(8,128)(2,1)S(1)} %bitcast.9, bf16[1536,256]{1,0:T(8,128)(2,1)} %collective-permute-done.2.other_ref), custom_call_target="tpu_custom_call" | custom-call | flops 805306368 | bytes 3145728 | tf_op jit(solution)/shard_map/pallas_call | solution.py:177
  158.8 9.8 %all-to-all-done.2 = bf16[8,64,192]{2,1,0:T(8,128)(2,1)S(1)} async-done(((bf16[8,64,192]{2,1,0:T(8,128)(2,1)}), bf16[8,64,192]{2,1,0:T(8,128)(2,1)S(1)}, u32[]{:S(2)}, u32[]{:S(2)}) %all-to-all-start.2) | async-done | bytes 196640 | tf_op jit(solution)/shard_map/all_to_all | solution.py:260
  168.6 4.7 %all-to-all-start.3 = ((bf16[8,64,512]{2,1,0:T(8,128)(2,1)}), bf16[8,64,512]{2,1,0:T(8,128)(2,1)S(1)}, u32[]{:S(2)}, u32[]{:S(2)}) async-start(bf16[8,64,512]{2,1,0:T(8,128)(2,1)} %bitcast.6), calls=%async_computation.3 | async-start | bytes 1048576 | tf_op jit(solution)/shard_map/all_to_all | solution.py:266
  173.3 0.7 reduce_sum.12
  174.0 8.9 %all-to-all-done.3.swapped_ref = bf16[8,64,512]{2,1,0:T(8,128)(2,1)S(1)} async-done(((bf16[8,64,512]{2,1,0:T(8,128)(2,1)}), bf16[8,64,512]{2,1,0:T(8,128)(2,1)S(1)}, u32[]{:S(2)}, u32[]{:S(2)}) %all-to-all-start.3) | async-done | bytes 524320 | tf_op jit(solution)/shard_map/all_to_all | solution.py:266
  182.9 0.8 shard_map.74
Async XLA Ops:
  10.9 23.3 %collective-permute-start = (bf16[192,1792]{1,0:T(8,128)(2,1)}, bf16[192,1792]{1,0:T(8,128)(2,1)S(1)}, u32[]{:S(2)}, u32[]{:S(2)}) collective-permute-start(bf16[192,1792]{1,0:T(8,128)(2,1)} %shard_map.68), channel_id=1, source_target_pairs={{0,64},{64,0},{128,192},{192,128},{256,320},{320,256},{384,448},{4... | collective-permute-start | bytes 2064392 | tf_op jit(solution)/shard_map/ppermute | solution.py:234
  36.6 51.3 %all-to-all-start = ((bf16[8,24,1792]{2,1,0:T(8,128)(2,1)}), bf16[8,24,1792]{2,1,0:T(8,128)(2,1)S(1)}, u32[]{:S(2)}, u32[]{:S(2)}) async-start(bf16[8,24,1792]{2,1,0:T(8,128)(2,1)} %bitcast.1), calls=%async_computation | async-start | bytes 1376256 | tf_op jit(solution)/shard_map/all_to_all | solution.py:238
  50.4 77.0 %all-gather.2.cloned.1.call-start = ((), (), s32[]{:S(2)}) async-start(), calls=%async_computation.4 | async-start | bytes 1769472 | tf_op jit(solution)/shard_map/all_gather | solution.py:236
  118.8 10.4 %copy-start = (bf16[192,1792]{1,0:T(8,128)(2,1)}, bf16[192,1792]{1,0:T(8,128)(2,1)S(1)}, u32[]{:S(2)}) copy-start(bf16[192,1792]{1,0:T(8,128)(2,1)S(1)} %all_gather.6.pair_ref) | copy-start | bytes 2064388
  119.7 15.2 %all-to-all-start.1 = ((bf16[8,192,256]{2,1,0:T(8,128)(2,1)}), bf16[8,192,256]{2,1,0:T(8,128)(2,1)S(1)}, u32[]{:S(2)}, u32[]{:S(2)}) async-start(bf16[8,192,256]{2,1,0:T(8,128)(2,1)} %shard_map.70), calls=%async_computation.1 | async-start | bytes 1572864 | tf_op jit(solution)/shard_map/all_to_all | solution.py:253
  125.5 20.3 %collective-permute-start.1 = (bf16[192,1792]{1,0:T(8,128)(2,1)S(1)}, bf16[192,1792]{1,0:T(8,128)(2,1)}, u32[]{:S(2)}, u32[]{:S(2)}) collective-permute-start(bf16[192,1792]{1,0:T(8,128)(2,1)S(1)} %all_gather.6.pair_ref), channel_id=1, source_target_pairs={{0,64},{64,0},{128,192},{192,128},{256,320},{320,256},{384,448},{4... | collective-permute-start | bytes 2064392 | tf_op jit(solution)/shard_map/ppermute | solution.py:247
  134.9 20.9 %collective-permute-start.2 = (bf16[1536,256]{1,0:T(8,128)(2,1)S(1)}, bf16[1536,256]{1,0:T(8,128)(2,1)}, u32[]{:S(2)}, u32[]{:S(2)}) collective-permute-start(bf16[1536,256]{1,0:T(8,128)(2,1)S(1)} %bitcast.8), channel_id=1, source_target_pairs={{0,64},{64,0},{128,192},{192,128},{256,320},{320,256},{384,448},{4... | collective-permute-start | bytes 2359304 | tf_op jit(solution)/shard_map/ppermute | solution.py:257
  150.3 18.2 %all-to-all-start.2 = ((bf16[8,64,192]{2,1,0:T(8,128)(2,1)}), bf16[8,64,192]{2,1,0:T(8,128)(2,1)S(1)}, u32[]{:S(2)}, u32[]{:S(2)}) async-start(bf16[8,64,192]{2,1,0:T(8,128)(2,1)} %bitcast.10), calls=%async_computation.2 | async-start | bytes 524288 | tf_op jit(solution)/shard_map/all_to_all | solution.py:260
  168.6 14.3 %all-to-all-start.3 = ((bf16[8,64,512]{2,1,0:T(8,128)(2,1)}), bf16[8,64,512]{2,1,0:T(8,128)(2,1)S(1)}, u32[]{:S(2)}, u32[]{:S(2)}) async-start(bf16[8,64,512]{2,1,0:T(8,128)(2,1)} %bitcast.6), calls=%async_computation.3 | async-start | bytes 1048576 | tf_op jit(solution)/shard_map/all_to_all | solution.py:266
Sparse Core Ops, SparseCore 0:
  53.9 52.3 all-gather.1

commit v5 on v4

v5 whole, which is shorter than its diff:
```python
import functools
import math

import jax
import jax.numpy as jnp
from jax import lax
from jax.experimental import pallas as pl
from jax.experimental.pallas import tpu as pltpu
from jax.sharding import PartitionSpec as P

BF16 = jnp.bfloat16
F32 = jnp.float32
LANES = 128
ROWS_BY_COLS = (((1,), (0,)), ((), ()))
COLS_BY_COLS = (((1,), (1,)), ((), ()))


def values_kernel(
    side_ref, tokens_hbm, gate_hbm, up_hbm, out_hbm, tokens_ref, gate_ref, up_ref, out_ref, sems
):
    half = gate_ref.shape[1]
    columns = pl.ds(pl.multiple_of(side_ref[0] * half, LANES), half)
    fetches = [
        pltpu.make_async_copy(tokens_hbm, tokens_ref, sems.at[0]),
        pltpu.make_async_copy(gate_hbm.at[:, columns], gate_ref, sems.at[1]),
        pltpu.make_async_copy(up_hbm.at[:, columns], up_ref, sems.at[2]),
    ]
    for fetch in fetches:
        fetch.start()
    fetches[0].wait()
    stores = []
    for u, w_ref in enumerate((gate_ref, up_ref)):
        fetches[1 + u].wait()
        part = lax.dot_general(
            tokens_ref[...], w_ref[...], ROWS_BY_COLS, preferred_element_type=F32
        )
        out_ref[u] = part.astype(out_ref.dtype)
        store = pltpu.make_async_copy(
            out_ref.at[u], out_hbm.at[:, pl.ds(u * half, half)], sems.at[3 + u]
        )
        store.start()
        stores.append(store)
    for store in stores:
        store.wait()


IN_HBM = pl.BlockSpec(memory_space=pltpu.HBM)
IN_SMEM = pl.BlockSpec(memory_space=pltpu.SMEM)
IN_VMEM = pl.BlockSpec(memory_space=pltpu.VMEM)
PARAMS = pltpu.CompilerParams(vmem_limit_bytes=16 * 2**20)
WHOLE = pltpu.CompilerParams(vmem_limit_bytes=60 * 2**20)


def partial_values(side, tokens, w_gate, w_up):
    token_count, feature_count = tokens.shape
    half = w_gate.shape[1] // 2
    return pl.pallas_call(
        values_kernel,
        out_shape=jax.ShapeDtypeStruct((token_count, 2 * half), BF16),
        in_specs=[IN_SMEM, IN_HBM, IN_HBM, IN_HBM],
        out_specs=IN_HBM,
        scratch_shapes=[
            pltpu.VMEM((token_count, feature_count), BF16),
            pltpu.VMEM((feature_count, half), BF16),
            pltpu.VMEM((feature_count, half), BF16),
            pltpu.VMEM((2, token_count, half), BF16),
            pltpu.SemaphoreType.DMA((5,)),
        ],
        compiler_params=WHOLE,
        cost_estimate=pl.CostEstimate(
            flops=4 * token_count * feature_count * half,
            bytes_accessed=4 * feature_count * half + 4 * token_count * half,
            transcendentals=0,
        ),
    )(side, tokens, w_gate, w_up)


def grads_kernel(terms_ref, cotangent_ref, pair_ref):
    half = cotangent_ref.shape[1]
    values = terms_ref[0].astype(F32)
    for k in range(1, terms_ref.shape[0]):
        values = values + terms_ref[k].astype(F32)
    gate_value = values[:, :half]
    up_value = values[:, half:]
    cotangent = cotangent_ref[...].astype(F32)
    sigmoid_gate = jax.nn.sigmoid(gate_value)
    grad_gate = cotangent * up_value * sigmoid_gate * (1.0 + gate_value * (1.0 - sigmoid_gate))
    grad_upper = cotangent * gate_value * sigmoid_gate
    pair_ref[:, :half] = grad_gate.astype(BF16)
    pair_ref[:, half:] = grad_upper.astype(BF16)


def grad_pair(terms, cotangent):
    rows, half = cotangent.shape
    return pl.pallas_call(
        grads_kernel,
        out_shape=jax.ShapeDtypeStruct((rows, 2 * half), BF16),
        compiler_params=PARAMS,
        cost_estimate=pl.CostEstimate(
            flops=40 * rows * half,
            bytes_accessed=2 * terms.size + 8 * rows * half,
            transcendentals=rows * half,
        ),
    )(terms, cotangent)


def pieces_kernel(starts, pair_ref, pieces_ref):
    half = pair_ref.shape[1] // 2
    width = pieces_ref.shape[2]
    for u in range(2):
        for b, start in enumerate(starts):
            first = u * half + start
            pieces_ref[u * len(starts) + b] = pair_ref[:, first : first + width]


def dep_pieces(pair, starts, width):
    shape = (2 * len(starts), pair.shape[0], width)
    return pl.pallas_call(
        functools.partial(pieces_kernel, starts),
        out_shape=jax.ShapeDtypeStruct(shape, BF16),
        compiler_params=PARAMS,
        cost_estimate=pl.CostEstimate(
            flops=0, bytes_accessed=4 * math.prod(shape), transcendentals=0
        ),
    )(pair)


def own_input_kernel(gate_ref, up_ref, pair_ref, out_ref):
    half = gate_ref.shape[1]
    out_ref[...] = sum(
        lax.dot_general(
            w_ref[...],
            pair_ref[:, u * half : (u + 1) * half],
            COLS_BY_COLS,
            preferred_element_type=F32,
        )
        for u, w_ref in enumerate((gate_ref, up_ref))
    )


def other_input_kernel(core_ref, gate_ref, up_ref, pair_ref, own_ref, kept_ref, given_ref, total):
    own_input_kernel(gate_ref, up_ref, pair_ref, total)
    blocks, rows, _ = kept_ref.shape
    core = core_ref[0]
    for y in range(blocks):
        for which, ref in ((core, kept_ref), (1 - core, given_ref)):
            at = pl.ds(pl.multiple_of((2 * y + which) * rows, rows), rows)
            ref[y] = (total[at, :] + own_ref[at, :]).astype(ref.dtype)


def product_cost(pair, feature_count):
    return pl.CostEstimate(
        flops=2 * pair.size * feature_count,
        bytes_accessed=2 * pair.shape[1] * feature_count + 8 * pair.shape[0] * feature_count,
        transcendentals=0,
    )


def own_input_terms(gate, up, pair):
    return pl.pallas_call(
        own_input_kernel,
        out_shape=jax.ShapeDtypeStruct((gate.shape[0], pair.shape[0]), F32),
        compiler_params=PARAMS,
        cost_estimate=product_cost(pair, gate.shape[0]),
    )(gate, up, pair)


def other_input_terms(core, gate, up, pair, own, out):
    feature_count, token_count = own.shape
    shape = (out // 2, feature_count // out, token_count)
    return pl.pallas_call(
        other_input_kernel,
        out_shape=(jax.ShapeDtypeStruct(shape, F32), jax.ShapeDtypeStruct(shape, BF16)),
        in_specs=[IN_SMEM] + [IN_VMEM] * 4,
        out_specs=(IN_VMEM, IN_VMEM),
        scratch_shapes=[pltpu.VMEM((feature_count, token_count), F32)],
        compiler_params=PARAMS,
        cost_estimate=product_cost(pair, feature_count),
    )(core, gate, up, pair, own)


def split_kernel(index_ref, kept_ref, received_ref, mine_ref, *sent_refs):
    for k, ref in enumerate((mine_ref, *sent_refs)):
        at = index_ref[0] ^ k
        ref[...] = (kept_ref[at] + received_ref[at].astype(F32)).astype(ref.dtype)


def split_shares(index, kept, received):
    shape = kept.shape[1:]
    others = kept.shape[0] - 1
    return pl.pallas_call(
        split_kernel,
        out_shape=[jax.ShapeDtypeStruct(shape, F32)] + [jax.ShapeDtypeStruct(shape, BF16)] * others,
        in_specs=[IN_SMEM, IN_VMEM, IN_VMEM],
        out_specs=[IN_VMEM] * (others + 1),
        compiler_params=PARAMS,
        cost_estimate=pl.CostEstimate(
            flops=2 * kept.size, bytes_accessed=10 * kept.size, transcendentals=0
        ),
    )(index, kept, received)


def weight_kernel(which, factor, tokens_ref, block_ref, out_ref):
    rows = out_ref.shape[0]
    total = lax.dot_general(
        tokens_ref[which * rows : (which + 1) * rows, :],
        block_ref[...],
        ROWS_BY_COLS,
        preferred_element_type=F32,
    )
    out_ref[...] = (total * factor).astype(BF16)


def weight_terms(tokens, which, block, factor):
    feature_count = tokens.shape[0] // 2
    token_count, width = block.shape
    return pl.pallas_call(
        functools.partial(weight_kernel, which, factor),
        out_shape=jax.ShapeDtypeStruct((feature_count, width), BF16),
        compiler_params=PARAMS,
        cost_estimate=pl.CostEstimate(
            flops=2 * token_count * feature_count * width,
            bytes_accessed=2 * token_count * (feature_count + width),
            transcendentals=0,
        ),
    )(tokens, block)


def finish_kernel(skips, side_ref, swapped_ref, gate_ref, up_ref):
    width = swapped_ref.shape[2] // 2
    half = gate_ref.shape[1] // 2
    blocks = len(skips)
    for u, out_ref in enumerate((gate_ref, up_ref)):
        for s in range(2):
            first = (side_ref[0] if s == 0 else 1 - side_ref[0]) * half
            for b, skip in enumerate(skips):
                at = pl.multiple_of(first + b * width, LANES)
                out_ref[:, pl.ds(at, width - skip)] = swapped_ref[u * blocks + b][
                    :, s * width + skip : (s + 1) * width
                ]


def finished(side, swapped, half, skips):
    shape = jax.ShapeDtypeStruct((swapped.shape[1], 2 * half), BF16)
    return pl.pallas_call(
        functools.partial(finish_kernel, skips),
        out_shape=(shape, shape),
        in_specs=[IN_SMEM, IN_VMEM],
        out_specs=(IN_VMEM, IN_VMEM),
        compiler_params=PARAMS,
        cost_estimate=pl.CostEstimate(
            flops=0, bytes_accessed=4 * swapped.size, transcendentals=0
        ),
    )(side, swapped)


def shards(tokens, grad_hidden, w_gate, w_up):
    token_count, feature_count = tokens.shape
    hidden = w_gate.shape[1]
    inp, out, dep = (lax.axis_size(name) for name in ("inp", "out", "dep"))
    factor = 1.0 / math.sqrt(token_count * dep)
    half = hidden // 2
    group = inp // 2
    rows = token_count // group
    pairs = [(i, i ^ 1) for i in range(inp)]
    alike = [[p + 2 * i for i in range(group)] for p in range(2)]
    place = lax.axis_index("inp")
    parity = place % 2
    own_side = parity.reshape(1)
    other_side = 1 - own_side

    theirs = lax.ppermute(tokens, "inp", pairs)
    given = partial_values(other_side, tokens, w_gate, w_up)
    kept = partial_values(own_side, tokens, w_gate, w_up)
    theirs, kept = lax.optimization_barrier((theirs, kept))
    two = jnp.concatenate([tokens, theirs], axis=1)
    all_tokens = lax.all_gather(two, "dep", axis=0, tiled=True)
    kept = kept.astype(F32) + lax.ppermute(given, "inp", pairs).astype(F32)
    kept, w_gate, w_up = lax.optimization_barrier((kept.astype(BF16), w_gate, w_up))
    terms = lax.all_to_all(
        kept.reshape(group, rows, hidden), "inp", 0, 0, axis_index_groups=alike
    )
    cotangent = lax.dynamic_slice(
        grad_hidden, ((place // 2) * rows, parity * half), (rows, half)
    )
    own_weights, other_weights = (
        [lax.dynamic_slice(w, (0, side * half), (feature_count, half)) for w in (w_gate, w_up)]
        for side in (parity, 1 - parity)
    )
    terms, own_weights, other_weights = lax.optimization_barrier(
        (terms, own_weights, other_weights)
    )
    own = lax.all_gather(
        grad_pair(terms, cotangent), "inp", axis=0, tiled=True, axis_index_groups=alike
    )
    other = lax.ppermute(own, "inp", pairs)

    width = 2 * LANES
    blocks = dep // 2
    starts = [min(b * width, half - width) for b in range(blocks)]
    skips = [b * width - s for b, s in enumerate(starts)]
    own_block = lax.all_to_all(dep_pieces(own, starts, width), "dep", 0, 0)
    own_block = own_block.reshape(dep * token_count, width)
    own_share = own_input_terms(*own_weights, own)
    own_block, across, own_share, other = lax.optimization_barrier(
        (own_block, all_tokens.T, own_share, other)
    )
    other_grad = lax.ppermute(weight_terms(across, 1, own_block, factor), "inp", pairs)
    own_grad = weight_terms(across, 0, own_block, factor)

    at_out = lax.axis_index("out")
    core = (at_out % 2).reshape(1)
    chip = (at_out // 2).reshape(1)
    kept, given = other_input_terms(core, *other_weights, other, own_share, out)
    received = lax.ppermute(given, "out", [(i, i ^ 1) for i in range(out)])
    own_grad, received = lax.optimization_barrier((own_grad, received))
    mine, *sent = split_shares(chip, kept, received)
    for k, block in enumerate(sent, 1):
        mine = mine + lax.ppermute(block, "out", [(i, i ^ 2 * k) for i in range(out)]).astype(F32)
    grad_input = mine.astype(BF16).T

    grad = jnp.concatenate([own_grad, other_grad], axis=1)
    swapped = lax.all_to_all(grad.reshape(dep, feature_count // dep, 2 * width), "dep", 0, 0)
    gate_grad, up_grad = finished(own_side, swapped, half, skips)
    return grad_input, gate_grad, up_grad


def solution(mesh):
    return jax.shard_map(
        shards,
        mesh=mesh,
        in_specs=(P("dep", "inp"), P("dep", "out"), P("inp", "out"), P("inp", "out")),
        out_specs=(P("dep", ("inp", "out")), P(("inp", "dep"), "out"), P(("inp", "dep"), "out")),
        check_vma=False,
    )
```

time: 191 us -> 199 us (1.042)
  the two profiles are of different devices: /device:TPU:64 before, /device:TPU:10 now
where the time goes in v5:
time: 199 us; the launch traced here: 198 us
  starting transfers between devices  59.3 us (30%)
  waiting for transfers between devices  53.7 us (27%)
  blocking collectives  38.1 us (19%)
  Pallas kernels  15.9 us (8%)
  between operations  14.3 us (7%)
  local copies, waits for them, and re-layouts  12.5 us (6%)
  other arithmetic  4.37 us (2%)
    all_gather x1, blocking collectives, shards(): lax.all_gather(grad_pair(terms, cotangent), 'inp', axis=0, tiled=True, ax...  38.1 us
    all_to_all x1, waiting for transfers between devices, shards(): lax.all_to_all(kept.reshape(group, rows, hidden), 'inp', 0, 0, axis_index...  25 us
    all_to_all x1, starting transfers between devices, shards(): lax.all_to_all(kept.reshape(group, rows, hidden), 'inp', 0, 0, axis_index...  17.8 us
    ppermute x1, waiting for transfers between devices, shards(): kept = kept.astype(F32) + lax.ppermute(given, 'inp', pairs).astype(F32)  15.1 us
    ppermute x3, starting transfers between devices, shards(): lax.ppermute(block, 'out', [(i, i ^ 2 * k) for i in range(out)]).astype(F32)  12.2 us
    all_to_all x1, starting transfers between devices, shards(): own_block = lax.all_to_all(dep_pieces(own, starts, width), 'dep', 0, 0)  6.71 us
    ppermute x1, waiting for transfers between devices, shards(): other = lax.ppermute(own, 'inp', pairs)  6.58 us
    pallas_call x2, Pallas kernels, partial_values(): pl.pallas_call(values_kernel, out_shape=jax.ShapeDtypeStruct((token_count...  5.81 us
  transfers between devices with their start and end apart: 12, of which 6 were waited for; matrix products, arithmetic and copies ran while one was open for 5% of the time, Pallas kernels for 7%

profile of v5, /device:TPU:10, one launch (start us, length us, event | category | flops | bytes accessed | tf_op | source)
XLA Modules:
  0.0 198.2 jit_solution(11846552348809087731)
XLA Ops:
  7.2 0.0 all-gather.2.cloned.1.call-start
  7.2 4.3 %collective-permute-start = (bf16[192,512]{1,0:T(8,128)(2,1)}, bf16[192,512]{1,0:T(8,128)(2,1)S(1)}, u32[]{:S(2)}, u32[]{:S(2)}) collective-permute-start(bf16[192,512]{1,0:T(8,128)(2,1)} %tokens_hbm.3), channel_id=1, source_target_pairs={{0,64},{64,0},{128,192},{192,128},{256,320},{320,256},{384,448},{4... | collective-permute-start | bytes 589832 | tf_op jit(solution)/shard_map/ppermute | solution.py:272
  11.5 0.0 copy-start.7
  11.5 2.9 %shard_map.67 = bf16[192,1792]{1,0:T(8,128)(2,1)} custom-call(s32[1]{0:T(128)} %bitcast.2.side_ref, bf16[192,512]{1,0:T(8,128)(2,1)} %tokens_hbm.3, bf16[512,1792]{1,0:T(8,128)(2,1)} %gate_hbm.3, bf16[512,1792]{1,0:T(8,128)(2,1)} %up_hbm.3), custom_call_target="tpu_custom_call" | custom-call | flops 352321536 | bytes 2523136 | tf_op jit(solution)/shard_map/pallas_call | solution.py:57
  14.4 2.2 %collective-permute-done = bf16[192,512]{1,0:T(8,128)(2,1)S(1)} collective-permute-done((bf16[192,512]{1,0:T(8,128)(2,1)}, bf16[192,512]{1,0:T(8,128)(2,1)S(1)}, u32[]{:S(2)}, u32[]{:S(2)}) %collective-permute-start) | collective-permute-done | bytes 196640 | tf_op jit(solution)/shard_map/ppermute | solution.py:272
  16.6 0.9 pad_maximum_fusion.1
  17.5 0.0 all-gather.2.cloned.1.call-update
  17.5 0.0 copy-start.6
  17.5 2.9 %shard_map.68 = bf16[192,1792]{1,0:T(8,128)(2,1)} custom-call(s32[1]{0:T(128)S(6)} %sub.14.side_ref, bf16[192,512]{1,0:T(8,128)(2,1)} %tokens_hbm.3, bf16[512,1792]{1,0:T(8,128)(2,1)} %gate_hbm.3, bf16[512,1792]{1,0:T(8,128)(2,1)} %up_hbm.3), custom_call_target="tpu_custom_call" | custom-call | flops 352321536 | bytes 2523136 | tf_op jit(solution)/shard_map/pallas_call | solution.py:57
  20.4 3.6 %collective-permute-start.1 = (bf16[192,1792]{1,0:T(8,128)(2,1)}, bf16[192,1792]{1,0:T(8,128)(2,1)S(1)}, u32[]{:S(2)}, u32[]{:S(2)}) collective-permute-start(bf16[192,1792]{1,0:T(8,128)(2,1)} %shard_map.68), channel_id=1, source_target_pairs={{0,64},{64,0},{128,192},{192,128},{256,320},{320,256},{384,448},{4... | collective-permute-start | bytes 2064392 | tf_op jit(solution)/shard_map/ppermute | solution.py:278
  24.1 15.1 %collective-permute-done.1 = bf16[192,1792]{1,0:T(8,128)(2,1)S(1)} collective-permute-done((bf16[192,1792]{1,0:T(8,128)(2,1)}, bf16[192,1792]{1,0:T(8,128)(2,1)S(1)}, u32[]{:S(2)}, u32[]{:S(2)}) %collective-permute-start.1) | collective-permute-done | bytes 688160 | tf_op jit(solution)/shard_map/ppermute | solution.py:278
  39.1 1.0 add_convert_fusion
  40.2 17.8 %all-to-all-start = ((bf16[8,24,1792]{2,1,0:T(8,128)(2,1)}), bf16[8,24,1792]{2,1,0:T(8,128)(2,1)S(1)}, u32[]{:S(2)}, u32[]{:S(2)}) async-start(bf16[8,24,1792]{2,1,0:T(8,128)(2,1)} %bitcast.3), calls=%async_computation | async-start | bytes 1376256 | tf_op jit(solution)/shard_map/all_to_all | solution.py:280
  58.0 0.8 dynamic_slice.19.cotangent_ref
  58.8 3.6 %constant_dynamic-slice_fusion = (bf16[512,896]{1,0:T(8,128)(2,1)}, bf16[512,896]{1,0:T(8,128)(2,1)S(1)}, bf16[512,896]{1,0:T(8,128)(2,1)S(1)}, bf16[512,896]{1,0:T(8,128)(2,1)}) fusion(bf16[512,1792]{1,0:T(8,128)(2,1)} %up_hbm.3, s32[]{:T(128)S(6)} %select_n.34, s32[]{:T(128)S(6)} %select_n.33, bf16[512,1792]{1,0:T(8,128)(2,1)} %gate_hbm.3), kind=kLoop, calls=%fused_computation.5 | loop fusion | bytes 7340040 | tf_op jit(solution)/shard_map/dynamic_slice | solution.py:287
  62.4 25.0 %all-to-all-done.terms_ref = bf16[8,24,1792]{2,1,0:T(8,128)(2,1)S(1)} async-done(((bf16[8,24,1792]{2,1,0:T(8,128)(2,1)}), bf16[8,24,1792]{2,1,0:T(8,128)(2,1)S(1)}, u32[]{:S(2)}, u32[]{:S(2)}) %all-to-all-start) | async-done | bytes 688160 | tf_op jit(solution)/shard_map/all_to_all | solution.py:280
  87.4 0.1 shard_map.69
  87.5 38.1 %all_gather.6.pair_ref = bf16[192,1792]{1,0:T(8,128)(2,1)} all-gather(bf16[24,1792]{1,0:T(8,128)(2,1)S(1)} %shard_map.69), channel_id=1, replica_groups={{0,128,256,384,512,640,768,896},{64,192,320,448,576,704,832,960},{1,129..., dimensions={0}, use_global_device_ids=true | all-gather | bytes 774144 | tf_op jit(solution)/shard_map/all_gather | solution.py:293
  125.6 2.0 %shard_map.70 = bf16[8,192,256]{2,1,0:T(8,128)(2,1)} custom-call(bf16[192,1792]{1,0:T(8,128)(2,1)} %all_gather.6.pair_ref), custom_call_target="tpu_custom_call" | custom-call | bytes 1572864 | tf_op jit(solution)/shard_map/pallas_call | solution.py:118
  127.7 6.7 %all-to-all-start.1 = ((bf16[8,192,256]{2,1,0:T(8,128)(2,1)}), bf16[8,192,256]{2,1,0:T(8,128)(2,1)}, u32[]{:S(2)}, u32[]{:S(2)}) async-start(bf16[8,192,256]{2,1,0:T(8,128)(2,1)} %shard_map.70), calls=%async_computation.1 | async-start | bytes 1572864 | tf_op jit(solution)/shard_map/all_to_all | solution.py:302
  134.4 3.5 %collective-permute-start.2 = (bf16[192,1792]{1,0:T(8,128)(2,1)}, bf16[192,1792]{1,0:T(8,128)(2,1)}, u32[]{:S(2)}, u32[]{:S(2)}) collective-permute-start(bf16[192,1792]{1,0:T(8,128)(2,1)} %all_gather.6.pair_ref), channel_id=1, source_target_pairs={{0,64},{64,0},{128,192},{192,128},{256,320},{320,256},{384,448},{4... | collective-permute-start | bytes 2064392 | tf_op jit(solution)/shard_map/ppermute | solution.py:296
  137.9 1.8 shard_map.71.own_ref
  139.7 0.8 copy-done.2
  140.6 3.2 %copy.9 = bf16[1536,1024]{0,1:T(8,128)(2,1)S(1)} copy(bf16[1536,1024]{1,0:T(8,128)(2,1)} %all-gather.2.cloned.1.call-done) | data formatting | bytes 6291456 | tf_op jit(solution)/shard_map/all_gather | solution.py:277
  143.8 6.6 %collective-permute-done.2.pair_ref = bf16[192,1792]{1,0:T(8,128)(2,1)} collective-permute-done((bf16[192,1792]{1,0:T(8,128)(2,1)}, bf16[192,1792]{1,0:T(8,128)(2,1)}, u32[]{:S(2)}, u32[]{:S(2)}) %collective-permute-start.2) | collective-permute-done | bytes 688160 | tf_op jit(solution)/shard_map/ppermute | solution.py:296
  150.3 0.0 all-to-all-done.1
  150.3 1.7 shard_map.75
  152.1 3.5 %collective-permute-start.7 = (bf16[512,256]{1,0:T(8,128)(2,1)S(1)}, bf16[512,256]{1,0:T(8,128)(2,1)}, u32[]{:S(2)}, u32[]{:S(2)}) collective-permute-start(bf16[512,256]{1,0:T(8,128)(2,1)S(1)} %shard_map.75), channel_id=1, source_target_pairs={{0,64},{64,0},{128,192},{192,128},{256,320},{320,256},{384,448},{4... | collective-permute-start | bytes 786440 | tf_op jit(solution)/shard_map/ppermute | solution.py:308
  155.6 1.2 copy-done
  156.8 1.2 copy-done.1
  157.9 1.0 copy-done.3
  159.0 1.9 shard_map.72
  160.9 0.7 copy-done.4
  161.5 1.9 collective-permute-start.3
  163.5 1.7 shard_map.73
  165.2 0.0 collective-permute-done.3.received_ref
  165.2 0.0 collective-permute-done.7
  165.2 1.8 pad_maximum_fusion
  167.0 5.7 %all-to-all-start.2 = ((bf16[8,64,512]{2,1,0:T(8,128)(2,1)}), bf16[8,64,512]{2,1,0:T(8,128)(2,1)S(1)}, u32[]{:S(2)}, u32[]{:S(2)}) async-start(bf16[8,64,512]{2,1,0:T(8,128)(2,1)} %bitcast.7), calls=%async_computation.2 | async-start | bytes 1048576 | tf_op jit(solution)/shard_map/all_to_all | solution.py:323
  172.8 2.8 %collective-permute-start.4 = (bf16[64,192]{1,0:T(8,128)(2,1)S(1)}, bf16[64,192]{1,0:T(8,128)(2,1)S(1)}, u32[]{:S(2)}, u32[]{:S(2)}) collective-permute-start(bf16[64,192]{1,0:T(8,128)(2,1)S(1)} %get-tuple-element.45), channel_id=1, source_target_pairs={{0,16},{8,24},{16,0},{24,8},{32,48},{40,56},{48,32},{56,40},{1,17}... | collective-permute-start | bytes 73736 | tf_op jit(solution)/shard_map/ppermute | solution.py:319
  175.6 6.0 %collective-permute-start.5 = (bf16[64,192]{1,0:T(8,128)(2,1)S(1)}, bf16[64,192]{1,0:T(8,128)(2,1)S(1)}, u32[]{:S(2)}, u32[]{:S(2)}) collective-permute-start(bf16[64,192]{1,0:T(8,128)(2,1)S(1)} %get-tuple-element.46), channel_id=1, source_target_pairs={{0,32},{8,40},{16,48},{24,56},{32,0},{40,8},{48,16},{56,24},{1,33}... | collective-permute-start | bytes 73736 | tf_op jit(solution)/shard_map/ppermute | solution.py:319
  181.6 3.4 %collective-permute-start.6 = (bf16[64,192]{1,0:T(8,128)(2,1)S(1)}, bf16[64,192]{1,0:T(8,128)(2,1)S(1)}, u32[]{:S(2)}, u32[]{:S(2)}) collective-permute-start(bf16[64,192]{1,0:T(8,128)(2,1)S(1)} %get-tuple-element.47), channel_id=1, source_target_pairs={{0,48},{8,56},{16,32},{24,40},{32,16},{40,24},{48,0},{56,8},{1,49}... | collective-permute-start | bytes 73736 | tf_op jit(solution)/shard_map/ppermute | solution.py:319
  185.0 0.0 collective-permute-done.4
  185.0 0.6 collective-permute-done.5
  185.7 4.2 %collective-permute-done.6 = bf16[64,192]{1,0:T(8,128)(2,1)S(1)} collective-permute-done((bf16[64,192]{1,0:T(8,128)(2,1)S(1)}, bf16[64,192]{1,0:T(8,128)(2,1)S(1)}, u32[]{:S(2)}, u32[]{:S(2)}) %collective-permute-start.6) | collective-permute-done | bytes 24608 | tf_op jit(solution)/shard_map/ppermute | solution.py:319
  189.9 0.6 fusion
  190.5 0.0 all-to-all-done.2.swapped_ref
  190.5 0.8 shard_map.76
  (11 shorter events, 0.0 us)
Async XLA Ops:
  7.2 133.4 %all-gather.2.cloned.1.call-start = ((), (), s32[]{:S(2)}) async-start(), calls=%async_computation.3 | async-start | bytes 3538944 | tf_op jit(solution)/shard_map/all_gather | solution.py:277
  7.2 9.4 %collective-permute-start = (bf16[192,512]{1,0:T(8,128)(2,1)}, bf16[192,512]{1,0:T(8,128)(2,1)S(1)}, u32[]{:S(2)}, u32[]{:S(2)}) collective-permute-start(bf16[192,512]{1,0:T(8,128)(2,1)} %tokens_hbm.3), channel_id=1, source_target_pairs={{0,64},{64,0},{128,192},{192,128},{256,320},{320,256},{384,448},{4... | collective-permute-start | bytes 589832 | tf_op jit(solution)/shard_map/ppermute | solution.py:272
  11.5 5.1 %copy-start.7 = (bf16[192,512]{1,0:T(8,128)(2,1)S(1)}, bf16[192,512]{1,0:T(8,128)(2,1)}, u32[]{:S(2)}) copy-start(bf16[192,512]{1,0:T(8,128)(2,1)} %tokens_hbm.3) | copy-start | bytes 589828
  17.5 21.7 %copy-start.6 = (bf16[192,1792]{1,0:T(8,128)(2,1)S(1)}, bf16[192,1792]{1,0:T(8,128)(2,1)}, u32[]{:S(2)}) copy-start(bf16[192,1792]{1,0:T(8,128)(2,1)} %shard_map.67) | copy-start | bytes 2064388
  20.4 18.7 %collective-permute-start.1 = (bf16[192,1792]{1,0:T(8,128)(2,1)}, bf16[192,1792]{1,0:T(8,128)(2,1)S(1)}, u32[]{:S(2)}, u32[]{:S(2)}) collective-permute-start(bf16[192,1792]{1,0:T(8,128)(2,1)} %shard_map.68), channel_id=1, source_target_pairs={{0,64},{64,0},{128,192},{192,128},{256,320},{320,256},{384,448},{4... | collective-permute-start | bytes 2064392 | tf_op jit(solution)/shard_map/ppermute | solution.py:278
  40.2 47.2 %all-to-all-start = ((bf16[8,24,1792]{2,1,0:T(8,128)(2,1)}), bf16[8,24,1792]{2,1,0:T(8,128)(2,1)S(1)}, u32[]{:S(2)}, u32[]{:S(2)}) async-start(bf16[8,24,1792]{2,1,0:T(8,128)(2,1)} %bitcast.3), calls=%async_computation | async-start | bytes 1376256 | tf_op jit(solution)/shard_map/all_to_all | solution.py:280
  127.7 22.7 %all-to-all-start.1 = ((bf16[8,192,256]{2,1,0:T(8,128)(2,1)}), bf16[8,192,256]{2,1,0:T(8,128)(2,1)}, u32[]{:S(2)}, u32[]{:S(2)}) async-start(bf16[8,192,256]{2,1,0:T(8,128)(2,1)} %shard_map.70), calls=%async_computation.1 | async-start | bytes 1572864 | tf_op jit(solution)/shard_map/all_to_all | solution.py:302
  134.4 15.9 %collective-permute-start.2 = (bf16[192,1792]{1,0:T(8,128)(2,1)}, bf16[192,1792]{1,0:T(8,128)(2,1)}, u32[]{:S(2)}, u32[]{:S(2)}) collective-permute-start(bf16[192,1792]{1,0:T(8,128)(2,1)} %all_gather.6.pair_ref), channel_id=1, source_target_pairs={{0,64},{64,0},{128,192},{192,128},{256,320},{320,256},{384,448},{4... | collective-permute-start | bytes 2064392 | tf_op jit(solution)/shard_map/ppermute | solution.py:296
  139.7 0.8 copy-start.2
  152.1 13.1 %collective-permute-start.7 = (bf16[512,256]{1,0:T(8,128)(2,1)S(1)}, bf16[512,256]{1,0:T(8,128)(2,1)}, u32[]{:S(2)}, u32[]{:S(2)}) collective-permute-start(bf16[512,256]{1,0:T(8,128)(2,1)S(1)} %shard_map.75), channel_id=1, source_target_pairs={{0,64},{64,0},{128,192},{192,128},{256,320},{320,256},{384,448},{4... | collective-permute-start | bytes 786440 | tf_op jit(solution)/shard_map/ppermute | solution.py:308
  155.6 1.2 copy-start
  156.8 1.2 copy-start.1
  157.9 1.0 copy-start.3
  160.8 0.7 copy-start.4
  161.5 3.6 %collective-permute-start.3 = (bf16[4,64,192]{2,1,0:T(8,128)(2,1)S(1)}, bf16[4,64,192]{2,1,0:T(8,128)(2,1)S(1)}, u32[]{:S(2)}, u32[]{:S(2)}) collective-permute-start(bf16[4,64,192]{2,1,0:T(8,128)(2,1)S(1)} %get-tuple-element.42), channel_id=1, source_target_pairs={{0,8},{8,0},{16,24},{24,16},{32,40},{40,32},{48,56},{56,48},{1,9},... | collective-permute-start | bytes 294920 | tf_op jit(solution)/shard_map/ppermute | solution.py:315
  165.2 7.6 %copy-start.5 = (f32[4,64,192]{2,1,0:T(8,128)S(1)}, f32[4,64,192]{2,1,0:T(8,128)}, u32[]{:S(2)}) copy-start(f32[4,64,192]{2,1,0:T(8,128)} %copy-done.4) | copy-start | bytes 589828
  167.0 23.5 %all-to-all-start.2 = ((bf16[8,64,512]{2,1,0:T(8,128)(2,1)}), bf16[8,64,512]{2,1,0:T(8,128)(2,1)S(1)}, u32[]{:S(2)}, u32[]{:S(2)}) async-start(bf16[8,64,512]{2,1,0:T(8,128)(2,1)} %bitcast.7), calls=%async_computation.2 | async-start | bytes 1048576 | tf_op jit(solution)/shard_map/all_to_all | solution.py:323
  172.8 12.2 %collective-permute-start.4 = (bf16[64,192]{1,0:T(8,128)(2,1)S(1)}, bf16[64,192]{1,0:T(8,128)(2,1)S(1)}, u32[]{:S(2)}, u32[]{:S(2)}) collective-permute-start(bf16[64,192]{1,0:T(8,128)(2,1)S(1)} %get-tuple-element.45), channel_id=1, source_target_pairs={{0,16},{8,24},{16,0},{24,8},{32,48},{40,56},{48,32},{56,40},{1,17}... | collective-permute-start | bytes 73736 | tf_op jit(solution)/shard_map/ppermute | solution.py:319
  175.6 10.1 %collective-permute-start.5 = (bf16[64,192]{1,0:T(8,128)(2,1)S(1)}, bf16[64,192]{1,0:T(8,128)(2,1)S(1)}, u32[]{:S(2)}, u32[]{:S(2)}) collective-permute-start(bf16[64,192]{1,0:T(8,128)(2,1)S(1)} %get-tuple-element.46), channel_id=1, source_target_pairs={{0,32},{8,40},{16,48},{24,56},{32,0},{40,8},{48,16},{56,24},{1,33}... | collective-permute-start | bytes 73736 | tf_op jit(solution)/shard_map/ppermute | solution.py:319
  181.6 8.3 %collective-permute-start.6 = (bf16[64,192]{1,0:T(8,128)(2,1)S(1)}, bf16[64,192]{1,0:T(8,128)(2,1)S(1)}, u32[]{:S(2)}, u32[]{:S(2)}) collective-permute-start(bf16[64,192]{1,0:T(8,128)(2,1)S(1)} %get-tuple-element.47), channel_id=1, source_target_pairs={{0,48},{8,56},{16,32},{24,40},{32,16},{40,24},{48,0},{56,8},{1,49}... | collective-permute-start | bytes 73736 | tf_op jit(solution)/shard_map/ppermute | solution.py:319
Sparse Core Ops, SparseCore 0:
  17.6 60.2 all-gather.1

commit v6 on v5

--- a/solution.py
+++ b/solution.py
@@ -118,7 +118,7 @@
     return pl.pallas_call(
         functools.partial(pieces_kernel, starts),
         out_shape=jax.ShapeDtypeStruct(shape, BF16),
-        compiler_params=PARAMS,
+        compiler_params=pltpu.CompilerParams(vmem_limit_bytes=40 * 2**20),
         cost_estimate=pl.CostEstimate(
             flops=0, bytes_accessed=4 * math.prod(shape), transcendentals=0
         ),
@@ -138,14 +138,17 @@
     )
 
 
-def other_input_kernel(core_ref, gate_ref, up_ref, pair_ref, own_ref, kept_ref, given_ref, total):
-    own_input_kernel(gate_ref, up_ref, pair_ref, total)
-    blocks, rows, _ = kept_ref.shape
-    core = core_ref[0]
-    for y in range(blocks):
-        for which, ref in ((core, kept_ref), (1 - core, given_ref)):
-            at = pl.ds(pl.multiple_of((2 * y + which) * rows, rows), rows)
-            ref[y] = (total[at, :] + own_ref[at, :]).astype(ref.dtype)
+def other_input_kernel(gate_ref, up_ref, pair_ref, own_ref, out_ref):
+    half = gate_ref.shape[1]
+    total = own_ref[...]
+    for u, w_ref in enumerate((gate_ref, up_ref)):
+        total = total + lax.dot_general(
+            w_ref[...],
+            pair_ref[:, u * half : (u + 1) * half],
+            COLS_BY_COLS,
+            preferred_element_type=F32,
+        )
+    out_ref[...] = total.astype(BF16)
 
 
 def product_cost(pair, feature_count):
@@ -165,39 +168,13 @@
     )(gate, up, pair)
 
 
-def other_input_terms(core, gate, up, pair, own, out):
-    feature_count, token_count = own.shape
-    shape = (out // 2, feature_count // out, token_count)
+def other_input_terms(gate, up, pair, own):
     return pl.pallas_call(
         other_input_kernel,
-        out_shape=(jax.ShapeDtypeStruct(shape, F32), jax.ShapeDtypeStruct(shape, BF16)),
-        in_specs=[IN_SMEM] + [IN_VMEM] * 4,
-        out_specs=(IN_VMEM, IN_VMEM),
-        scratch_shapes=[pltpu.VMEM((feature_count, token_count), F32)],
-        compiler_params=PARAMS,
-        cost_estimate=product_cost(pair, feature_count),
-    )(core, gate, up, pair, own)
-
-
-def split_kernel(index_ref, kept_ref, received_ref, mine_ref, *sent_refs):
-    for k, ref in enumerate((mine_ref, *sent_refs)):
-        at = index_ref[0] ^ k
-        ref[...] = (kept_ref[at] + received_ref[at].astype(F32)).astype(ref.dtype)
-
-
-def split_shares(index, kept, received):
-    shape = kept.shape[1:]
-    others = kept.shape[0] - 1
-    return pl.pallas_call(
-        split_kernel,
-        out_shape=[jax.ShapeDtypeStruct(shape, F32)] + [jax.ShapeDtypeStruct(shape, BF16)] * others,
-        in_specs=[IN_SMEM, IN_VMEM, IN_VMEM],
-        out_specs=[IN_VMEM] * (others + 1),
-        compiler_params=PARAMS,
-        cost_estimate=pl.CostEstimate(
-            flops=2 * kept.size, bytes_accessed=10 * kept.size, transcendentals=0
-        ),
-    )(index, kept, received)
+        out_shape=jax.ShapeDtypeStruct(own.shape, BF16),
+        compiler_params=PARAMS,
+        cost_estimate=product_cost(pair, own.shape[0]),
+    )(gate, up, pair, own)
 
 
 def weight_kernel(which, factor, tokens_ref, block_ref, out_ref):
@@ -269,14 +246,15 @@
     own_side = parity.reshape(1)
     other_side = 1 - own_side
 
-    theirs = lax.ppermute(tokens, "inp", pairs)
     given = partial_values(other_side, tokens, w_gate, w_up)
+    own_side, given = lax.optimization_barrier((own_side, given))
     kept = partial_values(own_side, tokens, w_gate, w_up)
-    theirs, kept = lax.optimization_barrier((theirs, kept))
+    mine, kept = lax.optimization_barrier((tokens, kept))
+    theirs = lax.ppermute(mine, "inp", pairs)
+    kept = kept.astype(F32) + lax.ppermute(given, "inp", pairs).astype(F32)
+    kept, w_gate, w_up, theirs = lax.optimization_barrier((kept.astype(BF16), w_gate, w_up, theirs))
     two = jnp.concatenate([tokens, theirs], axis=1)
     all_tokens = lax.all_gather(two, "dep", axis=0, tiled=True)
-    kept = kept.astype(F32) + lax.ppermute(given, "inp", pairs).astype(F32)
-    kept, w_gate, w_up = lax.optimization_barrier((kept.astype(BF16), w_gate, w_up))
     terms = lax.all_to_all(
         kept.reshape(group, rows, hidden), "inp", 0, 0, axis_index_groups=alike
     )
@@ -302,22 +280,14 @@
     own_block = lax.all_to_all(dep_pieces(own, starts, width), "dep", 0, 0)
     own_block = own_block.reshape(dep * token_count, width)
     own_share = own_input_terms(*own_weights, own)
-    own_block, across, own_share, other = lax.optimization_barrier(
-        (own_block, all_tokens.T, own_share, other)
-    )
+    shares = other_input_terms(*other_weights, other, own_share)
+    own_block, across, shares = lax.optimization_barrier((own_block, all_tokens.T, shares))
     other_grad = lax.ppermute(weight_terms(across, 1, own_block, factor), "inp", pairs)
     own_grad = weight_terms(across, 0, own_block, factor)
-
-    at_out = lax.axis_index("out")
-    core = (at_out % 2).reshape(1)
-    chip = (at_out // 2).reshape(1)
-    kept, given = other_input_terms(core, *other_weights, other, own_share, out)
-    received = lax.ppermute(given, "out", [(i, i ^ 1) for i in range(out)])
-    own_grad, received = lax.optimization_barrier((own_grad, received))
-    mine, *sent = split_shares(chip, kept, received)
-    for k, block in enumerate(sent, 1):
-        mine = mine + lax.ppermute(block, "out", [(i, i ^ 2 * k) for i in range(out)]).astype(F32)
-    grad_input = mine.astype(BF16).T
+    shares = lax.all_to_all(
+        shares.reshape(out, feature_count // out, token_count), "out", 0, 0
+    )
+    grad_input = jnp.sum(shares.astype(F32), axis=0).astype(BF16).T
 
     grad = jnp.concatenate([own_grad, other_grad], axis=1)
     swapped = lax.all_to_all(grad.reshape(dep, feature_count // dep, 2 * width), "dep", 0, 0)

time: 199 us -> 192 us (0.965)
  the two profiles are of different devices: /device:TPU:10 before, /device:TPU:8 now
where the time goes in v6:
time: 192 us; the launch traced here: 191 us
  waiting for transfers between devices  61.3 us (32%)
  starting transfers between devices  50.7 us (26%)
  blocking collectives  37.4 us (19%)
  between operations  14.2 us (7%)
  Pallas kernels  12.3 us (6%)
  local copies, waits for them, and re-layouts  9.29 us (5%)
  other arithmetic  6.31 us (3%)
    all_gather x1, blocking collectives, shards(): lax.all_gather(grad_pair(terms, cotangent), 'inp', axis=0, tiled=True, ax...  37.4 us
    all_to_all x1, waiting for transfers between devices, shards(): lax.all_to_all(kept.reshape(group, rows, hidden), 'inp', 0, 0, axis_index...  26.3 us
    all_to_all x1, starting transfers between devices, shards(): lax.all_to_all(kept.reshape(group, rows, hidden), 'inp', 0, 0, axis_index...  18.1 us
    ppermute x1, waiting for transfers between devices, shards(): kept = kept.astype(F32) + lax.ppermute(given, 'inp', pairs).astype(F32)  11.6 us
    all_to_all x1, waiting for transfers between devices, shards(): lax.all_to_all(shares.reshape(out, feature_count // out, token_count), 'o...  8.06 us
    all_to_all x1, waiting for transfers between devices, shards(): lax.all_to_all(grad.reshape(dep, feature_count // dep, 2 * width), 'dep',...  7.02 us
    ppermute x1, waiting for transfers between devices, shards(): other = lax.ppermute(own, 'inp', pairs)  6.99 us
    all_to_all x1, starting transfers between devices, shards(): lax.all_to_all(shares.reshape(out, feature_count // out, token_count), 'o...  6.43 us
  transfers between devices with their start and end apart: 9, of which 6 were waited for; matrix products, arithmetic and copies ran while one was open for 7% of the time, Pallas kernels for 4%

profile of v6, /device:TPU:8, one launch (start us, length us, event | category | flops | bytes accessed | tf_op | source)
XLA Modules:
  0.0 191.4 jit_solution(14790879033240608686)
XLA Ops:
  7.2 0.0 all-gather.2.cloned.1.call-start
  7.2 2.8 %shard_map.67 = bf16[192,1792]{1,0:T(8,128)(2,1)} custom-call(s32[1]{0:T(128)S(6)} %sub.10.side_ref, bf16[192,512]{1,0:T(8,128)(2,1)} %tokens_hbm.3, bf16[512,1792]{1,0:T(8,128)(2,1)} %gate_hbm.3, bf16[512,1792]{1,0:T(8,128)(2,1)} %up_hbm.3), custom_call_target="tpu_custom_call" | custom-call | flops 352321536 | bytes 2523136 | tf_op jit(solution)/shard_map/pallas_call | solution.py:57
  10.1 0.0 copy-start.2
  10.1 4.4 %collective-permute-start = (bf16[192,1792]{1,0:T(8,128)(2,1)}, bf16[192,1792]{1,0:T(8,128)(2,1)S(1)}, u32[]{:S(2)}, u32[]{:S(2)}) collective-permute-start(bf16[192,1792]{1,0:T(8,128)(2,1)} %shard_map.67), channel_id=1, source_target_pairs={{0,64},{64,0},{128,192},{192,128},{256,320},{320,256},{384,448},{4... | collective-permute-start | bytes 2064392 | tf_op jit(solution)/shard_map/ppermute | solution.py:254
  14.5 2.9 %shard_map.68 = bf16[192,1792]{1,0:T(8,128)(2,1)} custom-call(s32[1]{0:T(128)} %bitcast.side_ref, bf16[192,512]{1,0:T(8,128)(2,1)} %tokens_hbm.3, bf16[512,1792]{1,0:T(8,128)(2,1)} %gate_hbm.3, bf16[512,1792]{1,0:T(8,128)(2,1)} %up_hbm.3), custom_call_target="tpu_custom_call" | custom-call | flops 352321536 | bytes 2523136 | tf_op jit(solution)/shard_map/pallas_call | solution.py:57
  17.4 0.0 copy-done.2
  17.4 1.9 %collective-permute-start.1 = (bf16[192,512]{1,0:T(8,128)(2,1)S(1)}, bf16[192,512]{1,0:T(8,128)(2,1)S(1)}, u32[]{:S(2)}, u32[]{:S(2)}) collective-permute-start(bf16[192,512]{1,0:T(8,128)(2,1)S(1)} %copy-done.2), channel_id=1, source_target_pairs={{0,64},{64,0},{128,192},{192,128},{256,320},{320,256},{384,448},{4... | collective-permute-start | bytes 589832 | tf_op jit(solution)/shard_map/ppermute | solution.py:253
  19.3 11.6 %collective-permute-done = bf16[192,1792]{1,0:T(8,128)(2,1)S(1)} collective-permute-done((bf16[192,1792]{1,0:T(8,128)(2,1)}, bf16[192,1792]{1,0:T(8,128)(2,1)S(1)}, u32[]{:S(2)}, u32[]{:S(2)}) %collective-permute-start) | collective-permute-done | bytes 688160 | tf_op jit(solution)/shard_map/ppermute | solution.py:254
  31.0 2.1 %add_convert_fusion = bf16[192,1792]{1,0:T(8,128)(2,1)} fusion(bf16[192,1792]{1,0:T(8,128)(2,1)S(1)} %collective-permute-done, bf16[192,1792]{1,0:T(8,128)(2,1)} %shard_map.68), kind=kLoop, calls=%fused_computation | loop fusion | flops 1376256 | bytes 2064384 | tf_op jit(solution)/shard_map/convert_element_type | solution.py:255
  33.1 1.3 collective-permute-done.1
  34.3 0.8 pad_maximum_fusion.1
  35.2 0.0 all-gather.2.cloned.1.call-update
  35.2 18.1 %all-to-all-start = ((bf16[8,24,1792]{2,1,0:T(8,128)(2,1)}), bf16[8,24,1792]{2,1,0:T(8,128)(2,1)S(1)}, u32[]{:S(2)}, u32[]{:S(2)}) async-start(bf16[8,24,1792]{2,1,0:T(8,128)(2,1)} %bitcast.1), calls=%async_computation | async-start | bytes 1376256 | tf_op jit(solution)/shard_map/all_to_all | solution.py:258
  53.3 0.8 dynamic_slice.19.cotangent_ref
  54.1 3.3 %constant_dynamic-slice_fusion = (bf16[512,896]{1,0:T(8,128)(2,1)S(1)}, bf16[512,896]{1,0:T(8,128)(2,1)S(1)}, bf16[512,896]{1,0:T(8,128)(2,1)}, bf16[512,896]{1,0:T(8,128)(2,1)S(1)}) fusion(bf16[512,1792]{1,0:T(8,128)(2,1)} %up_hbm.3, s32[]{:T(128)S(6)} %select_n.25, s32[]{:T(128)S(6)} %select_n.24, bf16[512,1792]{1,0:T(8,128)(2,1)} %gate_hbm.3), kind=kLoop, calls=%fused_computation.3 | loop fusion | bytes 7340040 | tf_op jit(solution)/shard_map/dynamic_slice | solution.py:265
  57.4 26.3 %all-to-all-done.terms_ref = bf16[8,24,1792]{2,1,0:T(8,128)(2,1)S(1)} async-done(((bf16[8,24,1792]{2,1,0:T(8,128)(2,1)}), bf16[8,24,1792]{2,1,0:T(8,128)(2,1)S(1)}, u32[]{:S(2)}, u32[]{:S(2)}) %all-to-all-start) | async-done | bytes 688160 | tf_op jit(solution)/shard_map/all_to_all | solution.py:258
  83.7 0.1 shard_map.69
  83.8 37.4 %all_gather.6.pair_ref = bf16[192,1792]{1,0:T(8,128)(2,1)S(1)} all-gather(bf16[24,1792]{1,0:T(8,128)(2,1)S(1)} %shard_map.69), channel_id=1, replica_groups={{0,128,256,384,512,640,768,896},{64,192,320,448,576,704,832,960},{1,129..., dimensions={0}, use_global_device_ids=true | all-gather | bytes 774144 | tf_op jit(solution)/shard_map/all_gather | solution.py:271
  121.2 0.1 shard_map.70
  121.2 0.0 copy-start.1
  121.3 0.9 copy-done.1
  122.2 5.3 %all-to-all-start.1 = ((bf16[8,192,256]{2,1,0:T(8,128)(2,1)}), bf16[8,192,256]{2,1,0:T(8,128)(2,1)}, u32[]{:S(2)}, u32[]{:S(2)}) async-start(bf16[8,192,256]{2,1,0:T(8,128)(2,1)} %copy-done.1), calls=%async_computation.1 | async-start | bytes 1572864 | tf_op jit(solution)/shard_map/all_to_all | solution.py:280
  127.4 4.3 %collective-permute-start.2 = (bf16[192,1792]{1,0:T(8,128)(2,1)S(1)}, bf16[192,1792]{1,0:T(8,128)(2,1)S(1)}, u32[]{:S(2)}, u32[]{:S(2)}) collective-permute-start(bf16[192,1792]{1,0:T(8,128)(2,1)S(1)} %all_gather.6.pair_ref), channel_id=1, source_target_pairs={{0,64},{64,0},{128,192},{192,128},{256,320},{320,256},{384,448},{4... | collective-permute-start | bytes 2064392 | tf_op jit(solution)/shard_map/ppermute | solution.py:274
  131.8 0.0 copy-start
  131.8 1.2 copy-done
  133.0 0.7 shard_map.71.own_ref
  133.7 7.0 %collective-permute-done.2.pair_ref = bf16[192,1792]{1,0:T(8,128)(2,1)S(1)} collective-permute-done((bf16[192,1792]{1,0:T(8,128)(2,1)S(1)}, bf16[192,1792]{1,0:T(8,128)(2,1)S(1)}, u32[]{:S(2)}, u32[]{:S(2)}) %collective-permute-start.2) | collective-permute-done | bytes 688160 | tf_op jit(solution)/shard_map/ppermute | solution.py:274
  140.7 1.4 shard_map.72
  142.1 0.0 all-gather.2.cloned.1.call-done
  142.1 3.2 %copy.9 = bf16[1536,1024]{0,1:T(8,128)(2,1)S(1)} copy(bf16[1536,1024]{1,0:T(8,128)(2,1)} %all-gather.2.cloned.1.call-done) | data formatting | bytes 6291456 | tf_op jit(solution)/shard_map/all_gather | solution.py:257
  145.3 0.0 all-to-all-done.1
  145.3 1.7 shard_map.74
  147.0 3.9 %collective-permute-start.3 = (bf16[512,256]{1,0:T(8,128)(2,1)S(1)}, bf16[512,256]{1,0:T(8,128)(2,1)}, u32[]{:S(2)}, u32[]{:S(2)}) collective-permute-start(bf16[512,256]{1,0:T(8,128)(2,1)S(1)} %shard_map.74), channel_id=1, source_target_pairs={{0,64},{64,0},{128,192},{192,128},{256,320},{320,256},{384,448},{4... | collective-permute-start | bytes 786440 | tf_op jit(solution)/shard_map/ppermute | solution.py:285
  151.0 6.4 %all-to-all-start.2 = ((bf16[8,64,192]{2,1,0:T(8,128)(2,1)}), bf16[8,64,192]{2,1,0:T(8,128)(2,1)}, u32[]{:S(2)}, u32[]{:S(2)}) async-start(bf16[8,64,192]{2,1,0:T(8,128)(2,1)} %bitcast.4), calls=%async_computation.2 | async-start | bytes 524288 | tf_op jit(solution)/shard_map/all_to_all | solution.py:287
  157.4 1.7 shard_map.73
  159.1 0.0 collective-permute-done.3
  159.1 1.8 pad_maximum_fusion
  160.9 8.1 %all-to-all-done.2 = bf16[8,64,192]{2,1,0:T(8,128)(2,1)} async-done(((bf16[8,64,192]{2,1,0:T(8,128)(2,1)}), bf16[8,64,192]{2,1,0:T(8,128)(2,1)}, u32[]{:S(2)}, u32[]{:S(2)}) %all-to-all-start.2) | async-done | bytes 196640 | tf_op jit(solution)/shard_map/all_to_all | solution.py:287
  169.0 6.2 %all-to-all-start.3 = ((bf16[8,64,512]{2,1,0:T(8,128)(2,1)}), bf16[8,64,512]{2,1,0:T(8,128)(2,1)S(1)}, u32[]{:S(2)}, u32[]{:S(2)}) async-start(bf16[8,64,512]{2,1,0:T(8,128)(2,1)} %bitcast.6), calls=%async_computation.3 | async-start | bytes 1048576 | tf_op jit(solution)/shard_map/all_to_all | solution.py:293
  175.2 1.6 reduce_sum.12
  176.8 7.0 %all-to-all-done.3.swapped_ref = bf16[8,64,512]{2,1,0:T(8,128)(2,1)S(1)} async-done(((bf16[8,64,512]{2,1,0:T(8,128)(2,1)}), bf16[8,64,512]{2,1,0:T(8,128)(2,1)S(1)}, u32[]{:S(2)}, u32[]{:S(2)}) %all-to-all-start.3) | async-done | bytes 524320 | tf_op jit(solution)/shard_map/all_to_all | solution.py:293
  183.8 0.8 shard_map.75
Async XLA Ops:
  7.2 135.0 %all-gather.2.cloned.1.call-start = ((), (), s32[]{:S(2)}) async-start(), calls=%async_computation.4 | async-start | bytes 3538944 | tf_op jit(solution)/shard_map/all_gather | solution.py:257
  10.1 7.3 %copy-start.2 = (bf16[192,512]{1,0:T(8,128)(2,1)S(1)}, bf16[192,512]{1,0:T(8,128)(2,1)}, u32[]{:S(2)}) copy-start(bf16[192,512]{1,0:T(8,128)(2,1)} %tokens_hbm.3) | copy-start | bytes 589828
  10.1 20.9 %collective-permute-start = (bf16[192,1792]{1,0:T(8,128)(2,1)}, bf16[192,1792]{1,0:T(8,128)(2,1)S(1)}, u32[]{:S(2)}, u32[]{:S(2)}) collective-permute-start(bf16[192,1792]{1,0:T(8,128)(2,1)} %shard_map.67), channel_id=1, source_target_pairs={{0,64},{64,0},{128,192},{192,128},{256,320},{320,256},{384,448},{4... | collective-permute-start | bytes 2064392 | tf_op jit(solution)/shard_map/ppermute | solution.py:254
  17.4 16.9 %collective-permute-start.1 = (bf16[192,512]{1,0:T(8,128)(2,1)S(1)}, bf16[192,512]{1,0:T(8,128)(2,1)S(1)}, u32[]{:S(2)}, u32[]{:S(2)}) collective-permute-start(bf16[192,512]{1,0:T(8,128)(2,1)S(1)} %copy-done.2), channel_id=1, source_target_pairs={{0,64},{64,0},{128,192},{192,128},{256,320},{320,256},{384,448},{4... | collective-permute-start | bytes 589832 | tf_op jit(solution)/shard_map/ppermute | solution.py:253
  35.2 48.5 %all-to-all-start = ((bf16[8,24,1792]{2,1,0:T(8,128)(2,1)}), bf16[8,24,1792]{2,1,0:T(8,128)(2,1)S(1)}, u32[]{:S(2)}, u32[]{:S(2)}) async-start(bf16[8,24,1792]{2,1,0:T(8,128)(2,1)} %bitcast.1), calls=%async_computation | async-start | bytes 1376256 | tf_op jit(solution)/shard_map/all_to_all | solution.py:258
  121.2 0.9 copy-start.1
  122.2 23.2 %all-to-all-start.1 = ((bf16[8,192,256]{2,1,0:T(8,128)(2,1)}), bf16[8,192,256]{2,1,0:T(8,128)(2,1)}, u32[]{:S(2)}, u32[]{:S(2)}) async-start(bf16[8,192,256]{2,1,0:T(8,128)(2,1)} %copy-done.1), calls=%async_computation.1 | async-start | bytes 1572864 | tf_op jit(solution)/shard_map/all_to_all | solution.py:280
  127.4 13.2 %collective-permute-start.2 = (bf16[192,1792]{1,0:T(8,128)(2,1)S(1)}, bf16[192,1792]{1,0:T(8,128)(2,1)S(1)}, u32[]{:S(2)}, u32[]{:S(2)}) collective-permute-start(bf16[192,1792]{1,0:T(8,128)(2,1)S(1)} %all_gather.6.pair_ref), channel_id=1, source_target_pairs={{0,64},{64,0},{128,192},{192,128},{256,320},{320,256},{384,448},{4... | collective-permute-start | bytes 2064392 | tf_op jit(solution)/shard_map/ppermute | solution.py:274
  131.8 1.2 copy-start
  147.0 12.1 %collective-permute-start.3 = (bf16[512,256]{1,0:T(8,128)(2,1)S(1)}, bf16[512,256]{1,0:T(8,128)(2,1)}, u32[]{:S(2)}, u32[]{:S(2)}) collective-permute-start(bf16[512,256]{1,0:T(8,128)(2,1)S(1)} %shard_map.74), channel_id=1, source_target_pairs={{0,64},{64,0},{128,192},{192,128},{256,320},{320,256},{384,448},{4... | collective-permute-start | bytes 786440 | tf_op jit(solution)/shard_map/ppermute | solution.py:285
  151.0 18.0 %all-to-all-start.2 = ((bf16[8,64,192]{2,1,0:T(8,128)(2,1)}), bf16[8,64,192]{2,1,0:T(8,128)(2,1)}, u32[]{:S(2)}, u32[]{:S(2)}) async-start(bf16[8,64,192]{2,1,0:T(8,128)(2,1)} %bitcast.4), calls=%async_computation.2 | async-start | bytes 524288 | tf_op jit(solution)/shard_map/all_to_all | solution.py:287
  169.0 14.8 %all-to-all-start.3 = ((bf16[8,64,512]{2,1,0:T(8,128)(2,1)}), bf16[8,64,512]{2,1,0:T(8,128)(2,1)S(1)}, u32[]{:S(2)}, u32[]{:S(2)}) async-start(bf16[8,64,512]{2,1,0:T(8,128)(2,1)} %bitcast.6), calls=%async_computation.3 | async-start | bytes 1048576 | tf_op jit(solution)/shard_map/all_to_all | solution.py:293
Sparse Core Ops, SparseCore 0:
  35.3 60.8 all-gather.1

commit v7 on v6

--- a/solution.py
+++ b/solution.py
@@ -177,27 +177,62 @@
     )(gate, up, pair, own)
 
 
-def weight_kernel(which, factor, tokens_ref, block_ref, out_ref):
-    rows = out_ref.shape[0]
-    total = lax.dot_general(
-        tokens_ref[which * rows : (which + 1) * rows, :],
-        block_ref[...],
-        ROWS_BY_COLS,
-        preferred_element_type=F32,
-    )
-    out_ref[...] = (total * factor).astype(BF16)
+def across_kernel(mine_ref, theirs_ref, out_ref):
+    rows = mine_ref.shape[1]
+    out_ref[:rows, :] = mine_ref[...].astype(F32).T.astype(BF16)
+    out_ref[rows:, :] = theirs_ref[...].astype(F32).T.astype(BF16)
+
+
+def features_by_tokens(mine, theirs):
+    token_count, feature_count = mine.shape
+    return pl.pallas_call(
+        across_kernel,
+        out_shape=jax.ShapeDtypeStruct((2 * feature_count, token_count), BF16),
+        compiler_params=PARAMS,
+        cost_estimate=pl.CostEstimate(flops=0, bytes_accessed=8 * mine.size, transcendentals=0),
+    )(mine, theirs)
+
+
+def weight_kernel(factor, tokens_ref, block_ref, out_ref, total_ref):
+    step = pl.program_id(0)
+    term = lax.dot_general(
+        tokens_ref[0], block_ref[0], ROWS_BY_COLS, preferred_element_type=F32
+    )
+    for more in range(1, tokens_ref.shape[0]):
+        term = term + lax.dot_general(
+            tokens_ref[more], block_ref[more], ROWS_BY_COLS, preferred_element_type=F32
+        )
+
+    @pl.when(step == 0)
+    def _():
+        total_ref[...] = term
+
+    @pl.when(step > 0)
+    def _():
+        total_ref[...] += term
+
+    @pl.when(step == pl.num_programs(0) - 1)
+    def _():
+        out_ref[...] = (total_ref[...] * factor).astype(BF16)
 
 
 def weight_terms(tokens, which, block, factor):
-    feature_count = tokens.shape[0] // 2
-    token_count, width = block.shape
-    return pl.pallas_call(
-        functools.partial(weight_kernel, which, factor),
+    dep, token_count, width = block.shape
+    feature_count = tokens.shape[1] // 2
+    return pl.pallas_call(
+        functools.partial(weight_kernel, factor),
         out_shape=jax.ShapeDtypeStruct((feature_count, width), BF16),
-        compiler_params=PARAMS,
-        cost_estimate=pl.CostEstimate(
-            flops=2 * token_count * feature_count * width,
-            bytes_accessed=2 * token_count * (feature_count + width),
+        grid=(dep // 2,),
+        in_specs=[
+            pl.BlockSpec((2, feature_count, token_count), lambda d: (d, which, 0)),
+            pl.BlockSpec((2, token_count, width), lambda d: (d, 0, 0)),
+        ],
+        out_specs=pl.BlockSpec((feature_count, width), lambda d: (0, 0)),
+        scratch_shapes=[pltpu.VMEM((feature_count, width), F32)],
+        compiler_params=WHOLE,
+        cost_estimate=pl.CostEstimate(
+            flops=2 * dep * token_count * feature_count * width,
+            bytes_accessed=2 * dep * token_count * (feature_count + width),
             transcendentals=0,
         ),
     )(tokens, block)
@@ -253,8 +288,7 @@
     theirs = lax.ppermute(mine, "inp", pairs)
     kept = kept.astype(F32) + lax.ppermute(given, "inp", pairs).astype(F32)
     kept, w_gate, w_up, theirs = lax.optimization_barrier((kept.astype(BF16), w_gate, w_up, theirs))
-    two = jnp.concatenate([tokens, theirs], axis=1)
-    all_tokens = lax.all_gather(two, "dep", axis=0, tiled=True)
+    across = lax.all_gather(features_by_tokens(tokens, theirs), "dep", axis=0)
     terms = lax.all_to_all(
         kept.reshape(group, rows, hidden), "inp", 0, 0, axis_index_groups=alike
     )
@@ -278,10 +312,9 @@
     starts = [min(b * width, half - width) for b in range(blocks)]
     skips = [b * width - s for b, s in enumerate(starts)]
     own_block = lax.all_to_all(dep_pieces(own, starts, width), "dep", 0, 0)
-    own_block = own_block.reshape(dep * token_count, width)
     own_share = own_input_terms(*own_weights, own)
     shares = other_input_terms(*other_weights, other, own_share)
-    own_block, across, shares = lax.optimization_barrier((own_block, all_tokens.T, shares))
+    own_block, shares = lax.optimization_barrier((own_block, shares))
     other_grad = lax.ppermute(weight_terms(across, 1, own_block, factor), "inp", pairs)
     own_grad = weight_terms(across, 0, own_block, factor)
     shares = lax.all_to_all(

time: 192 us -> 191 us (level)
  Pallas kernels: 12.3 us -> 17.9 us
  local copies, waits for them, and re-layouts: 9.29 us -> 6.08 us
    pallas_call x2 -> x3, Pallas kernels: 3.41 us -> 9.02 us  [the longest x2 8.01 us: weight_terms(): pl.pallas_call(functools.partial(weight_kernel, factor), out_shape=jax.Sh...]
    all_gather x1 -> x0, local copies, waits for them, and re-layouts: 3.18 us -> none  [shards(): all_tokens = lax.all_gather(two, 'dep', axis=0, tiled=True)]
    all_to_all x1, waiting for transfers between devices: 8.06 us -> 5.63 us  [shards(): lax.all_to_all(shares.reshape(out, feature_count // out, token_count), 'o...]
  transfers between devices with their start and end apart: 9 -> 9, of which waited for: 6 -> 6; matrix products, arithmetic and copies ran while one was open for 7% -> 5% of each run, Pallas kernels for 4% -> 5%
where the time goes in v7:
time: 191 us; the launch traced here: 190 us
  waiting for transfers between devices  59.9 us (31%)
  starting transfers between devices  50.6 us (26%)
  blocking collectives  37.2 us (19%)
  Pallas kernels  17.9 us (9%)
  between operations  14.1 us (7%)
  local copies, waits for them, and re-layouts  6.08 us (3%)
  other arithmetic  4.59 us (2%)
    all_gather x1, blocking collectives, shards(): lax.all_gather(grad_pair(terms, cotangent), 'inp', axis=0, tiled=True, ax...  37.2 us
    all_to_all x1, waiting for transfers between devices, shards(): lax.all_to_all(kept.reshape(group, rows, hidden), 'inp', 0, 0, axis_index...  26.4 us
    all_to_all x1, starting transfers between devices, shards(): lax.all_to_all(kept.reshape(group, rows, hidden), 'inp', 0, 0, axis_index...  18.1 us
    ppermute x1, waiting for transfers between devices, shards(): kept = kept.astype(F32) + lax.ppermute(given, 'inp', pairs).astype(F32)  11.6 us
    pallas_call x2, Pallas kernels, weight_terms(): pl.pallas_call(functools.partial(weight_kernel, factor), out_shape=jax.Sh...  8.01 us
    all_to_all x1, waiting for transfers between devices, shards(): lax.all_to_all(grad.reshape(dep, feature_count // dep, 2 * width), 'dep',...  7.97 us
    ppermute x1, waiting for transfers between devices, shards(): other = lax.ppermute(own, 'inp', pairs)  6.99 us
    all_to_all x1, starting transfers between devices, shards(): lax.all_to_all(shares.reshape(out, feature_count // out, token_count), 'o...  6.38 us
  transfers between devices with their start and end apart: 9, of which 6 were waited for; matrix products, arithmetic and copies ran while one was open for 5% of the time, Pallas kernels for 5%

profile of v7, /device:TPU:8, one launch (start us, length us, event | category | flops | bytes accessed | tf_op | source)
XLA Modules:
  0.0 190.3 jit_solution(17228423156163790499)
XLA Ops:
  7.2 0.0 all-gather.3.cloned.1.call-start
  7.2 2.8 %shard_map.67 = bf16[192,1792]{1,0:T(8,128)(2,1)} custom-call(s32[1]{0:T(128)S(6)} %sub.10.side_ref, bf16[192,512]{1,0:T(8,128)(2,1)} %mine_ref.1, bf16[512,1792]{1,0:T(8,128)(2,1)} %gate_hbm.3, bf16[512,1792]{1,0:T(8,128)(2,1)} %up_hbm.3), custom_call_target="tpu_custom_call" | custom-call | flops 352321536 | bytes 2523136 | tf_op jit(solution)/shard_map/pallas_call | solution.py:57
  10.1 0.0 copy-start.2
  10.1 4.4 %collective-permute-start = (bf16[192,1792]{1,0:T(8,128)(2,1)}, bf16[192,1792]{1,0:T(8,128)(2,1)S(1)}, u32[]{:S(2)}, u32[]{:S(2)}) collective-permute-start(bf16[192,1792]{1,0:T(8,128)(2,1)} %shard_map.67), channel_id=1, source_target_pairs={{0,64},{64,0},{128,192},{192,128},{256,320},{320,256},{384,448},{4... | collective-permute-start | bytes 2064392 | tf_op jit(solution)/shard_map/ppermute | solution.py:289
  14.5 2.9 %shard_map.68 = bf16[192,1792]{1,0:T(8,128)(2,1)} custom-call(s32[1]{0:T(128)} %bitcast.side_ref, bf16[192,512]{1,0:T(8,128)(2,1)} %mine_ref.1, bf16[512,1792]{1,0:T(8,128)(2,1)} %gate_hbm.3, bf16[512,1792]{1,0:T(8,128)(2,1)} %up_hbm.3), custom_call_target="tpu_custom_call" | custom-call | flops 352321536 | bytes 2523136 | tf_op jit(solution)/shard_map/pallas_call | solution.py:57
  17.4 0.0 copy-done.2
  17.4 1.9 %collective-permute-start.1 = (bf16[192,512]{1,0:T(8,128)(2,1)S(1)}, bf16[192,512]{1,0:T(8,128)(2,1)S(1)}, u32[]{:S(2)}, u32[]{:S(2)}) collective-permute-start(bf16[192,512]{1,0:T(8,128)(2,1)S(1)} %copy-done.2), channel_id=1, source_target_pairs={{0,64},{64,0},{128,192},{192,128},{256,320},{320,256},{384,448},{4... | collective-permute-start | bytes 589832 | tf_op jit(solution)/shard_map/ppermute | solution.py:288
  19.3 11.6 %collective-permute-done = bf16[192,1792]{1,0:T(8,128)(2,1)S(1)} collective-permute-done((bf16[192,1792]{1,0:T(8,128)(2,1)}, bf16[192,1792]{1,0:T(8,128)(2,1)S(1)}, u32[]{:S(2)}, u32[]{:S(2)}) %collective-permute-start) | collective-permute-done | bytes 688160 | tf_op jit(solution)/shard_map/ppermute | solution.py:289
  31.0 2.2 %add_convert_fusion = bf16[192,1792]{1,0:T(8,128)(2,1)} fusion(bf16[192,1792]{1,0:T(8,128)(2,1)S(1)} %collective-permute-done, bf16[192,1792]{1,0:T(8,128)(2,1)} %shard_map.68), kind=kLoop, calls=%fused_computation | loop fusion | flops 1376256 | bytes 2064384 | tf_op jit(solution)/shard_map/convert_element_type | solution.py:290
  33.1 1.2 collective-permute-done.1.theirs_ref
  34.3 1.0 shard_map.73
  35.4 0.0 all-gather.3.cloned.1.call-update
  35.4 18.1 %all-to-all-start = ((bf16[8,24,1792]{2,1,0:T(8,128)(2,1)}), bf16[8,24,1792]{2,1,0:T(8,128)(2,1)S(1)}, u32[]{:S(2)}, u32[]{:S(2)}) async-start(bf16[8,24,1792]{2,1,0:T(8,128)(2,1)} %bitcast.1), calls=%async_computation | async-start | bytes 1376256 | tf_op jit(solution)/shard_map/all_to_all | solution.py:292
  53.5 0.8 dynamic_slice.19.cotangent_ref
  54.3 3.2 %constant_dynamic-slice_fusion = (bf16[512,896]{1,0:T(8,128)(2,1)S(1)}, bf16[512,896]{1,0:T(8,128)(2,1)S(1)}, bf16[512,896]{1,0:T(8,128)(2,1)}, bf16[512,896]{1,0:T(8,128)(2,1)S(1)}) fusion(bf16[512,1792]{1,0:T(8,128)(2,1)} %up_hbm.3, s32[]{:T(128)S(6)} %select_n.25, s32[]{:T(128)S(6)} %select_n.24, bf16[512,1792]{1,0:T(8,128)(2,1)} %gate_hbm.3), kind=kLoop, calls=%fused_computation.2 | loop fusion | bytes 7340040 | tf_op jit(solution)/shard_map/dynamic_slice | solution.py:299
  57.5 26.4 %all-to-all-done.terms_ref = bf16[8,24,1792]{2,1,0:T(8,128)(2,1)S(1)} async-done(((bf16[8,24,1792]{2,1,0:T(8,128)(2,1)}), bf16[8,24,1792]{2,1,0:T(8,128)(2,1)S(1)}, u32[]{:S(2)}, u32[]{:S(2)}) %all-to-all-start) | async-done | bytes 688160 | tf_op jit(solution)/shard_map/all_to_all | solution.py:292
  83.9 0.1 shard_map.69
  84.0 37.2 %all_gather.9.pair_ref = bf16[192,1792]{1,0:T(8,128)(2,1)S(1)} all-gather(bf16[24,1792]{1,0:T(8,128)(2,1)S(1)} %shard_map.69), channel_id=1, replica_groups={{0,128,256,384,512,640,768,896},{64,192,320,448,576,704,832,960},{1,129..., dimensions={0}, use_global_device_ids=true | all-gather | bytes 774144 | tf_op jit(solution)/shard_map/all_gather | solution.py:305
  121.2 0.1 shard_map.70
  121.3 0.0 copy-start.1
  121.3 0.9 copy-done.1
  122.2 5.5 %all-to-all-start.1 = ((bf16[8,192,256]{2,1,0:T(8,128)(2,1)}), bf16[8,192,256]{2,1,0:T(8,128)(2,1)}, u32[]{:S(2)}, u32[]{:S(2)}) async-start(bf16[8,192,256]{2,1,0:T(8,128)(2,1)} %copy-done.1), calls=%async_computation.1 | async-start | bytes 1572864 | tf_op jit(solution)/shard_map/all_to_all | solution.py:314
  127.7 4.1 %collective-permute-start.2 = (bf16[192,1792]{1,0:T(8,128)(2,1)S(1)}, bf16[192,1792]{1,0:T(8,128)(2,1)S(1)}, u32[]{:S(2)}, u32[]{:S(2)}) collective-permute-start(bf16[192,1792]{1,0:T(8,128)(2,1)S(1)} %all_gather.9.pair_ref), channel_id=1, source_target_pairs={{0,64},{64,0},{128,192},{192,128},{256,320},{320,256},{384,448},{4... | collective-permute-start | bytes 2064392 | tf_op jit(solution)/shard_map/ppermute | solution.py:308
  131.7 0.0 copy-start
  131.7 1.2 copy-done
  132.9 0.7 shard_map.71.own_ref
  133.6 7.0 %collective-permute-done.2.pair_ref = bf16[192,1792]{1,0:T(8,128)(2,1)S(1)} collective-permute-done((bf16[192,1792]{1,0:T(8,128)(2,1)S(1)}, bf16[192,1792]{1,0:T(8,128)(2,1)S(1)}, u32[]{:S(2)}, u32[]{:S(2)}) %collective-permute-start.2) | collective-permute-done | bytes 688160 | tf_op jit(solution)/shard_map/ppermute | solution.py:308
  140.6 1.4 shard_map.72
  142.1 0.0 all-to-all-done.1.block_ref
  142.1 0.0 all-gather.3.cloned.1.call-done
  142.1 4.0 %shard_map.75 = bf16[512,256]{1,0:T(8,128)(2,1)} custom-call(bf16[8,1024,192]{2,1,0:T(8,128)(2,1)} %bitcast.6, bf16[8,192,256]{2,1,0:T(8,128)(2,1)} %all-to-all-done.1.block_ref), custom_call_target="tpu_custom_call" | custom-call | flops 402653184 | bytes 2359296 | tf_op jit(solution)/shard_map/pallas_call | solution.py:222
  146.1 3.9 %collective-permute-start.3 = (bf16[512,256]{1,0:T(8,128)(2,1)}, bf16[512,256]{1,0:T(8,128)(2,1)S(1)}, u32[]{:S(2)}, u32[]{:S(2)}) collective-permute-start(bf16[512,256]{1,0:T(8,128)(2,1)} %shard_map.75), channel_id=1, source_target_pairs={{0,64},{64,0},{128,192},{192,128},{256,320},{320,256},{384,448},{4... | collective-permute-start | bytes 786440 | tf_op jit(solution)/shard_map/ppermute | solution.py:318
  150.0 6.4 %all-to-all-start.2 = ((bf16[8,64,192]{2,1,0:T(8,128)(2,1)}), bf16[8,64,192]{2,1,0:T(8,128)(2,1)S(1)}, u32[]{:S(2)}, u32[]{:S(2)}) async-start(bf16[8,64,192]{2,1,0:T(8,128)(2,1)} %bitcast.2), calls=%async_computation.2 | async-start | bytes 524288 | tf_op jit(solution)/shard_map/all_to_all | solution.py:320
  156.4 4.0 %shard_map.74 = bf16[512,256]{1,0:T(8,128)(2,1)} custom-call(bf16[8,1024,192]{2,1,0:T(8,128)(2,1)} %bitcast.7, bf16[8,192,256]{2,1,0:T(8,128)(2,1)} %all-to-all-done.1.block_ref), custom_call_target="tpu_custom_call" | custom-call | flops 402653184 | bytes 2359296 | tf_op jit(solution)/shard_map/pallas_call | solution.py:222
  160.4 0.0 collective-permute-done.3
  160.4 1.8 pad_maximum_fusion
  162.2 5.6 %all-to-all-done.2 = bf16[8,64,192]{2,1,0:T(8,128)(2,1)S(1)} async-done(((bf16[8,64,192]{2,1,0:T(8,128)(2,1)}), bf16[8,64,192]{2,1,0:T(8,128)(2,1)S(1)}, u32[]{:S(2)}, u32[]{:S(2)}) %all-to-all-start.2) | async-done | bytes 196640 | tf_op jit(solution)/shard_map/all_to_all | solution.py:320
  167.8 6.2 %all-to-all-start.3 = ((bf16[8,64,512]{2,1,0:T(8,128)(2,1)}), bf16[8,64,512]{2,1,0:T(8,128)(2,1)S(1)}, u32[]{:S(2)}, u32[]{:S(2)}) async-start(bf16[8,64,512]{2,1,0:T(8,128)(2,1)} %bitcast.5), calls=%async_computation.3 | async-start | bytes 1048576 | tf_op jit(solution)/shard_map/all_to_all | solution.py:326
  174.0 0.7 reduce_sum.12
  174.7 8.0 %all-to-all-done.3.swapped_ref = bf16[8,64,512]{2,1,0:T(8,128)(2,1)S(1)} async-done(((bf16[8,64,512]{2,1,0:T(8,128)(2,1)}), bf16[8,64,512]{2,1,0:T(8,128)(2,1)S(1)}, u32[]{:S(2)}, u32[]{:S(2)}) %all-to-all-start.3) | async-done | bytes 524320 | tf_op jit(solution)/shard_map/all_to_all | solution.py:326
  182.7 0.8 shard_map.76
Async XLA Ops:
  7.2 134.9 %all-gather.3.cloned.1.call-start = ((), (), s32[]{:S(2)}) async-start(), calls=%async_computation.4 | async-start | bytes 4718592 | tf_op jit(solution)/shard_map/all_gather | solution.py:291
  10.1 7.3 %copy-start.2 = (bf16[192,512]{1,0:T(8,128)(2,1)S(1)}, bf16[192,512]{1,0:T(8,128)(2,1)}, u32[]{:S(2)}) copy-start(bf16[192,512]{1,0:T(8,128)(2,1)} %mine_ref.1) | copy-start | bytes 589828
  10.1 20.9 %collective-permute-start = (bf16[192,1792]{1,0:T(8,128)(2,1)}, bf16[192,1792]{1,0:T(8,128)(2,1)S(1)}, u32[]{:S(2)}, u32[]{:S(2)}) collective-permute-start(bf16[192,1792]{1,0:T(8,128)(2,1)} %shard_map.67), channel_id=1, source_target_pairs={{0,64},{64,0},{128,192},{192,128},{256,320},{320,256},{384,448},{4... | collective-permute-start | bytes 2064392 | tf_op jit(solution)/shard_map/ppermute | solution.py:289
  17.4 17.0 %collective-permute-start.1 = (bf16[192,512]{1,0:T(8,128)(2,1)S(1)}, bf16[192,512]{1,0:T(8,128)(2,1)S(1)}, u32[]{:S(2)}, u32[]{:S(2)}) collective-permute-start(bf16[192,512]{1,0:T(8,128)(2,1)S(1)} %copy-done.2), channel_id=1, source_target_pairs={{0,64},{64,0},{128,192},{192,128},{256,320},{320,256},{384,448},{4... | collective-permute-start | bytes 589832 | tf_op jit(solution)/shard_map/ppermute | solution.py:288
  35.4 48.5 %all-to-all-start = ((bf16[8,24,1792]{2,1,0:T(8,128)(2,1)}), bf16[8,24,1792]{2,1,0:T(8,128)(2,1)S(1)}, u32[]{:S(2)}, u32[]{:S(2)}) async-start(bf16[8,24,1792]{2,1,0:T(8,128)(2,1)} %bitcast.1), calls=%async_computation | async-start | bytes 1376256 | tf_op jit(solution)/shard_map/all_to_all | solution.py:292
  121.3 0.9 copy-start.1
  122.2 19.9 %all-to-all-start.1 = ((bf16[8,192,256]{2,1,0:T(8,128)(2,1)}), bf16[8,192,256]{2,1,0:T(8,128)(2,1)}, u32[]{:S(2)}, u32[]{:S(2)}) async-start(bf16[8,192,256]{2,1,0:T(8,128)(2,1)} %copy-done.1), calls=%async_computation.1 | async-start | bytes 1572864 | tf_op jit(solution)/shard_map/all_to_all | solution.py:314
  127.7 13.0 %collective-permute-start.2 = (bf16[192,1792]{1,0:T(8,128)(2,1)S(1)}, bf16[192,1792]{1,0:T(8,128)(2,1)S(1)}, u32[]{:S(2)}, u32[]{:S(2)}) collective-permute-start(bf16[192,1792]{1,0:T(8,128)(2,1)S(1)} %all_gather.9.pair_ref), channel_id=1, source_target_pairs={{0,64},{64,0},{128,192},{192,128},{256,320},{320,256},{384,448},{4... | collective-permute-start | bytes 2064392 | tf_op jit(solution)/shard_map/ppermute | solution.py:308
  131.7 1.2 copy-start
  146.1 14.3 %collective-permute-start.3 = (bf16[512,256]{1,0:T(8,128)(2,1)}, bf16[512,256]{1,0:T(8,128)(2,1)S(1)}, u32[]{:S(2)}, u32[]{:S(2)}) collective-permute-start(bf16[512,256]{1,0:T(8,128)(2,1)} %shard_map.75), channel_id=1, source_target_pairs={{0,64},{64,0},{128,192},{192,128},{256,320},{320,256},{384,448},{4... | collective-permute-start | bytes 786440 | tf_op jit(solution)/shard_map/ppermute | solution.py:318
  150.0 17.8 %all-to-all-start.2 = ((bf16[8,64,192]{2,1,0:T(8,128)(2,1)}), bf16[8,64,192]{2,1,0:T(8,128)(2,1)S(1)}, u32[]{:S(2)}, u32[]{:S(2)}) async-start(bf16[8,64,192]{2,1,0:T(8,128)(2,1)} %bitcast.2), calls=%async_computation.2 | async-start | bytes 524288 | tf_op jit(solution)/shard_map/all_to_all | solution.py:320
  167.8 14.9 %all-to-all-start.3 = ((bf16[8,64,512]{2,1,0:T(8,128)(2,1)}), bf16[8,64,512]{2,1,0:T(8,128)(2,1)S(1)}, u32[]{:S(2)}, u32[]{:S(2)}) async-start(bf16[8,64,512]{2,1,0:T(8,128)(2,1)} %bitcast.5), calls=%async_computation.3 | async-start | bytes 1048576 | tf_op jit(solution)/shard_map/all_to_all | solution.py:326
Sparse Core Ops, SparseCore 0:
  35.5 69.3 all-gather.2

commit v8 on v7

--- a/solution.py
+++ b/solution.py
@@ -177,65 +177,72 @@
     )(gate, up, pair, own)
 
 
-def across_kernel(mine_ref, theirs_ref, out_ref):
-    rows = mine_ref.shape[1]
-    out_ref[:rows, :] = mine_ref[...].astype(F32).T.astype(BF16)
-    out_ref[rows:, :] = theirs_ref[...].astype(F32).T.astype(BF16)
-
-
-def features_by_tokens(mine, theirs):
-    token_count, feature_count = mine.shape
+def across_kernel(tokens_ref, out_ref):
+    out_ref[...] = tokens_ref[...].astype(F32).T.astype(BF16)
+
+
+def features_by_tokens(tokens):
     return pl.pallas_call(
         across_kernel,
-        out_shape=jax.ShapeDtypeStruct((2 * feature_count, token_count), BF16),
-        compiler_params=PARAMS,
-        cost_estimate=pl.CostEstimate(flops=0, bytes_accessed=8 * mine.size, transcendentals=0),
-    )(mine, theirs)
-
-
-def weight_kernel(factor, tokens_ref, block_ref, out_ref, total_ref):
+        out_shape=jax.ShapeDtypeStruct(tokens.shape[::-1], BF16),
+        compiler_params=PARAMS,
+        cost_estimate=pl.CostEstimate(flops=0, bytes_accessed=4 * tokens.size, transcendentals=0),
+    )(tokens)
+
+
+def weight_kernel(factor, tokens_ref, own_ref, other_ref, out_ref, total_ref):
     step = pl.program_id(0)
-    term = lax.dot_general(
-        tokens_ref[0], block_ref[0], ROWS_BY_COLS, preferred_element_type=F32
-    )
-    for more in range(1, tokens_ref.shape[0]):
-        term = term + lax.dot_general(
-            tokens_ref[more], block_ref[more], ROWS_BY_COLS, preferred_element_type=F32
+    terms = []
+    for block_ref in (own_ref, other_ref):
+        terms.append(
+            sum(
+                lax.dot_general(
+                    tokens_ref[k], block_ref[k], ROWS_BY_COLS, preferred_element_type=F32
+                )
+                for k in range(tokens_ref.shape[0])
+            )
         )
 
     @pl.when(step == 0)
     def _():
-        total_ref[...] = term
+        for side, term in enumerate(terms):
+            total_ref[side] = term
 
     @pl.when(step > 0)
     def _():
-        total_ref[...] += term
+        for side, term in enumerate(terms):
+            total_ref[side] += term
 
     @pl.when(step == pl.num_programs(0) - 1)
     def _():
-        out_ref[...] = (total_ref[...] * factor).astype(BF16)
-
-
-def weight_terms(tokens, which, block, factor):
-    dep, token_count, width = block.shape
-    feature_count = tokens.shape[1] // 2
+        width = total_ref.shape[2]
+        for side in range(2):
+            out_ref[:, side * width : (side + 1) * width] = (total_ref[side] * factor).astype(BF16)
+
+
+def weight_terms(tokens, own, other, factor):
+    dep, feature_count, token_count = tokens.shape
+    width = own.shape[2]
+    steps = 4
+    block = pl.BlockSpec((dep // steps, token_count, width), lambda d: (d, 0, 0))
     return pl.pallas_call(
         functools.partial(weight_kernel, factor),
-        out_shape=jax.ShapeDtypeStruct((feature_count, width), BF16),
-        grid=(dep // 2,),
+        out_shape=jax.ShapeDtypeStruct((feature_count, 2 * width), BF16),
+        grid=(steps,),
         in_specs=[
-            pl.BlockSpec((2, feature_count, token_count), lambda d: (d, which, 0)),
-            pl.BlockSpec((2, token_count, width), lambda d: (d, 0, 0)),
+            pl.BlockSpec((dep // steps, feature_count, token_count), lambda d: (d, 0, 0)),
+            block,
+            block,
         ],
-        out_specs=pl.BlockSpec((feature_count, width), lambda d: (0, 0)),
-        scratch_shapes=[pltpu.VMEM((feature_count, width), F32)],
+        out_specs=pl.BlockSpec((feature_count, 2 * width), lambda d: (0, 0)),
+        scratch_shapes=[pltpu.VMEM((2, feature_count, width), F32)],
         compiler_params=WHOLE,
         cost_estimate=pl.CostEstimate(
-            flops=2 * dep * token_count * feature_count * width,
-            bytes_accessed=2 * dep * token_count * (feature_count + width),
+            flops=4 * dep * token_count * feature_count * width,
+            bytes_accessed=2 * dep * token_count * (feature_count + 2 * width),
             transcendentals=0,
         ),
-    )(tokens, block)
+    )(tokens, own, other)
 
 
 def finish_kernel(skips, side_ref, swapped_ref, gate_ref, up_ref):
@@ -284,11 +291,11 @@
     given = partial_values(other_side, tokens, w_gate, w_up)
     own_side, given = lax.optimization_barrier((own_side, given))
     kept = partial_values(own_side, tokens, w_gate, w_up)
-    mine, kept = lax.optimization_barrier((tokens, kept))
-    theirs = lax.ppermute(mine, "inp", pairs)
     kept = kept.astype(F32) + lax.ppermute(given, "inp", pairs).astype(F32)
-    kept, w_gate, w_up, theirs = lax.optimization_barrier((kept.astype(BF16), w_gate, w_up, theirs))
-    across = lax.all_gather(features_by_tokens(tokens, theirs), "dep", axis=0)
+    kept, w_gate, w_up, tokens = lax.optimization_barrier(
+        (kept.astype(BF16), w_gate, w_up, tokens)
+    )
+    across = lax.all_gather(features_by_tokens(tokens), "dep", axis=0)
     terms = lax.all_to_all(
         kept.reshape(group, rows, hidden), "inp", 0, 0, axis_index_groups=alike
     )
@@ -313,16 +320,16 @@
     skips = [b * width - s for b, s in enumerate(starts)]
     own_block = lax.all_to_all(dep_pieces(own, starts, width), "dep", 0, 0)
     own_share = own_input_terms(*own_weights, own)
+    own_block, own_share = lax.optimization_barrier((own_block, own_share))
+    other_block = lax.ppermute(own_block, "inp", pairs)
+
     shares = other_input_terms(*other_weights, other, own_share)
-    own_block, shares = lax.optimization_barrier((own_block, shares))
-    other_grad = lax.ppermute(weight_terms(across, 1, own_block, factor), "inp", pairs)
-    own_grad = weight_terms(across, 0, own_block, factor)
     shares = lax.all_to_all(
         shares.reshape(out, feature_count // out, token_count), "out", 0, 0
     )
     grad_input = jnp.sum(shares.astype(F32), axis=0).astype(BF16).T
 
-    grad = jnp.concatenate([own_grad, other_grad], axis=1)
+    grad = weight_terms(across, own_block, other_block, factor)
     swapped = lax.all_to_all(grad.reshape(dep, feature_count // dep, 2 * width), "dep", 0, 0)
     gate_grad, up_grad = finished(own_side, swapped, half, skips)
     return grad_input, gate_grad, up_grad

time: 191 us -> 189 us (0.990)
  local copies, waits for them, and re-layouts: 6.08 us -> 8.79 us
  Pallas kernels: 17.9 us -> 15.7 us
    pallas_call x2 -> x1, Pallas kernels: 8.01 us -> 4.86 us  [weight_terms(): pl.pallas_call(functools.partial(weight_kernel, factor), out_shape=jax.Sh...]
    unnamed x6 -> x12, local copies, waits for them, and re-layouts: 2.07 us -> 4.77 us
    ppermute x2 -> x1, starting transfers between devices: 5.84 us -> 4.6 us  [shards(): other_block = lax.ppermute(own_block, 'inp', pairs)]
  transfers between devices with their start and end apart: 9 -> 8, of which waited for: 6 -> 6; matrix products, arithmetic and copies ran while one was open for 5% -> 2% of each run, Pallas kernels for 5% -> 6%
where the time goes in v8:
time: 189 us; the launch traced here: 188 us
  waiting for transfers between devices  60.9 us (32%)
  starting transfers between devices  48.9 us (26%)
  blocking collectives  36.9 us (20%)
  Pallas kernels  15.7 us (8%)
  between operations  14.2 us (8%)
  local copies, waits for them, and re-layouts  8.79 us (5%)
  other arithmetic  2.76 us (1%)
    all_gather x1, blocking collectives, shards(): lax.all_gather(grad_pair(terms, cotangent), 'inp', axis=0, tiled=True, ax...  36.9 us
    all_to_all x1, waiting for transfers between devices, shards(): lax.all_to_all(kept.reshape(group, rows, hidden), 'inp', 0, 0, axis_index...  25.6 us
    all_to_all x1, starting transfers between devices, shards(): lax.all_to_all(kept.reshape(group, rows, hidden), 'inp', 0, 0, axis_index...  18.1 us
    ppermute x1, waiting for transfers between devices, shards(): kept = kept.astype(F32) + lax.ppermute(given, 'inp', pairs).astype(F32)  12.7 us
    all_to_all x1, waiting for transfers between devices, shards(): lax.all_to_all(grad.reshape(dep, feature_count // dep, 2 * width), 'dep',...  7.97 us
    ppermute x1, waiting for transfers between devices, shards(): other = lax.ppermute(own, 'inp', pairs)  7.64 us
    all_to_all x1, starting transfers between devices, shards(): lax.all_to_all(grad.reshape(dep, feature_count // dep, 2 * width), 'dep',...  6.05 us
    all_to_all x1, starting transfers between devices, shards(): lax.all_to_all(shares.reshape(out, feature_count // out, token_count), 'o...  5.78 us
  transfers between devices with their start and end apart: 8, of which 6 were waited for; matrix products, arithmetic and copies ran while one was open for 2% of the time, Pallas kernels for 6%

profile of v8, /device:TPU:8, one launch (start us, length us, event | category | flops | bytes accessed | tf_op | source)
XLA Modules:
  0.0 188.2 jit_solution(6217317628607853037)
XLA Ops:
  7.2 2.8 %shard_map.67 = bf16[192,1792]{1,0:T(8,128)(2,1)} custom-call(s32[1]{0:T(128)S(6)} %sub.10.side_ref, bf16[192,512]{1,0:T(8,128)(2,1)} %tokens_ref, bf16[512,1792]{1,0:T(8,128)(2,1)} %gate_hbm.3, bf16[512,1792]{1,0:T(8,128)(2,1)} %up_hbm.3), custom_call_target="tpu_custom_call" | custom-call | flops 352321536 | bytes 2523136 | tf_op jit(solution)/shard_map/pallas_call | solution.py:57
  10.0 4.3 %collective-permute-start = (bf16[192,1792]{1,0:T(8,128)(2,1)}, bf16[192,1792]{1,0:T(8,128)(2,1)S(1)}, u32[]{:S(2)}, u32[]{:S(2)}) collective-permute-start(bf16[192,1792]{1,0:T(8,128)(2,1)} %shard_map.67), channel_id=1, source_target_pairs={{0,64},{64,0},{128,192},{192,128},{256,320},{320,256},{384,448},{4... | collective-permute-start | bytes 2064392 | tf_op jit(solution)/shard_map/ppermute | solution.py:294
  14.3 2.9 %shard_map.68 = bf16[192,1792]{1,0:T(8,128)(2,1)} custom-call(s32[1]{0:T(128)} %bitcast.side_ref, bf16[192,512]{1,0:T(8,128)(2,1)} %tokens_ref, bf16[512,1792]{1,0:T(8,128)(2,1)} %gate_hbm.3, bf16[512,1792]{1,0:T(8,128)(2,1)} %up_hbm.3), custom_call_target="tpu_custom_call" | custom-call | flops 352321536 | bytes 2523136 | tf_op jit(solution)/shard_map/pallas_call | solution.py:57
  17.2 0.0 copy-start.4
  17.2 12.7 %collective-permute-done = bf16[192,1792]{1,0:T(8,128)(2,1)S(1)} collective-permute-done((bf16[192,1792]{1,0:T(8,128)(2,1)}, bf16[192,1792]{1,0:T(8,128)(2,1)S(1)}, u32[]{:S(2)}, u32[]{:S(2)}) %collective-permute-start) | collective-permute-done | bytes 688160 | tf_op jit(solution)/shard_map/ppermute | solution.py:294
  30.0 2.1 %add_convert_fusion = bf16[192,1792]{1,0:T(8,128)(2,1)} fusion(bf16[192,1792]{1,0:T(8,128)(2,1)S(1)} %collective-permute-done, bf16[192,1792]{1,0:T(8,128)(2,1)} %shard_map.68), kind=kLoop, calls=%fused_computation | loop fusion | flops 1376256 | bytes 2064384 | tf_op jit(solution)/shard_map/convert_element_type | solution.py:296
  32.1 18.1 %all-to-all-start = ((bf16[8,24,1792]{2,1,0:T(8,128)(2,1)}), bf16[8,24,1792]{2,1,0:T(8,128)(2,1)S(1)}, u32[]{:S(2)}, u32[]{:S(2)}) async-start(bf16[8,24,1792]{2,1,0:T(8,128)(2,1)} %bitcast.1), calls=%async_computation | async-start | bytes 1376256 | tf_op jit(solution)/shard_map/all_to_all | solution.py:299
  50.2 0.0 all-gather.3.cloned.1.call-start
  50.2 0.0 copy-done.4
  50.2 0.8 shard_map.73
  51.1 0.0 all-gather.3.cloned.1.call-update
  51.1 0.8 dynamic_slice.19.cotangent_ref
  51.9 3.2 %constant_dynamic-slice_fusion = (bf16[512,896]{1,0:T(8,128)(2,1)S(1)}, bf16[512,896]{1,0:T(8,128)(2,1)S(1)}, bf16[512,896]{1,0:T(8,128)(2,1)}, bf16[512,896]{1,0:T(8,128)(2,1)S(1)}) fusion(bf16[512,1792]{1,0:T(8,128)(2,1)} %up_hbm.3, s32[]{:T(128)S(6)} %select_n.25, s32[]{:T(128)S(6)} %select_n.24, bf16[512,1792]{1,0:T(8,128)(2,1)} %gate_hbm.3), kind=kLoop, calls=%fused_computation.1 | loop fusion | bytes 7340040 | tf_op jit(solution)/shard_map/dynamic_slice | solution.py:306
  55.1 25.6 %all-to-all-done.terms_ref = bf16[8,24,1792]{2,1,0:T(8,128)(2,1)S(1)} async-done(((bf16[8,24,1792]{2,1,0:T(8,128)(2,1)}), bf16[8,24,1792]{2,1,0:T(8,128)(2,1)S(1)}, u32[]{:S(2)}, u32[]{:S(2)}) %all-to-all-start) | async-done | bytes 688160 | tf_op jit(solution)/shard_map/all_to_all | solution.py:299
  80.7 0.1 shard_map.69
  80.8 36.9 %all_gather.9.pair_ref = bf16[192,1792]{1,0:T(8,128)(2,1)S(1)} all-gather(bf16[24,1792]{1,0:T(8,128)(2,1)S(1)} %shard_map.69), channel_id=1, replica_groups={{0,128,256,384,512,640,768,896},{64,192,320,448,576,704,832,960},{1,129..., dimensions={0}, use_global_device_ids=true | all-gather | bytes 774144 | tf_op jit(solution)/shard_map/all_gather | solution.py:312
  117.8 0.1 shard_map.70
  117.8 0.0 copy-start.1
  117.8 0.9 copy-done.1
  118.7 5.5 %all-to-all-start.1 = ((bf16[8,192,256]{2,1,0:T(8,128)(2,1)}), bf16[8,192,256]{2,1,0:T(8,128)(2,1)}, u32[]{:S(2)}, u32[]{:S(2)}) async-start(bf16[8,192,256]{2,1,0:T(8,128)(2,1)} %copy-done.1), calls=%async_computation.1 | async-start | bytes 1572864 | tf_op jit(solution)/shard_map/all_to_all | solution.py:321
  124.1 4.6 %collective-permute-start.1 = (bf16[192,1792]{1,0:T(8,128)(2,1)S(1)}, bf16[192,1792]{1,0:T(8,128)(2,1)}, u32[]{:S(2)}, u32[]{:S(2)}) collective-permute-start(bf16[192,1792]{1,0:T(8,128)(2,1)S(1)} %all_gather.9.pair_ref), channel_id=1, source_target_pairs={{0,64},{64,0},{128,192},{192,128},{256,320},{320,256},{384,448},{4... | collective-permute-start | bytes 2064392 | tf_op jit(solution)/shard_map/ppermute | solution.py:315
  128.7 0.0 copy-start
  128.8 1.2 copy-done
  129.9 0.7 shard_map.71.own_ref
  130.7 0.0 copy-start.2
  130.7 0.8 copy-done.2
  131.5 1.4 all-to-all-done.1.own_ref
  132.9 4.6 %collective-permute-start.2 = (bf16[8,192,256]{2,1,0:T(8,128)(2,1)}, bf16[8,192,256]{2,1,0:T(8,128)(2,1)S(1)}, u32[]{:S(2)}, u32[]{:S(2)}) collective-permute-start(bf16[8,192,256]{2,1,0:T(8,128)(2,1)} %all-to-all-done.1.own_ref), channel_id=1, source_target_pairs={{0,64},{64,0},{128,192},{192,128},{256,320},{320,256},{384,448},{4... | collective-permute-start | bytes 2359304 | tf_op jit(solution)/shard_map/ppermute | solution.py:324
  137.5 7.6 %collective-permute-done.1.pair_ref = bf16[192,1792]{1,0:T(8,128)(2,1)} collective-permute-done((bf16[192,1792]{1,0:T(8,128)(2,1)S(1)}, bf16[192,1792]{1,0:T(8,128)(2,1)}, u32[]{:S(2)}, u32[]{:S(2)}) %collective-permute-start.1) | collective-permute-done | bytes 688160 | tf_op jit(solution)/shard_map/ppermute | solution.py:315
  145.1 0.0 copy-start.3
  145.1 1.0 copy-done.3
  146.2 2.5 %shard_map.72 = bf16[512,192]{1,0:T(8,128)(2,1)} custom-call(bf16[512,896]{1,0:T(8,128)(2,1)S(1)} %get-tuple-element.23.gate_ref, bf16[512,896]{1,0:T(8,128)(2,1)S(1)} %get-tuple-element.24.up_ref, bf16[192,1792]{1,0:T(8,128)(2,1)} %collective-permute-done.1.pair_ref, f32[512,192]{1,0:T(8,128)S(1)} %copy-done.3), custom_call_target="tpu_custom_call" | custom-call | flops 352321536 | bytes 2621440 | tf_op jit(solution)/shard_map/pallas_call | solution.py:172
  148.7 5.8 %all-to-all-start.2 = ((bf16[8,64,192]{2,1,0:T(8,128)(2,1)}), bf16[8,64,192]{2,1,0:T(8,128)(2,1)S(1)}, u32[]{:S(2)}, u32[]{:S(2)}) async-start(bf16[8,64,192]{2,1,0:T(8,128)(2,1)} %bitcast.2), calls=%async_computation.2 | async-start | bytes 524288 | tf_op jit(solution)/shard_map/all_to_all | solution.py:327
  154.5 0.0 all-gather.3.cloned.1.call-done
  154.5 0.0 collective-permute-done.2.other_ref
  154.5 0.0 copy-start.5
  154.5 0.9 copy-done.5
  155.4 4.9 %shard_map.74 = bf16[512,512]{1,0:T(8,128)(2,1)} custom-call(bf16[8,512,192]{2,1,0:T(8,128)(2,1)} %bitcast.6, bf16[8,192,256]{2,1,0:T(8,128)(2,1)} %all-to-all-done.1.own_ref, bf16[8,192,256]{2,1,0:T(8,128)(2,1)} %copy-done.5), custom_call_target="tpu_custom_call" | custom-call | flops 805306368 | bytes 3145728 | tf_op jit(solution)/shard_map/pallas_call | solution.py:228
  160.3 5.6 %all-to-all-done.2 = bf16[8,64,192]{2,1,0:T(8,128)(2,1)S(1)} async-done(((bf16[8,64,192]{2,1,0:T(8,128)(2,1)}), bf16[8,64,192]{2,1,0:T(8,128)(2,1)S(1)}, u32[]{:S(2)}, u32[]{:S(2)}) %all-to-all-start.2) | async-done | bytes 196640 | tf_op jit(solution)/shard_map/all_to_all | solution.py:327
  165.8 6.0 %all-to-all-start.3 = ((bf16[8,64,512]{2,1,0:T(8,128)(2,1)}), bf16[8,64,512]{2,1,0:T(8,128)(2,1)S(1)}, u32[]{:S(2)}, u32[]{:S(2)}) async-start(bf16[8,64,512]{2,1,0:T(8,128)(2,1)} %bitcast.7), calls=%async_computation.3 | async-start | bytes 1048576 | tf_op jit(solution)/shard_map/all_to_all | solution.py:333
  171.9 0.7 reduce_sum.12
  172.6 8.0 %all-to-all-done.3.swapped_ref = bf16[8,64,512]{2,1,0:T(8,128)(2,1)S(1)} async-done(((bf16[8,64,512]{2,1,0:T(8,128)(2,1)}), bf16[8,64,512]{2,1,0:T(8,128)(2,1)S(1)}, u32[]{:S(2)}, u32[]{:S(2)}) %all-to-all-start.3) | async-done | bytes 524320 | tf_op jit(solution)/shard_map/all_to_all | solution.py:333
  180.5 0.8 shard_map.75
Async XLA Ops:
  10.0 19.9 %collective-permute-start = (bf16[192,1792]{1,0:T(8,128)(2,1)}, bf16[192,1792]{1,0:T(8,128)(2,1)S(1)}, u32[]{:S(2)}, u32[]{:S(2)}) collective-permute-start(bf16[192,1792]{1,0:T(8,128)(2,1)} %shard_map.67), channel_id=1, source_target_pairs={{0,64},{64,0},{128,192},{192,128},{256,320},{320,256},{384,448},{4... | collective-permute-start | bytes 2064392 | tf_op jit(solution)/shard_map/ppermute | solution.py:294
  17.2 33.0 %copy-start.4 = (bf16[192,512]{1,0:T(8,128)(2,1)S(1)}, bf16[192,512]{1,0:T(8,128)(2,1)}, u32[]{:S(2)}) copy-start(bf16[192,512]{1,0:T(8,128)(2,1)} %tokens_ref) | copy-start | bytes 589828
  32.1 48.7 %all-to-all-start = ((bf16[8,24,1792]{2,1,0:T(8,128)(2,1)}), bf16[8,24,1792]{2,1,0:T(8,128)(2,1)S(1)}, u32[]{:S(2)}, u32[]{:S(2)}) async-start(bf16[8,24,1792]{2,1,0:T(8,128)(2,1)} %bitcast.1), calls=%async_computation | async-start | bytes 1376256 | tf_op jit(solution)/shard_map/all_to_all | solution.py:299
  50.2 104.3 %all-gather.3.cloned.1.call-start = ((), (), s32[]{:S(2)}) async-start(), calls=%async_computation.4 | async-start | bytes 2359296 | tf_op jit(solution)/shard_map/all_gather | solution.py:298
  117.8 0.9 copy-start.1
  118.7 14.2 %all-to-all-start.1 = ((bf16[8,192,256]{2,1,0:T(8,128)(2,1)}), bf16[8,192,256]{2,1,0:T(8,128)(2,1)}, u32[]{:S(2)}, u32[]{:S(2)}) async-start(bf16[8,192,256]{2,1,0:T(8,128)(2,1)} %copy-done.1), calls=%async_computation.1 | async-start | bytes 1572864 | tf_op jit(solution)/shard_map/all_to_all | solution.py:321
  124.1 21.0 %collective-permute-start.1 = (bf16[192,1792]{1,0:T(8,128)(2,1)S(1)}, bf16[192,1792]{1,0:T(8,128)(2,1)}, u32[]{:S(2)}, u32[]{:S(2)}) collective-permute-start(bf16[192,1792]{1,0:T(8,128)(2,1)S(1)} %all_gather.9.pair_ref), channel_id=1, source_target_pairs={{0,64},{64,0},{128,192},{192,128},{256,320},{320,256},{384,448},{4... | collective-permute-start | bytes 2064392 | tf_op jit(solution)/shard_map/ppermute | solution.py:315
  128.7 1.2 copy-start
  130.7 0.8 copy-start.2
  132.9 21.6 %collective-permute-start.2 = (bf16[8,192,256]{2,1,0:T(8,128)(2,1)}, bf16[8,192,256]{2,1,0:T(8,128)(2,1)S(1)}, u32[]{:S(2)}, u32[]{:S(2)}) collective-permute-start(bf16[8,192,256]{2,1,0:T(8,128)(2,1)} %all-to-all-done.1.own_ref), channel_id=1, source_target_pairs={{0,64},{64,0},{128,192},{192,128},{256,320},{320,256},{384,448},{4... | collective-permute-start | bytes 2359304 | tf_op jit(solution)/shard_map/ppermute | solution.py:324
  145.1 1.0 copy-start.3
  148.7 17.1 %all-to-all-start.2 = ((bf16[8,64,192]{2,1,0:T(8,128)(2,1)}), bf16[8,64,192]{2,1,0:T(8,128)(2,1)S(1)}, u32[]{:S(2)}, u32[]{:S(2)}) async-start(bf16[8,64,192]{2,1,0:T(8,128)(2,1)} %bitcast.2), calls=%async_computation.2 | async-start | bytes 524288 | tf_op jit(solution)/shard_map/all_to_all | solution.py:327
  154.5 0.9 copy-start.5
  165.8 14.7 %all-to-all-start.3 = ((bf16[8,64,512]{2,1,0:T(8,128)(2,1)}), bf16[8,64,512]{2,1,0:T(8,128)(2,1)S(1)}, u32[]{:S(2)}, u32[]{:S(2)}) async-start(bf16[8,64,512]{2,1,0:T(8,128)(2,1)} %bitcast.7), calls=%async_computation.3 | async-start | bytes 1048576 | tf_op jit(solution)/shard_map/all_to_all | solution.py:333
Sparse Core Ops, SparseCore 0:
  53.7 51.9 all-gather.2

commit v9 on v8

--- a/solution.py
+++ b/solution.py
@@ -138,17 +138,14 @@
     )
 
 
-def other_input_kernel(gate_ref, up_ref, pair_ref, own_ref, out_ref):
-    half = gate_ref.shape[1]
-    total = own_ref[...]
-    for u, w_ref in enumerate((gate_ref, up_ref)):
-        total = total + lax.dot_general(
-            w_ref[...],
-            pair_ref[:, u * half : (u + 1) * half],
-            COLS_BY_COLS,
-            preferred_element_type=F32,
-        )
-    out_ref[...] = total.astype(BF16)
+def other_input_kernel(core_ref, gate_ref, up_ref, pair_ref, own_ref, kept_ref, given_ref, total):
+    own_input_kernel(gate_ref, up_ref, pair_ref, total)
+    blocks, rows, _ = kept_ref.shape
+    core = core_ref[0]
+    for y in range(blocks):
+        for which, ref in ((core, kept_ref), (1 - core, given_ref)):
+            at = pl.ds(pl.multiple_of((2 * y + which) * rows, rows), rows)
+            ref[y] = (total[at, :] + own_ref[at, :]).astype(ref.dtype)
 
 
 def product_cost(pair, feature_count):
@@ -168,13 +165,39 @@
     )(gate, up, pair)
 
 
-def other_input_terms(gate, up, pair, own):
+def other_input_terms(core, gate, up, pair, own, out):
+    feature_count, token_count = own.shape
+    shape = (out // 2, feature_count // out, token_count)
     return pl.pallas_call(
         other_input_kernel,
-        out_shape=jax.ShapeDtypeStruct(own.shape, BF16),
-        compiler_params=PARAMS,
-        cost_estimate=product_cost(pair, own.shape[0]),
-    )(gate, up, pair, own)
+        out_shape=(jax.ShapeDtypeStruct(shape, F32), jax.ShapeDtypeStruct(shape, BF16)),
+        in_specs=[IN_SMEM] + [IN_VMEM] * 4,
+        out_specs=(IN_VMEM, IN_VMEM),
+        scratch_shapes=[pltpu.VMEM((feature_count, token_count), F32)],
+        compiler_params=PARAMS,
+        cost_estimate=product_cost(pair, feature_count),
+    )(core, gate, up, pair, own)
+
+
+def split_kernel(index_ref, kept_ref, received_ref, mine_ref, *sent_refs):
+    for k, ref in enumerate((mine_ref, *sent_refs)):
+        at = index_ref[0] ^ k
+        ref[...] = (kept_ref[at] + received_ref[at].astype(F32)).astype(ref.dtype)
+
+
+def split_shares(index, kept, received):
+    shape = kept.shape[1:]
+    others = kept.shape[0] - 1
+    return pl.pallas_call(
+        split_kernel,
+        out_shape=[jax.ShapeDtypeStruct(shape, F32)] + [jax.ShapeDtypeStruct(shape, BF16)] * others,
+        in_specs=[IN_SMEM, IN_VMEM, IN_VMEM],
+        out_specs=[IN_VMEM] * (others + 1),
+        compiler_params=PARAMS,
+        cost_estimate=pl.CostEstimate(
+            flops=2 * kept.size, bytes_accessed=10 * kept.size, transcendentals=0
+        ),
+    )(index, kept, received)
 
 
 def across_kernel(tokens_ref, out_ref):
@@ -323,11 +346,16 @@
     own_block, own_share = lax.optimization_barrier((own_block, own_share))
     other_block = lax.ppermute(own_block, "inp", pairs)
 
-    shares = other_input_terms(*other_weights, other, own_share)
-    shares = lax.all_to_all(
-        shares.reshape(out, feature_count // out, token_count), "out", 0, 0
-    )
-    grad_input = jnp.sum(shares.astype(F32), axis=0).astype(BF16).T
+    at_out = lax.axis_index("out")
+    core = (at_out % 2).reshape(1)
+    chip = (at_out // 2).reshape(1)
+    kept, given = other_input_terms(core, *other_weights, other, own_share, out)
+    received = lax.ppermute(given, "out", [(i, i ^ 1) for i in range(out)])
+    mine, *sent = split_shares(chip, kept, received)
+    other_block, mine, sent = lax.optimization_barrier((other_block, mine, sent))
+    for k, block in enumerate(sent, 1):
+        mine = mine + lax.ppermute(block, "out", [(i, i ^ 2 * k) for i in range(out)]).astype(F32)
+    grad_input = mine.astype(BF16).T
 
     grad = weight_terms(across, own_block, other_block, factor)
     swapped = lax.all_to_all(grad.reshape(dep, feature_count // dep, 2 * width), "dep", 0, 0)

time: 189 us -> 192 us (1.016)
  the two profiles are of different devices: /device:TPU:8 before, /device:TPU:10 now
where the time goes in v9:
time: 192 us; the launch traced here: 191 us
  starting transfers between devices  57.2 us (30%)
  waiting for transfers between devices  55.9 us (29%)
  blocking collectives  36.9 us (19%)
  Pallas kernels  15 us (8%)
  between operations  14.3 us (7%)
  local copies, waits for them, and re-layouts  8.78 us (5%)
  other arithmetic  2.76 us (1%)
    all_gather x1, blocking collectives, shards(): lax.all_gather(grad_pair(terms, cotangent), 'inp', axis=0, tiled=True, ax...  36.9 us
    all_to_all x1, waiting for transfers between devices, shards(): lax.all_to_all(kept.reshape(group, rows, hidden), 'inp', 0, 0, axis_index...  25.4 us
    all_to_all x1, starting transfers between devices, shards(): lax.all_to_all(kept.reshape(group, rows, hidden), 'inp', 0, 0, axis_index...  18.1 us
    ppermute x1, waiting for transfers between devices, shards(): kept = kept.astype(F32) + lax.ppermute(given, 'inp', pairs).astype(F32)  12.8 us
    ppermute x3, starting transfers between devices, shards(): lax.ppermute(block, 'out', [(i, i ^ 2 * k) for i in range(out)]).astype(F32)  12.2 us
    ppermute x1, waiting for transfers between devices, shards(): other = lax.ppermute(own, 'inp', pairs)  7.87 us
    ppermute x3, waiting for transfers between devices, shards(): lax.ppermute(block, 'out', [(i, i ^ 2 * k) for i in range(out)]).astype(F32)  5.79 us
    pallas_call x2, Pallas kernels, partial_values(): pl.pallas_call(values_kernel, out_shape=jax.ShapeDtypeStruct((token_count...  5.7 us
  transfers between devices with their start and end apart: 11, of which 8 were waited for; matrix products, arithmetic and copies ran while one was open for 2% of the time, Pallas kernels for 3%

profile of v9, /device:TPU:10, one launch (start us, length us, event | category | flops | bytes accessed | tf_op | source)
XLA Modules:
  0.0 190.9 jit_solution(11791947919361784227)
XLA Ops:
  7.2 2.8 %shard_map.67 = bf16[192,1792]{1,0:T(8,128)(2,1)} custom-call(s32[1]{0:T(128)S(6)} %sub.13.side_ref, bf16[192,512]{1,0:T(8,128)(2,1)} %tokens_ref, bf16[512,1792]{1,0:T(8,128)(2,1)} %gate_hbm.3, bf16[512,1792]{1,0:T(8,128)(2,1)} %up_hbm.3), custom_call_target="tpu_custom_call" | custom-call | flops 352321536 | bytes 2523136 | tf_op jit(solution)/shard_map/pallas_call | solution.py:57
  10.0 4.3 %collective-permute-start = (bf16[192,1792]{1,0:T(8,128)(2,1)}, bf16[192,1792]{1,0:T(8,128)(2,1)S(1)}, u32[]{:S(2)}, u32[]{:S(2)}) collective-permute-start(bf16[192,1792]{1,0:T(8,128)(2,1)} %shard_map.67), channel_id=1, source_target_pairs={{0,64},{64,0},{128,192},{192,128},{256,320},{320,256},{384,448},{4... | collective-permute-start | bytes 2064392 | tf_op jit(solution)/shard_map/ppermute | solution.py:317
  14.3 2.8 %shard_map.68 = bf16[192,1792]{1,0:T(8,128)(2,1)} custom-call(s32[1]{0:T(128)} %bitcast.side_ref, bf16[192,512]{1,0:T(8,128)(2,1)} %tokens_ref, bf16[512,1792]{1,0:T(8,128)(2,1)} %gate_hbm.3, bf16[512,1792]{1,0:T(8,128)(2,1)} %up_hbm.3), custom_call_target="tpu_custom_call" | custom-call | flops 352321536 | bytes 2523136 | tf_op jit(solution)/shard_map/pallas_call | solution.py:57
  17.2 0.0 copy-start.4
  17.2 12.8 %collective-permute-done = bf16[192,1792]{1,0:T(8,128)(2,1)S(1)} collective-permute-done((bf16[192,1792]{1,0:T(8,128)(2,1)}, bf16[192,1792]{1,0:T(8,128)(2,1)S(1)}, u32[]{:S(2)}, u32[]{:S(2)}) %collective-permute-start) | collective-permute-done | bytes 688160 | tf_op jit(solution)/shard_map/ppermute | solution.py:317
  29.9 2.1 %add_convert_fusion = bf16[192,1792]{1,0:T(8,128)(2,1)} fusion(bf16[192,1792]{1,0:T(8,128)(2,1)S(1)} %collective-permute-done, bf16[192,1792]{1,0:T(8,128)(2,1)} %shard_map.68), kind=kLoop, calls=%fused_computation | loop fusion | flops 1376256 | bytes 2064384 | tf_op jit(solution)/shard_map/convert_element_type | solution.py:319
  32.1 18.1 %all-to-all-start = ((bf16[8,24,1792]{2,1,0:T(8,128)(2,1)}), bf16[8,24,1792]{2,1,0:T(8,128)(2,1)S(1)}, u32[]{:S(2)}, u32[]{:S(2)}) async-start(bf16[8,24,1792]{2,1,0:T(8,128)(2,1)} %bitcast.1), calls=%async_computation | async-start | bytes 1376256 | tf_op jit(solution)/shard_map/all_to_all | solution.py:322
  50.2 0.0 all-gather.3.cloned.1.call-start
  50.2 0.0 copy-done.4
  50.2 0.8 shard_map.74
  51.1 0.0 all-gather.3.cloned.1.call-update
  51.1 0.8 dynamic_slice.19.cotangent_ref
  51.9 3.2 %constant_dynamic-slice_fusion = (bf16[512,896]{1,0:T(8,128)(2,1)S(1)}, bf16[512,896]{1,0:T(8,128)(2,1)S(1)}, bf16[512,896]{1,0:T(8,128)(2,1)}, bf16[512,896]{1,0:T(8,128)(2,1)S(1)}) fusion(bf16[512,1792]{1,0:T(8,128)(2,1)} %up_hbm.3, s32[]{:T(128)S(6)} %select_n.32, s32[]{:T(128)S(6)} %select_n.31, bf16[512,1792]{1,0:T(8,128)(2,1)} %gate_hbm.3), kind=kLoop, calls=%fused_computation.3 | loop fusion | bytes 7340040 | tf_op jit(solution)/shard_map/dynamic_slice | solution.py:329
  55.2 25.4 %all-to-all-done.terms_ref = bf16[8,24,1792]{2,1,0:T(8,128)(2,1)S(1)} async-done(((bf16[8,24,1792]{2,1,0:T(8,128)(2,1)}), bf16[8,24,1792]{2,1,0:T(8,128)(2,1)S(1)}, u32[]{:S(2)}, u32[]{:S(2)}) %all-to-all-start) | async-done | bytes 688160 | tf_op jit(solution)/shard_map/all_to_all | solution.py:322
  80.6 0.1 shard_map.69
  80.7 36.9 %all_gather.9.pair_ref = bf16[192,1792]{1,0:T(8,128)(2,1)S(1)} all-gather(bf16[24,1792]{1,0:T(8,128)(2,1)S(1)} %shard_map.69), channel_id=1, replica_groups={{0,128,256,384,512,640,768,896},{64,192,320,448,576,704,832,960},{1,129..., dimensions={0}, use_global_device_ids=true | all-gather | bytes 774144 | tf_op jit(solution)/shard_map/all_gather | solution.py:335
  117.6 0.1 shard_map.70
  117.7 0.0 copy-start.1
  117.7 0.9 copy-done.1
  118.5 5.6 %all-to-all-start.1 = ((bf16[8,192,256]{2,1,0:T(8,128)(2,1)}), bf16[8,192,256]{2,1,0:T(8,128)(2,1)}, u32[]{:S(2)}, u32[]{:S(2)}) async-start(bf16[8,192,256]{2,1,0:T(8,128)(2,1)} %copy-done.1), calls=%async_computation.1 | async-start | bytes 1572864 | tf_op jit(solution)/shard_map/all_to_all | solution.py:344
  124.1 4.8 %collective-permute-start.2 = (bf16[192,1792]{1,0:T(8,128)(2,1)S(1)}, bf16[192,1792]{1,0:T(8,128)(2,1)}, u32[]{:S(2)}, u32[]{:S(2)}) collective-permute-start(bf16[192,1792]{1,0:T(8,128)(2,1)S(1)} %all_gather.9.pair_ref), channel_id=1, source_target_pairs={{0,64},{64,0},{128,192},{192,128},{256,320},{320,256},{384,448},{4... | collective-permute-start | bytes 2064392 | tf_op jit(solution)/shard_map/ppermute | solution.py:338
  128.9 0.0 copy-start
  128.9 1.2 copy-done
  130.0 0.7 shard_map.71.own_ref
  130.8 0.0 copy-start.2
  130.8 0.8 copy-done.2
  131.6 0.7 all-to-all-done.1.own_ref
  132.2 4.8 %collective-permute-start.1 = (bf16[8,192,256]{2,1,0:T(8,128)(2,1)}, bf16[8,192,256]{2,1,0:T(8,128)(2,1)S(1)}, u32[]{:S(2)}, u32[]{:S(2)}) collective-permute-start(bf16[8,192,256]{2,1,0:T(8,128)(2,1)} %all-to-all-done.1.own_ref), channel_id=1, source_target_pairs={{0,64},{64,0},{128,192},{192,128},{256,320},{320,256},{384,448},{4... | collective-permute-start | bytes 2359304 | tf_op jit(solution)/shard_map/ppermute | solution.py:347
  137.0 7.9 %collective-permute-done.2.pair_ref = bf16[192,1792]{1,0:T(8,128)(2,1)} collective-permute-done((bf16[192,1792]{1,0:T(8,128)(2,1)S(1)}, bf16[192,1792]{1,0:T(8,128)(2,1)}, u32[]{:S(2)}, u32[]{:S(2)}) %collective-permute-start.2) | collective-permute-done | bytes 688160 | tf_op jit(solution)/shard_map/ppermute | solution.py:338
  144.9 0.0 copy-start.3
  144.9 1.0 copy-done.3
  145.9 1.9 shard_map.72
  147.8 1.9 %collective-permute-start.3 = (bf16[4,64,192]{2,1,0:T(8,128)(2,1)S(1)}, bf16[4,64,192]{2,1,0:T(8,128)(2,1)S(1)}, u32[]{:S(2)}, u32[]{:S(2)}) collective-permute-start(bf16[4,64,192]{2,1,0:T(8,128)(2,1)S(1)} %get-tuple-element.42), channel_id=1, source_target_pairs={{0,8},{8,0},{16,24},{24,16},{32,40},{40,32},{48,56},{56,48},{1,9},... | collective-permute-start | bytes 294920 | tf_op jit(solution)/shard_map/ppermute | solution.py:353
  149.7 1.3 collective-permute-done.3.received_ref
  151.1 2.1 %collective-permute-done.1.other_ref = bf16[8,192,256]{2,1,0:T(8,128)(2,1)S(1)} collective-permute-done((bf16[8,192,256]{2,1,0:T(8,128)(2,1)}, bf16[8,192,256]{2,1,0:T(8,128)(2,1)S(1)}, u32[]{:S(2)}, u32[]{:S(2)}) %collective-permute-start.1) | collective-permute-done | bytes 786464 | tf_op jit(solution)/shard_map/ppermute | solution.py:347
  153.2 0.0 copy-start.5
  153.2 0.9 copy-done.5
  154.1 4.9 %shard_map.75 = bf16[512,512]{1,0:T(8,128)(2,1)} custom-call(bf16[8,512,192]{2,1,0:T(8,128)(2,1)} %bitcast.8, bf16[8,192,256]{2,1,0:T(8,128)(2,1)} %all-to-all-done.1.own_ref, bf16[8,192,256]{2,1,0:T(8,128)(2,1)} %copy-done.5), custom_call_target="tpu_custom_call" | custom-call | flops 805306368 | bytes 3145728 | tf_op jit(solution)/shard_map/pallas_call | solution.py:251
  158.9 5.6 %all-to-all-start.2 = ((bf16[8,64,512]{2,1,0:T(8,128)(2,1)}), bf16[8,64,512]{2,1,0:T(8,128)(2,1)S(1)}, u32[]{:S(2)}, u32[]{:S(2)}) async-start(bf16[8,64,512]{2,1,0:T(8,128)(2,1)} %bitcast.9), calls=%async_computation.2 | async-start | bytes 1048576 | tf_op jit(solution)/shard_map/all_to_all | solution.py:361
  164.6 4.1 %collective-permute-start.4 = (bf16[64,192]{1,0:T(8,128)(2,1)S(1)}, bf16[64,192]{1,0:T(8,128)(2,1)S(1)}, u32[]{:S(2)}, u32[]{:S(2)}) collective-permute-start(bf16[64,192]{1,0:T(8,128)(2,1)S(1)} %get-tuple-element.48), channel_id=1, source_target_pairs={{0,16},{8,24},{16,0},{24,8},{32,48},{40,56},{48,32},{56,40},{1,17}... | collective-permute-start | bytes 73736 | tf_op jit(solution)/shard_map/ppermute | solution.py:357
  168.7 5.6 %collective-permute-start.5 = (bf16[64,192]{1,0:T(8,128)(2,1)S(1)}, bf16[64,192]{1,0:T(8,128)(2,1)S(1)}, u32[]{:S(2)}, u32[]{:S(2)}) collective-permute-start(bf16[64,192]{1,0:T(8,128)(2,1)S(1)} %get-tuple-element.49), channel_id=1, source_target_pairs={{0,32},{8,40},{16,48},{24,56},{32,0},{40,8},{48,16},{56,24},{1,33}... | collective-permute-start | bytes 73736 | tf_op jit(solution)/shard_map/ppermute | solution.py:357
  174.3 2.5 %collective-permute-start.6 = (bf16[64,192]{1,0:T(8,128)(2,1)S(1)}, bf16[64,192]{1,0:T(8,128)(2,1)S(1)}, u32[]{:S(2)}, u32[]{:S(2)}) collective-permute-start(bf16[64,192]{1,0:T(8,128)(2,1)S(1)} %get-tuple-element.50), channel_id=1, source_target_pairs={{0,48},{8,56},{16,32},{24,40},{32,16},{40,24},{48,0},{56,8},{1,49}... | collective-permute-start | bytes 73736 | tf_op jit(solution)/shard_map/ppermute | solution.py:357
  176.8 0.0 collective-permute-done.4
  176.8 2.0 %collective-permute-done.5 = bf16[64,192]{1,0:T(8,128)(2,1)S(1)} collective-permute-done((bf16[64,192]{1,0:T(8,128)(2,1)S(1)}, bf16[64,192]{1,0:T(8,128)(2,1)S(1)}, u32[]{:S(2)}, u32[]{:S(2)}) %collective-permute-start.5) | collective-permute-done | bytes 24608 | tf_op jit(solution)/shard_map/ppermute | solution.py:357
  178.8 3.8 %collective-permute-done.6 = bf16[64,192]{1,0:T(8,128)(2,1)S(1)} collective-permute-done((bf16[64,192]{1,0:T(8,128)(2,1)S(1)}, bf16[64,192]{1,0:T(8,128)(2,1)S(1)}, u32[]{:S(2)}, u32[]{:S(2)}) %collective-permute-start.6) | collective-permute-done | bytes 24608 | tf_op jit(solution)/shard_map/ppermute | solution.py:357
  182.6 0.6 fusion
  183.2 0.0 all-to-all-done.2.swapped_ref
  183.2 0.8 shard_map.76
  (2 shorter events, 0.0 us)
Async XLA Ops:
  10.0 19.9 %collective-permute-start = (bf16[192,1792]{1,0:T(8,128)(2,1)}, bf16[192,1792]{1,0:T(8,128)(2,1)S(1)}, u32[]{:S(2)}, u32[]{:S(2)}) collective-permute-start(bf16[192,1792]{1,0:T(8,128)(2,1)} %shard_map.67), channel_id=1, source_target_pairs={{0,64},{64,0},{128,192},{192,128},{256,320},{320,256},{384,448},{4... | collective-permute-start | bytes 2064392 | tf_op jit(solution)/shard_map/ppermute | solution.py:317
  17.2 33.1 %copy-start.4 = (bf16[192,512]{1,0:T(8,128)(2,1)S(1)}, bf16[192,512]{1,0:T(8,128)(2,1)}, u32[]{:S(2)}) copy-start(bf16[192,512]{1,0:T(8,128)(2,1)} %tokens_ref) | copy-start | bytes 589828
  32.1 48.5 %all-to-all-start = ((bf16[8,24,1792]{2,1,0:T(8,128)(2,1)}), bf16[8,24,1792]{2,1,0:T(8,128)(2,1)S(1)}, u32[]{:S(2)}, u32[]{:S(2)}) async-start(bf16[8,24,1792]{2,1,0:T(8,128)(2,1)} %bitcast.1), calls=%async_computation | async-start | bytes 1376256 | tf_op jit(solution)/shard_map/all_to_all | solution.py:322
  50.2 103.0 %all-gather.3.cloned.1.call-start = ((), (), s32[]{:S(2)}) async-start(), calls=%async_computation.3 | async-start | bytes 2359296 | tf_op jit(solution)/shard_map/all_gather | solution.py:321
  117.7 0.9 copy-start.1
  118.5 13.7 %all-to-all-start.1 = ((bf16[8,192,256]{2,1,0:T(8,128)(2,1)}), bf16[8,192,256]{2,1,0:T(8,128)(2,1)}, u32[]{:S(2)}, u32[]{:S(2)}) async-start(bf16[8,192,256]{2,1,0:T(8,128)(2,1)} %copy-done.1), calls=%async_computation.1 | async-start | bytes 1572864 | tf_op jit(solution)/shard_map/all_to_all | solution.py:344
  124.1 20.8 %collective-permute-start.2 = (bf16[192,1792]{1,0:T(8,128)(2,1)S(1)}, bf16[192,1792]{1,0:T(8,128)(2,1)}, u32[]{:S(2)}, u32[]{:S(2)}) collective-permute-start(bf16[192,1792]{1,0:T(8,128)(2,1)S(1)} %all_gather.9.pair_ref), channel_id=1, source_target_pairs={{0,64},{64,0},{128,192},{192,128},{256,320},{320,256},{384,448},{4... | collective-permute-start | bytes 2064392 | tf_op jit(solution)/shard_map/ppermute | solution.py:338
  128.9 1.2 copy-start
  130.8 0.8 copy-start.2
  132.2 21.0 %collective-permute-start.1 = (bf16[8,192,256]{2,1,0:T(8,128)(2,1)}, bf16[8,192,256]{2,1,0:T(8,128)(2,1)S(1)}, u32[]{:S(2)}, u32[]{:S(2)}) collective-permute-start(bf16[8,192,256]{2,1,0:T(8,128)(2,1)} %all-to-all-done.1.own_ref), channel_id=1, source_target_pairs={{0,64},{64,0},{128,192},{192,128},{256,320},{320,256},{384,448},{4... | collective-permute-start | bytes 2359304 | tf_op jit(solution)/shard_map/ppermute | solution.py:347
  144.9 1.0 copy-start.3
  147.8 3.2 %collective-permute-start.3 = (bf16[4,64,192]{2,1,0:T(8,128)(2,1)S(1)}, bf16[4,64,192]{2,1,0:T(8,128)(2,1)S(1)}, u32[]{:S(2)}, u32[]{:S(2)}) collective-permute-start(bf16[4,64,192]{2,1,0:T(8,128)(2,1)S(1)} %get-tuple-element.42), channel_id=1, source_target_pairs={{0,8},{8,0},{16,24},{24,16},{32,40},{40,32},{48,56},{56,48},{1,9},... | collective-permute-start | bytes 294920 | tf_op jit(solution)/shard_map/ppermute | solution.py:353
  153.2 0.9 copy-start.5
  158.9 24.3 %all-to-all-start.2 = ((bf16[8,64,512]{2,1,0:T(8,128)(2,1)}), bf16[8,64,512]{2,1,0:T(8,128)(2,1)S(1)}, u32[]{:S(2)}, u32[]{:S(2)}) async-start(bf16[8,64,512]{2,1,0:T(8,128)(2,1)} %bitcast.9), calls=%async_computation.2 | async-start | bytes 1048576 | tf_op jit(solution)/shard_map/all_to_all | solution.py:361
  164.6 12.2 %collective-permute-start.4 = (bf16[64,192]{1,0:T(8,128)(2,1)S(1)}, bf16[64,192]{1,0:T(8,128)(2,1)S(1)}, u32[]{:S(2)}, u32[]{:S(2)}) collective-permute-start(bf16[64,192]{1,0:T(8,128)(2,1)S(1)} %get-tuple-element.48), channel_id=1, source_target_pairs={{0,16},{8,24},{16,0},{24,8},{32,48},{40,56},{48,32},{56,40},{1,17}... | collective-permute-start | bytes 73736 | tf_op jit(solution)/shard_map/ppermute | solution.py:357
  168.7 10.1 %collective-permute-start.5 = (bf16[64,192]{1,0:T(8,128)(2,1)S(1)}, bf16[64,192]{1,0:T(8,128)(2,1)S(1)}, u32[]{:S(2)}, u32[]{:S(2)}) collective-permute-start(bf16[64,192]{1,0:T(8,128)(2,1)S(1)} %get-tuple-element.49), channel_id=1, source_target_pairs={{0,32},{8,40},{16,48},{24,56},{32,0},{40,8},{48,16},{56,24},{1,33}... | collective-permute-start | bytes 73736 | tf_op jit(solution)/shard_map/ppermute | solution.py:357
  174.3 8.3 %collective-permute-start.6 = (bf16[64,192]{1,0:T(8,128)(2,1)S(1)}, bf16[64,192]{1,0:T(8,128)(2,1)S(1)}, u32[]{:S(2)}, u32[]{:S(2)}) collective-permute-start(bf16[64,192]{1,0:T(8,128)(2,1)S(1)} %get-tuple-element.50), channel_id=1, source_target_pairs={{0,48},{8,56},{16,32},{24,40},{32,16},{40,24},{48,0},{56,8},{1,49}... | collective-permute-start | bytes 73736 | tf_op jit(solution)/shard_map/ppermute | solution.py:357
Sparse Core Ops, SparseCore 0:
  53.7 50.4 all-gather.2

commit v10 on v8

--- a/solution.py
+++ b/solution.py
@@ -49,9 +49,10 @@
 IN_VMEM = pl.BlockSpec(memory_space=pltpu.VMEM)
 PARAMS = pltpu.CompilerParams(vmem_limit_bytes=16 * 2**20)
 WHOLE = pltpu.CompilerParams(vmem_limit_bytes=60 * 2**20)
-
-
-def partial_values(side, tokens, w_gate, w_up):
+ROOM = pltpu.CompilerParams(vmem_limit_bytes=40 * 2**20)
+
+
+def partial_values(side, tokens, w_gate, w_up, params):
     token_count, feature_count = tokens.shape
     half = w_gate.shape[1] // 2
     return pl.pallas_call(
@@ -66,7 +67,7 @@
             pltpu.VMEM((2, token_count, half), BF16),
             pltpu.SemaphoreType.DMA((5,)),
         ],
-        compiler_params=WHOLE,
+        compiler_params=params,
         cost_estimate=pl.CostEstimate(
             flops=4 * token_count * feature_count * half,
             bytes_accessed=4 * feature_count * half + 4 * token_count * half,
@@ -288,9 +289,9 @@
     own_side = parity.reshape(1)
     other_side = 1 - own_side
 
-    given = partial_values(other_side, tokens, w_gate, w_up)
+    given = partial_values(other_side, tokens, w_gate, w_up, WHOLE)
     own_side, given = lax.optimization_barrier((own_side, given))
-    kept = partial_values(own_side, tokens, w_gate, w_up)
+    kept = partial_values(own_side, tokens, w_gate, w_up, ROOM)
     kept = kept.astype(F32) + lax.ppermute(given, "inp", pairs).astype(F32)
     kept, w_gate, w_up, tokens = lax.optimization_barrier(
         (kept.astype(BF16), w_gate, w_up, tokens)

time: 189 us -> 187 us (0.989)
  no operation moved by 1% of the time
where the time goes in v10:
time: 187 us; the launch traced here: 186 us
  waiting for transfers between devices  61.6 us (33%)
  starting transfers between devices  49.1 us (26%)
  blocking collectives  36.9 us (20%)
  Pallas kernels  15.1 us (8%)
  between operations  14.2 us (8%)
  local copies, waits for them, and re-layouts  7.73 us (4%)
    all_gather x1, blocking collectives, shards(): lax.all_gather(grad_pair(terms, cotangent), 'inp', axis=0, tiled=True, ax...  36.9 us
    all_to_all x1, waiting for transfers between devices, shards(): lax.all_to_all(kept.reshape(group, rows, hidden), 'inp', 0, 0, axis_index...  25.7 us
    all_to_all x1, starting transfers between devices, shards(): lax.all_to_all(kept.reshape(group, rows, hidden), 'inp', 0, 0, axis_index...  18.1 us
    ppermute x1, waiting for transfers between devices, shards(): kept = kept.astype(F32) + lax.ppermute(given, 'inp', pairs).astype(F32)  12.8 us
    all_to_all x1, waiting for transfers between devices, shards(): lax.all_to_all(grad.reshape(dep, feature_count // dep, 2 * width), 'dep',...  7.97 us
    ppermute x1, waiting for transfers between devices, shards(): other = lax.ppermute(own, 'inp', pairs)  7.64 us
    all_to_all x1, waiting for transfers between devices, shards(): lax.all_to_all(shares.reshape(out, feature_count // out, token_count), 'o...  6.49 us
    all_to_all x1, starting transfers between devices, shards(): lax.all_to_all(grad.reshape(dep, feature_count // dep, 2 * width), 'dep',...  5.97 us
  transfers between devices with their start and end apart: 8, of which 6 were waited for; matrix products, arithmetic and copies ran while one was open for 2% of the time, Pallas kernels for 6%

profile of v10, /device:TPU:8, one launch (start us, length us, event | category | flops | bytes accessed | tf_op | source)
XLA Modules:
  0.0 186.4 jit_solution(7892522332665978973)
XLA Ops:
  7.2 0.0 copy-start
  7.2 0.0 copy-start.5
  7.2 3.0 %shard_map.67 = bf16[192,1792]{1,0:T(8,128)(2,1)} custom-call(s32[1]{0:T(128)S(6)} %sub.10.side_ref, bf16[192,512]{1,0:T(8,128)(2,1)} %tokens_ref, bf16[512,1792]{1,0:T(8,128)(2,1)} %gate_hbm.3, bf16[512,1792]{1,0:T(8,128)(2,1)} %up_hbm.3), custom_call_target="tpu_custom_call" | custom-call | flops 352321536 | bytes 2523136 | tf_op jit(solution)/shard_map/pallas_call | solution.py:58
  10.2 4.3 %collective-permute-start = (bf16[192,1792]{1,0:T(8,128)(2,1)}, bf16[192,1792]{1,0:T(8,128)(2,1)S(1)}, u32[]{:S(2)}, u32[]{:S(2)}) collective-permute-start(bf16[192,1792]{1,0:T(8,128)(2,1)} %shard_map.67), channel_id=1, source_target_pairs={{0,64},{64,0},{128,192},{192,128},{256,320},{320,256},{384,448},{4... | collective-permute-start | bytes 2064392 | tf_op jit(solution)/shard_map/ppermute | solution.py:295
  14.5 0.0 copy-done
  14.5 0.0 copy-done.5
  14.5 0.0 copy-start.1
  14.5 1.5 copy-done.1
  16.0 1.3 shard_map.68
  17.3 12.8 %collective-permute-done = bf16[192,1792]{1,0:T(8,128)(2,1)S(1)} collective-permute-done((bf16[192,1792]{1,0:T(8,128)(2,1)}, bf16[192,1792]{1,0:T(8,128)(2,1)S(1)}, u32[]{:S(2)}, u32[]{:S(2)}) %collective-permute-start) | collective-permute-done | bytes 688160 | tf_op jit(solution)/shard_map/ppermute | solution.py:295
  30.1 1.0 add_convert_fusion
  31.1 18.1 %all-to-all-start = ((bf16[8,24,1792]{2,1,0:T(8,128)(2,1)}), bf16[8,24,1792]{2,1,0:T(8,128)(2,1)S(1)}, u32[]{:S(2)}, u32[]{:S(2)}) async-start(bf16[8,24,1792]{2,1,0:T(8,128)(2,1)} %bitcast.1), calls=%async_computation | async-start | bytes 1376256 | tf_op jit(solution)/shard_map/all_to_all | solution.py:300
  49.2 0.0 all-gather.3.cloned.1.call-start
  49.3 0.8 shard_map.73
  50.1 0.0 all-gather.3.cloned.1.call-update
  50.2 0.8 dynamic_slice.19.cotangent_ref
  51.0 3.1 %constant_dynamic-slice_fusion = (bf16[512,896]{1,0:T(8,128)(2,1)S(1)}, bf16[512,896]{1,0:T(8,128)(2,1)}, bf16[512,896]{1,0:T(8,128)(2,1)}, bf16[512,896]{1,0:T(8,128)(2,1)}) fusion(bf16[512,1792]{1,0:T(8,128)(2,1)S(1)} %copy-done, s32[]{:T(128)S(6)} %select_n.25, s32[]{:T(128)S(6)} %select_n.24, bf16[512,1792]{1,0:T(8,128)(2,1)} %gate_hbm.3), kind=kLoop, calls=%fused_computation.1 | loop fusion | bytes 7340040 | tf_op jit(solution)/shard_map/dynamic_slice | solution.py:307
  54.0 25.7 %all-to-all-done.terms_ref = bf16[8,24,1792]{2,1,0:T(8,128)(2,1)S(1)} async-done(((bf16[8,24,1792]{2,1,0:T(8,128)(2,1)}), bf16[8,24,1792]{2,1,0:T(8,128)(2,1)S(1)}, u32[]{:S(2)}, u32[]{:S(2)}) %all-to-all-start) | async-done | bytes 688160 | tf_op jit(solution)/shard_map/all_to_all | solution.py:300
  79.8 0.1 shard_map.69
  79.9 36.9 %all_gather.9.pair_ref = bf16[192,1792]{1,0:T(8,128)(2,1)S(1)} all-gather(bf16[24,1792]{1,0:T(8,128)(2,1)S(1)} %shard_map.69), channel_id=1, replica_groups={{0,128,256,384,512,640,768,896},{64,192,320,448,576,704,832,960},{1,129..., dimensions={0}, use_global_device_ids=true | all-gather | bytes 774144 | tf_op jit(solution)/shard_map/all_gather | solution.py:313
  116.8 0.9 shard_map.70
  117.8 5.5 %all-to-all-start.1 = ((bf16[8,192,256]{2,1,0:T(8,128)(2,1)}), bf16[8,192,256]{2,1,0:T(8,128)(2,1)}, u32[]{:S(2)}, u32[]{:S(2)}) async-start(bf16[8,192,256]{2,1,0:T(8,128)(2,1)} %shard_map.70), calls=%async_computation.1 | async-start | bytes 1572864 | tf_op jit(solution)/shard_map/all_to_all | solution.py:322
  123.2 0.0 copy-start.2
  123.2 4.7 %collective-permute-start.1 = (bf16[192,1792]{1,0:T(8,128)(2,1)S(1)}, bf16[192,1792]{1,0:T(8,128)(2,1)}, u32[]{:S(2)}, u32[]{:S(2)}) collective-permute-start(bf16[192,1792]{1,0:T(8,128)(2,1)S(1)} %all_gather.9.pair_ref), channel_id=1, source_target_pairs={{0,64},{64,0},{128,192},{192,128},{256,320},{320,256},{384,448},{4... | collective-permute-start | bytes 2064392 | tf_op jit(solution)/shard_map/ppermute | solution.py:316
  128.0 0.0 copy-start.3
  128.0 1.2 copy-done.3
  129.1 0.0 copy-start.4
  129.1 1.2 copy-done.4
  130.3 0.7 shard_map.71.own_ref
  131.0 0.9 all-to-all-done.1.own_ref
  132.0 4.6 %collective-permute-start.2 = (bf16[8,192,256]{2,1,0:T(8,128)(2,1)}, bf16[8,192,256]{2,1,0:T(8,128)(2,1)}, u32[]{:S(2)}, u32[]{:S(2)}) collective-permute-start(bf16[8,192,256]{2,1,0:T(8,128)(2,1)} %all-to-all-done.1.own_ref), channel_id=1, source_target_pairs={{0,64},{64,0},{128,192},{192,128},{256,320},{320,256},{384,448},{4... | collective-permute-start | bytes 2359304 | tf_op jit(solution)/shard_map/ppermute | solution.py:325
  136.6 7.6 %collective-permute-done.1.pair_ref = bf16[192,1792]{1,0:T(8,128)(2,1)} collective-permute-done((bf16[192,1792]{1,0:T(8,128)(2,1)S(1)}, bf16[192,1792]{1,0:T(8,128)(2,1)}, u32[]{:S(2)}, u32[]{:S(2)}) %collective-permute-start.1) | collective-permute-done | bytes 688160 | tf_op jit(solution)/shard_map/ppermute | solution.py:316
  144.2 0.0 copy-done.2
  144.2 2.6 %shard_map.72 = bf16[512,192]{1,0:T(8,128)(2,1)} custom-call(bf16[512,896]{1,0:T(8,128)(2,1)S(1)} %copy-done.2, bf16[512,896]{1,0:T(8,128)(2,1)S(1)} %get-tuple-element.24.up_ref, bf16[192,1792]{1,0:T(8,128)(2,1)} %collective-permute-done.1.pair_ref, f32[512,192]{1,0:T(8,128)S(1)} %shard_map.71.own_ref), custom_call_target="tpu_custom_call" | custom-call | flops 352321536 | bytes 2621440 | tf_op jit(solution)/shard_map/pallas_call | solution.py:173
  146.8 5.9 %all-to-all-start.2 = ((bf16[8,64,192]{2,1,0:T(8,128)(2,1)}), bf16[8,64,192]{2,1,0:T(8,128)(2,1)S(1)}, u32[]{:S(2)}, u32[]{:S(2)}) async-start(bf16[8,64,192]{2,1,0:T(8,128)(2,1)} %bitcast.2), calls=%async_computation.2 | async-start | bytes 524288 | tf_op jit(solution)/shard_map/all_to_all | solution.py:328
  152.7 0.0 all-gather.3.cloned.1.call-done
  152.7 0.0 collective-permute-done.2.other_ref
  152.7 4.9 %shard_map.74 = bf16[512,512]{1,0:T(8,128)(2,1)} custom-call(bf16[8,512,192]{2,1,0:T(8,128)(2,1)} %bitcast.6, bf16[8,192,256]{2,1,0:T(8,128)(2,1)} %all-to-all-done.1.own_ref, bf16[8,192,256]{2,1,0:T(8,128)(2,1)} %collective-permute-done.2.other_ref), custom_call_target="tpu_custom_call" | custom-call | flops 805306368 | bytes 3145728 | tf_op jit(solution)/shard_map/pallas_call | solution.py:229
  157.6 6.5 %all-to-all-done.2 = bf16[8,64,192]{2,1,0:T(8,128)(2,1)S(1)} async-done(((bf16[8,64,192]{2,1,0:T(8,128)(2,1)}), bf16[8,64,192]{2,1,0:T(8,128)(2,1)S(1)}, u32[]{:S(2)}, u32[]{:S(2)}) %all-to-all-start.2) | async-done | bytes 196640 | tf_op jit(solution)/shard_map/all_to_all | solution.py:328
  164.1 6.0 %all-to-all-start.3 = ((bf16[8,64,512]{2,1,0:T(8,128)(2,1)}), bf16[8,64,512]{2,1,0:T(8,128)(2,1)S(1)}, u32[]{:S(2)}, u32[]{:S(2)}) async-start(bf16[8,64,512]{2,1,0:T(8,128)(2,1)} %bitcast.7), calls=%async_computation.3 | async-start | bytes 1048576 | tf_op jit(solution)/shard_map/all_to_all | solution.py:334
  170.1 0.7 reduce_sum.12
  170.7 8.0 %all-to-all-done.3.swapped_ref = bf16[8,64,512]{2,1,0:T(8,128)(2,1)S(1)} async-done(((bf16[8,64,512]{2,1,0:T(8,128)(2,1)}), bf16[8,64,512]{2,1,0:T(8,128)(2,1)S(1)}, u32[]{:S(2)}, u32[]{:S(2)}) %all-to-all-start.3) | async-done | bytes 524320 | tf_op jit(solution)/shard_map/all_to_all | solution.py:334
  178.7 0.8 shard_map.75
Async XLA Ops:
  7.2 7.3 %copy-start = (bf16[512,1792]{1,0:T(8,128)(2,1)S(1)}, bf16[512,1792]{1,0:T(8,128)(2,1)}, u32[]{:S(2)}) copy-start(bf16[512,1792]{1,0:T(8,128)(2,1)} %up_hbm.3) | copy-start | bytes 5505028
  7.2 7.3 %copy-start.5 = (bf16[192,512]{1,0:T(8,128)(2,1)S(1)}, bf16[192,512]{1,0:T(8,128)(2,1)}, u32[]{:S(2)}) copy-start(bf16[192,512]{1,0:T(8,128)(2,1)} %tokens_ref) | copy-start | bytes 589828
  10.2 19.9 %collective-permute-start = (bf16[192,1792]{1,0:T(8,128)(2,1)}, bf16[192,1792]{1,0:T(8,128)(2,1)S(1)}, u32[]{:S(2)}, u32[]{:S(2)}) collective-permute-start(bf16[192,1792]{1,0:T(8,128)(2,1)} %shard_map.67), channel_id=1, source_target_pairs={{0,64},{64,0},{128,192},{192,128},{256,320},{320,256},{384,448},{4... | collective-permute-start | bytes 2064392 | tf_op jit(solution)/shard_map/ppermute | solution.py:295
  14.5 1.5 copy-start.1
  31.1 48.7 %all-to-all-start = ((bf16[8,24,1792]{2,1,0:T(8,128)(2,1)}), bf16[8,24,1792]{2,1,0:T(8,128)(2,1)S(1)}, u32[]{:S(2)}, u32[]{:S(2)}) async-start(bf16[8,24,1792]{2,1,0:T(8,128)(2,1)} %bitcast.1), calls=%async_computation | async-start | bytes 1376256 | tf_op jit(solution)/shard_map/all_to_all | solution.py:300
  49.2 103.5 %all-gather.3.cloned.1.call-start = ((), (), s32[]{:S(2)}) async-start(), calls=%async_computation.4 | async-start | bytes 2359296 | tf_op jit(solution)/shard_map/all_gather | solution.py:299
  117.8 14.2 %all-to-all-start.1 = ((bf16[8,192,256]{2,1,0:T(8,128)(2,1)}), bf16[8,192,256]{2,1,0:T(8,128)(2,1)}, u32[]{:S(2)}, u32[]{:S(2)}) async-start(bf16[8,192,256]{2,1,0:T(8,128)(2,1)} %shard_map.70), calls=%async_computation.1 | async-start | bytes 1572864 | tf_op jit(solution)/shard_map/all_to_all | solution.py:322
  123.2 21.0 %copy-start.2 = (bf16[512,896]{1,0:T(8,128)(2,1)S(1)}, bf16[512,896]{1,0:T(8,128)(2,1)}, u32[]{:S(2)}) copy-start(bf16[512,896]{1,0:T(8,128)(2,1)} %get-tuple-element.23.gate_ref) | copy-start | bytes 2752516
  123.2 21.0 %collective-permute-start.1 = (bf16[192,1792]{1,0:T(8,128)(2,1)S(1)}, bf16[192,1792]{1,0:T(8,128)(2,1)}, u32[]{:S(2)}, u32[]{:S(2)}) collective-permute-start(bf16[192,1792]{1,0:T(8,128)(2,1)S(1)} %all_gather.9.pair_ref), channel_id=1, source_target_pairs={{0,64},{64,0},{128,192},{192,128},{256,320},{320,256},{384,448},{4... | collective-permute-start | bytes 2064392 | tf_op jit(solution)/shard_map/ppermute | solution.py:316
  128.0 1.2 copy-start.3
  129.1 1.2 copy-start.4
  132.0 20.8 %collective-permute-start.2 = (bf16[8,192,256]{2,1,0:T(8,128)(2,1)}, bf16[8,192,256]{2,1,0:T(8,128)(2,1)}, u32[]{:S(2)}, u32[]{:S(2)}) collective-permute-start(bf16[8,192,256]{2,1,0:T(8,128)(2,1)} %all-to-all-done.1.own_ref), channel_id=1, source_target_pairs={{0,64},{64,0},{128,192},{192,128},{256,320},{320,256},{384,448},{4... | collective-permute-start | bytes 2359304 | tf_op jit(solution)/shard_map/ppermute | solution.py:325
  146.8 17.3 %all-to-all-start.2 = ((bf16[8,64,192]{2,1,0:T(8,128)(2,1)}), bf16[8,64,192]{2,1,0:T(8,128)(2,1)S(1)}, u32[]{:S(2)}, u32[]{:S(2)}) async-start(bf16[8,64,192]{2,1,0:T(8,128)(2,1)} %bitcast.2), calls=%async_computation.2 | async-start | bytes 524288 | tf_op jit(solution)/shard_map/all_to_all | solution.py:328
  164.1 14.6 %all-to-all-start.3 = ((bf16[8,64,512]{2,1,0:T(8,128)(2,1)}), bf16[8,64,512]{2,1,0:T(8,128)(2,1)S(1)}, u32[]{:S(2)}, u32[]{:S(2)}) async-start(bf16[8,64,512]{2,1,0:T(8,128)(2,1)} %bitcast.7), calls=%async_computation.3 | async-start | bytes 1048576 | tf_op jit(solution)/shard_map/all_to_all | solution.py:334
Sparse Core Ops, SparseCore 0:
  52.7 51.9 all-gather.2
